TPU v7x, 32 devices: a whole 2x2x4 slice. The times are simulated.
32 devices in a mesh: atoms: 8 (over z, y), sig: 4 (over x, core).
Axes of the slice: x: 2, y: 2, z: 4, core: 2. Of those that a mesh axis runs over, the one named last changes fastest.
Arguments:
- signals: bfloat16 [1024, 512], P(None, 'sig'), may hold values from -6 to 6
- dictionary: bfloat16 [1024, 4096], P(None, ('atoms', 'sig')), may hold values from -0.1875 to 0.1875
- selected: int32 [2, 4], P(None, 'sig'), may hold values from 0 to 63
- inverses: bfloat16 [2, 4, 64, 64], P(None, 'sig'), may hold values from -0.14 to 1.14
Outputs:
- correlations: bfloat16 [4096, 512], P('atoms', 'sig')
- coefficients: bfloat16 [2, 64, 512], P(None, None, 'sig')
- peak: float32 [512], P('sig')
All inputs are finite; a program needn't handle non-finite values.
Results may differ from a plain program's by a relative error of at most 0.006.
Values may be sent and summed in bfloat16 or wider, within the bound.
No kernel may reach another device: no remote copies, remote signals or barrier semaphores. Data moves between devices by JAX's collectives and lax.ppermute only.
A program may use at most 128 MiB of HBM per device.

v0:
```python
import jax
import jax.numpy as jnp
from jax import lax
from jax.sharding import PartitionSpec as P

BLK = 64
SB = 128
STEPS = 2


def spread(block, axis, holder):
    block = jnp.where(lax.axis_index(axis) == holder, block, jnp.zeros_like(block))
    return lax.psum(block, axis)


def shards(signals, dictionary, selected, inverses):
    gathered = lax.all_gather(dictionary, "sig", axis=1, tiled=True)
    width = gathered.shape[1]
    blocks_here = width // BLK
    block_total = signals.shape[1] // SB
    correlation = lax.dot_general(
        gathered, signals, (((0,), (0,)), ((), ())), preferred_element_type=jnp.float32
    )
    coefficients = jnp.zeros((STEPS, BLK, signals.shape[1]), jnp.bfloat16)

    def locate(step, slot):
        block_id = selected[step, slot]
        owner_index = block_id // blocks_here
        offset = block_id % blocks_here * BLK
        return (owner_index, offset)

    def panel_of(atom_block):
        return lax.dot_general(
            gathered, atom_block, (((0,), (0,)), ((), ())), preferred_element_type=jnp.float32
        ).astype(jnp.bfloat16)

    def refit(step, slot, rows_block):
        return jnp.dot(
            inverses[step, slot].astype(jnp.float32),
            rows_block,
            precision=lax.Precision.HIGHEST,
            preferred_element_type=jnp.float32,
        ).astype(jnp.bfloat16)

    def solve_block(correlation, step, slot, offset):
        rows_block = lax.dynamic_slice(correlation, (offset, slot * SB), (BLK, SB))
        return refit(step, slot, rows_block)

    def apply_block(correlation, coefficients, gram_panel, weights_block, step, slot):
        column_start = slot * SB
        columns = correlation
        columns = columns - jnp.dot(gram_panel, weights_block, preferred_element_type=jnp.float32)
        correlation = columns
        coefficients = lax.dynamic_update_slice(
            coefficients, weights_block[None], (step, 0, column_start)
        )
        return (correlation, coefficients)

    for step in range(STEPS):

        def advance(slot, carried):
            correlation, coefficients = carried
            owner_index, offset = locate(step, slot)
            atom_block = lax.dynamic_slice_in_dim(gathered, offset, BLK, 1)
            weights_block = solve_block(correlation, step, slot, offset)
            atom_block, weights_block = (
                spread(atom_block, "atoms", owner_index),
                spread(weights_block, "atoms", owner_index),
            )
            gram_panel = panel_of(atom_block)
            return apply_block(correlation, coefficients, gram_panel, weights_block, step, slot)

        correlation, coefficients = lax.fori_loop(
            0, block_total, advance, (correlation, coefficients)
        )
    largest = lax.pmax(jnp.max(jnp.abs(correlation), axis=0), "atoms")
    return (correlation.astype(jnp.bfloat16), coefficients, largest)


def solution(mesh):
    placed = (P(None, "sig"), P(None, ("atoms", "sig")), P(None, "sig"), P(None, "sig", None, None))
    return jax.shard_map(
        shards,
        mesh=mesh,
        in_specs=placed,
        out_specs=(P("atoms", "sig"), P(None, None, "sig"), P("sig")),
        check_vma=False,
    )
```

profile of v0, /device:TPU:0, one launch (start us, length us, event | category | flops | bytes accessed | tf_op | source)
XLA Modules:
  0.0 168.5 jit_solution(2854032412302445752)
XLA Ops:
  7.2 0.0 copy-start
  7.2 0.0 copy-start.4
  7.2 0.0 all-gather.2.cloned.1.call-start
  7.2 0.7 all-gather.2.cloned.1.call-update
  7.9 0.0 all-reduce.3.cloned.1.call-start
  8.0 0.0 copy-done.4
  8.0 0.6 fusion.12
  13.8 15.3 %all-gather.2.cloned.1.call-done = bf16[1024,512]{1,0:T(8,128)(2,1)} async-done(((bf16[1024,128]{1,0:T(8,128)(2,1)}), bf16[1024,512]{1,0:T(8,128)(2,1)}) %all-gather.2.cloned.1.call-update) | async-done | bytes 1048592 | tf_op jit(solution)/shard_map/all_gather | solution.py:17
  29.1 0.0 copy-start.1
  29.2 2.2 %dynamic-slice_select_fusion = (bf16[1024,64]{1,0:T(8,128)(2,1)}, bf16[1024,64]{1,0:T(8,128)(2,1)}) fusion(bf16[1024,512]{1,0:T(8,128)(2,1)} %all-gather.2.cloned.1.call-done, s32[]{:T(128)S(6)} %select_n.99, pred[]{:T(512)S(6)} %eq.16, s32[]{:T(128)S(6)} %select_n.91, pred[]{:T(512)S(6)} %eq.15), kind=kLoop, calls=%fused_computation.11 | loop fusion | flops 131072 | bytes 524298 | tf_op jit(solution)/shard_map/while/body/eval_jaxpr/jit(_where)/select_n | solution.py:12
  31.3 0.0 all-reduce.3.cloned.1.call-update
  31.3 0.0 copy-done
  31.3 0.0 copy-done.1
  31.4 0.0 copy-start.3
  31.4 0.5 fusion.13
  31.8 0.3 copy-done.3
  32.1 0.2 fusion.1
  32.3 37.3 %psum.33 = bf16[64,128]{1,0:T(8,128)(2,1)S(1)} all-reduce(bf16[64,128]{1,0:T(8,128)(2,1)S(1)} %fusion.1), channel_id=1, replica_groups=mesh['atoms'=8,'sig'=4] {'atoms'}, use_global_device_ids=true, to_apply=%region_1.2 | all-reduce | flops 8192 | bytes 32768 | tf_op jit(solution)/shard_map/while/body/eval_jaxpr/psum | solution.py:13
  69.5 35.7 %all-reduce.3.cloned.1.call-done = (bf16[1024,64]{1,0:T(8,128)(2,1)}, bf16[1024,64]{1,0:T(8,128)(2,1)}) async-done(((bf16[1024,64]{1,0:T(8,128)(2,1)}, bf16[1024,64]{1,0:T(8,128)(2,1)}), (bf16[1024,64]{1,0:T(8,128)(2,1)}, bf16[1024,64]{1,0:T(8,128)(2,1)})) %all-reduce.3.cloned.1.call-update) | async-done | bytes 262160 | tf_op jit(solution)/shard_map/while/body/eval_jaxpr/psum | solution.py:13
  105.2 0.0 copy-start.2
  105.2 1.5 convolution_subtract_fusion.1
  106.7 0.2 fusion.3
  106.9 35.4 %psum.35 = bf16[64,128]{1,0:T(8,128)(2,1)S(1)} all-reduce(bf16[64,128]{1,0:T(8,128)(2,1)S(1)} %fusion.3), channel_id=1, replica_groups=mesh['atoms'=8,'sig'=4] {'atoms'}, use_global_device_ids=true, to_apply=%region_3.4 | all-reduce | flops 8192 | bytes 32768 | tf_op jit(solution)/shard_map/while/body/eval_jaxpr/psum | solution.py:13
  142.3 0.0 copy-done.2
  142.3 1.2 abs_reduce_fusion
  143.4 17.6 %pmax.7 = f32[128]{0:T(128)} all-reduce(f32[128]{0:T(128)S(1)} %get-tuple-element.42), channel_id=1, replica_groups=mesh['atoms'=8,'sig'=4] {'atoms'}, use_global_device_ids=true, to_apply=%region_5.6 | all-reduce | flops 128 | bytes 1024 | tf_op jit(solution)/shard_map/pmax | solution.py:76
  161.1 0.6 pad_maximum_fusion
Async XLA Ops:
  7.2 24.2 %copy-start = (bf16[1024,128]{1,0:T(8,128)(2,1)S(1)}, bf16[1024,128]{1,0:T(8,128)(2,1)}, u32[]{:S(2)}) copy-start(bf16[1024,128]{1,0:T(8,128)(2,1)} %param.4) | copy-start | bytes 786436
  7.2 0.8 copy-start.4
  7.2 22.0 %all-gather.2.cloned.1.call-start = ((), (), s32[]{:S(2)}) async-start(), calls=%async_computation | async-start | bytes 1310720 | tf_op jit(solution)/shard_map/all_gather | solution.py:17
  7.9 97.3 %all-reduce.3.cloned.1.call-start = ((), (), s32[]{:S(2)}) async-start(), calls=%async_computation.1 | async-start | bytes 1048576 | tf_op jit(solution)/shard_map/while/body/eval_jaxpr/psum | solution.py:13
  29.1 2.2 %copy-start.1 = (bf16[1024,512]{1,0:T(8,128)(2,1)S(1)}, bf16[1024,512]{1,0:T(8,128)(2,1)}, u32[]{:S(2)}) copy-start(bf16[1024,512]{1,0:T(8,128)(2,1)} %all-gather.2.cloned.1.call-done) | copy-start | bytes 3145732
  31.4 0.8 copy-start.3
  105.2 37.0 %copy-start.2 = (bf16[1024,64]{1,0:T(8,128)(2,1)S(1)}, bf16[1024,64]{1,0:T(8,128)(2,1)}, u32[]{:S(2)}) copy-start(bf16[1024,64]{1,0:T(8,128)(2,1)} %get-tuple-element.32) | copy-start | bytes 393220
Sparse Core Ops, SparseCore 0:
  9.6 19.5 all-gather.1
  32.6 72.5 all-reduce.2
where the time goes:
time: 169 us
  blocking collectives  90.2 us (53%)
  waiting for transfers between devices  51.7 us (31%)
  between operations  19.3 us (11%)
  matrix products  3.47 us (2%)
  other arithmetic  2.78 us (2%)
    psum x2, blocking collectives, spread(): return lax.psum(block, axis)  72.6 us
    psum x1, waiting for transfers between devices, spread(): return lax.psum(block, axis)  35.7 us
    pmax x1, blocking collectives, shards(): largest = lax.pmax(jnp.max(jnp.abs(correlation), axis=0), 'atoms')  17.6 us
    all_gather x1, waiting for transfers between devices, shards(): gathered = lax.all_gather(dictionary, 'sig', axis=1, tiled=True)  15.3 us
  transfers between devices with their start and end apart: 2, of which 2 were waited for; matrix products, arithmetic and copies ran while one was open for 1% of the time, Pallas kernels for 0%

commit v1 on v0

v1 whole, which is shorter than its diff:
```python
import functools

import jax
import jax.numpy as jnp
from jax import lax
from jax.experimental import pallas as pl
from jax.experimental.pallas import tpu as pltpu
from jax.sharding import PartitionSpec as P

BLK = 64
SB = 128
STEPS = 2

VMEM = pl.BlockSpec(memory_space=pltpu.VMEM)
SMEM = pl.BlockSpec(memory_space=pltpu.SMEM)


def swap(block, axis, size, mask):
    return lax.ppermute(block, axis, [(i, i ^ mask) for i in range(size)])


def matmul(a, b):
    return jnp.dot(a, b, preferred_element_type=jnp.float32)


def pick_kernel(tags, selected, homes, *refs):
    pieces, out = refs[:-1], refs[-1]
    row = lax.broadcasted_iota(jnp.int32, (SB, STEPS * BLK), 0)
    column = lax.broadcasted_iota(jnp.int32, (SB, STEPS * BLK), 1)
    wanted = jnp.where(column < BLK, selected[0, 0] * BLK, selected[1, 0] * BLK - BLK) + column
    total = jnp.zeros(out.shape, jnp.float32)
    for tag, piece in zip(tags, pieces):
        hot = (row + homes[tag] * SB == wanted).astype(jnp.float32).astype(jnp.bfloat16)
        total += matmul(piece[...], hot)
    out[...] = total.astype(jnp.bfloat16)


def pick(selected, homes, tags, pieces):
    return pl.pallas_call(
        functools.partial(pick_kernel, tags),
        out_shape=jax.ShapeDtypeStruct((pieces[0].shape[0], STEPS * BLK), jnp.bfloat16),
        in_specs=[SMEM, SMEM] + [VMEM] * len(pieces),
        out_specs=VMEM,
    )(selected, homes, *pieces)


def exact(matrix, rows):
    high = rows.astype(jnp.bfloat16)
    rest = rows - high.astype(jnp.float32)
    middle = rest.astype(jnp.bfloat16)
    low = (rest - middle.astype(jnp.float32)).astype(jnp.bfloat16)
    return matmul(matrix, low) + matmul(matrix, middle) + matmul(matrix, high)


def finish_kernel(n_terms, n_halves, own, spots, inverses, signals, *refs):
    terms = [refs[i * n_halves : (i + 1) * n_halves] for i in range(n_terms)]
    pieces = refs[n_terms * n_halves : -3]
    corr_out, coef_out, peak_out = refs[-3:]
    halves = []
    for h in range(n_halves):
        total = terms[0][h][...]
        for term in terms[1:]:
            total = total + term[h][...]
        halves.append(total)
    chosen = jnp.concatenate(halves, 0) if n_halves > 1 else halves[0]
    chosen_t = chosen.T
    signals_t = signals[...].T
    rows = matmul(chosen_t, signals[...])
    gram = matmul(chosen_t, chosen).astype(jnp.bfloat16)
    first = exact(inverses[0, 0], rows[:BLK]).astype(jnp.bfloat16)
    rows_next = rows[BLK:] - matmul(gram[BLK:, :BLK], first)
    second = exact(inverses[1, 0], rows_next).astype(jnp.bfloat16)
    coef_out[0] = first
    coef_out[1] = second
    weights_t = jnp.concatenate([first, second], 0).T
    left = jnp.concatenate([signals_t, chosen_t], 0)
    best = jnp.zeros((SB, SB), jnp.float32)
    for i, piece in enumerate(pieces):
        both = matmul(left, piece[...])
        panel_t = both[SB:].astype(jnp.bfloat16)
        corr_t = both[:SB] - matmul(weights_t, panel_t)
        if i < own:
            start = pl.multiple_of(spots[i] * SB, SB)
            corr_out[pl.ds(start, SB), :] = corr_t.T.astype(jnp.bfloat16)
        best = jnp.maximum(best, jnp.abs(corr_t))
    peak_out[...] = jnp.max(best.T, axis=0, keepdims=True)


def finish(spots, inverses, signals, terms, pieces, own):
    n_halves = len(terms[0])
    flat = [half for term in terms for half in term]
    return pl.pallas_call(
        functools.partial(finish_kernel, len(terms), n_halves, own),
        out_shape=(
            jax.ShapeDtypeStruct((own * SB, SB), jnp.bfloat16),
            jax.ShapeDtypeStruct((STEPS, BLK, SB), jnp.bfloat16),
            jax.ShapeDtypeStruct((1, SB), jnp.float32),
        ),
        in_specs=[SMEM] + [VMEM] * (2 + len(flat) + len(pieces)),
        out_specs=(VMEM, VMEM, VMEM),
    )(spots, inverses, signals, *flat, *pieces)


def shards(n_atoms, n_sig, signals, dictionary, selected, inverses):
    me = lax.axis_index("sig")
    group = lax.axis_index("atoms")
    pieces = {0: dictionary}
    bit = n_sig // 2
    while bit:
        for mask in list(pieces):
            pieces[mask | bit] = swap(pieces[mask], "sig", n_sig, bit)
        bit //= 2
    masks = sorted(pieces)
    spots = jnp.stack([me ^ mask for mask in masks])
    listed = [pieces[mask] for mask in masks]
    chosen = pick(selected, group * n_sig + spots, list(range(n_sig)), listed)
    bit = 1
    while bit < n_atoms // 2:
        chosen = chosen + swap(chosen, "atoms", n_atoms, bit)
        bit *= 2
    terms = [[chosen], [swap(chosen, "atoms", n_atoms, bit)]]
    correlations, coefficients, peak = finish(spots, inverses, signals, terms, listed, n_sig)
    bit = 1
    while bit < n_atoms:
        peak = jnp.maximum(peak, swap(peak, "atoms", n_atoms, bit))
        bit *= 2
    return correlations, coefficients, peak[0]


def solution(mesh):
    placed = (P(None, "sig"), P(None, ("atoms", "sig")), P(None, "sig"), P(None, "sig", None, None))
    return jax.shard_map(
        functools.partial(shards, mesh.shape["atoms"], mesh.shape["sig"]),
        mesh=mesh,
        in_specs=placed,
        out_specs=(P("atoms", "sig"), P(None, None, "sig"), P("sig")),
        check_vma=False,
    )
```

time: 169 us -> 64.7 us (0.38)
  blocking collectives: 90.2 us -> 0 us
  between operations: 19.3 us -> 0.68 us
  starting transfers between devices: 0.08 us -> 13.8 us
  waiting for transfers between devices: 51.7 us -> 38 us
  Pallas kernels: 0 us -> 6.32 us
  matrix products: 3.47 us -> 0 us
  local copies, waits for them, and re-layouts: 0.88 us -> 3.45 us
    psum x2 -> x0, blocking collectives: 72.6 us -> none  [spread(): return lax.psum(block, axis)]
    ppermute x0 -> x9, waiting for transfers between devices: none -> 38 us  [swap(): return lax.ppermute(block, axis, [(i, i ^ mask) for i in range(size)])]
    psum x1 -> x0, waiting for transfers between devices: 35.7 us -> none  [spread(): return lax.psum(block, axis)]
    pmax x1 -> x0, blocking collectives: 17.6 us -> none  [shards(): largest = lax.pmax(jnp.max(jnp.abs(correlation), axis=0), 'atoms')]
    all_gather x1 -> x0, waiting for transfers between devices: 15.3 us -> none  [shards(): gathered = lax.all_gather(dictionary, 'sig', axis=1, tiled=True)]
    ppermute x0 -> x9, starting transfers between devices: none -> 13.8 us  [swap(): return lax.ppermute(block, axis, [(i, i ^ mask) for i in range(size)])]
    pallas_call x0 -> x2, Pallas kernels: none -> 6.32 us  [the longest x1 3.98 us: finish(): pl.pallas_call(functools.partial(finish_kernel, len(terms), n_halves, own...]
    dot_general x5 -> x0, matrix products: 3.47 us -> none  [the longest x2 2.69 us: apply_block(): jnp.dot(gram_panel, weights_block, preferred_element_type=jnp.float32)]
  transfers between devices with their start and end apart: 2 -> 9, of which waited for: 2 -> 7; matrix products, arithmetic and copies ran while one was open for 1% -> 2% of each run, Pallas kernels for 0% -> 0%
where the time goes in v1:
time: 64.7 us; the launch traced here: 64.5 us
  waiting for transfers between devices  38 us (59%)
  starting transfers between devices  13.8 us (21%)
  Pallas kernels  6.32 us (10%)
  local copies, waits for them, and re-layouts  3.45 us (5%)
  other arithmetic  2.27 us (4%)
  between operations  0.68 us (1%)
    ppermute x9, waiting for transfers between devices, swap(): return lax.ppermute(block, axis, [(i, i ^ mask) for i in range(size)])  38 us
    ppermute x9, starting transfers between devices, swap(): return lax.ppermute(block, axis, [(i, i ^ mask) for i in range(size)])  13.8 us
    pallas_call x1, Pallas kernels, finish(): pl.pallas_call(functools.partial(finish_kernel, len(terms), n_halves, own...  3.98 us
    unnamed x15, local copies, waits for them, and re-layouts  3.45 us
    pallas_call x1, Pallas kernels, pick(): pl.pallas_call(functools.partial(pick_kernel, tags), out_shape=jax.ShapeD...  2.34 us
  transfers between devices with their start and end apart: 9, of which 7 were waited for; matrix products, arithmetic and copies ran while one was open for 2% of the time, Pallas kernels for 0%

profile of v1, /device:TPU:0, one launch (start us, length us, event | category | flops | bytes accessed | tf_op | source)
XLA Modules:
  0.0 64.5 jit_solution(6368865287820164532)
XLA Ops:
  0.6 3.0 %collective-permute-start.1 = (bf16[1024,128]{1,0:T(8,128)(2,1)}, bf16[1024,128]{1,0:T(8,128)(2,1)S(1)}, u32[]{:S(2)}, u32[]{:S(2)}) collective-permute-start(bf16[1024,128]{1,0:T(8,128)(2,1)} %refs_2_.1), channel_id=1, source_target_pairs={{0,2},{1,3},{2,0},{3,1},{4,6},{5,7},{6,4},{7,5},{8,10},{9,11},{10,... | collective-permute-start | bytes 786440 | tf_op jit(solution)/shard_map/ppermute | solution.py:19
  3.6 0.0 collective-permute-start
  3.6 6.5 %collective-permute-done.1.refs_2_.refs_4_ = bf16[1024,128]{1,0:T(8,128)(2,1)S(1)} collective-permute-done((bf16[1024,128]{1,0:T(8,128)(2,1)}, bf16[1024,128]{1,0:T(8,128)(2,1)S(1)}, u32[]{:S(2)}, u32[]{:S(2)}) %collective-permute-start.1) | collective-permute-done | bytes 262176 | tf_op jit(solution)/shard_map/ppermute | solution.py:19
  10.2 0.0 copy-start.1
  10.2 0.0 collective-permute-start.2
  10.2 0.0 copy-start.5
  10.2 0.7 %copy-done.5 = s32[2,1]{0,1:T(1,128)S(1)} copy-done((s32[2,1]{0,1:T(1,128)S(1)}, s32[2,1]{0,1:T(1,128)}, u32[]{:S(2)}) %copy-start.5) | copy-done | bytes 32
  10.8 0.6 %copy.7.selected = s32[2,1]{1,0:T(2,128)} copy(s32[2,1]{0,1:T(1,128)S(1)} %copy-done.5) | data formatting | bytes 16 | tf_op args[2]
  11.5 0.7 %broadcast_add_fusion = (s32[4]{0:T(128)}, s32[4]{0:T(128)}) fusion(s32[]{:T(128)S(6)} %mul.3, s32[1]{0:T(128)} %bitcast.3, s32[1]{0:T(128)} %bitcast.2, s32[1]{0:T(128)} %bitcast.1, s32[1]{0:T(128)} %bitcast), kind=kLoop, calls=%fused_computation.2 | loop fusion | flops 16 | bytes 52 | tf_op jit(solution)/shard_map/add | solution.py:116
  12.1 0.0 collective-permute-done.refs_1_.refs_3_
  12.1 0.0 copy-start.2
  12.1 0.0 collective-permute-done.2.refs_3_.refs_5_
  12.1 0.0 copy-start.3
  12.1 0.0 copy-done.1
  12.2 0.7 %copy-done.2 = bf16[1024,128]{1,0:T(8,128)(2,1)} copy-done((bf16[1024,128]{1,0:T(8,128)(2,1)}, bf16[1024,128]{1,0:T(8,128)(2,1)S(1)}, u32[]{:S(2)}) %copy-start.2) | copy-done | bytes 262168
  12.8 0.1 copy-done.3
  12.9 2.3 %shard_map.67 = bf16[1024,128]{1,0:T(8,128)(2,1)} custom-call(s32[2,1]{1,0:T(2,128)} %copy.7.selected, s32[4]{0:T(128)} %get-tuple-element.9.homes, bf16[1024,128]{1,0:T(8,128)(2,1)} %refs_2_.1, bf16[1024,128]{1,0:T(8,128)(2,1)} %copy-done.2, bf16[1024,128]{1,0:T(8,128)(2,1)} %copy-done.1, bf16[1024,128]{1,0:T(8,128)(2,1)} %copy-done.3), custom_call_target="tpu_custom_call" | custom-call | tf_op jit(solution)/shard_map/pallas_call | solution.py:39
  15.3 1.8 %collective-permute-start.3 = (bf16[1024,128]{1,0:T(8,128)(2,1)}, bf16[1024,128]{1,0:T(8,128)(2,1)S(1)}, u32[]{:S(2)}, u32[]{:S(2)}) collective-permute-start(bf16[1024,128]{1,0:T(8,128)(2,1)} %shard_map.67), channel_id=1, source_target_pairs={{0,4},{4,0},{8,12},{12,8},{16,20},{20,16},{24,28},{28,24},{1,5},{5... | collective-permute-start | bytes 786440 | tf_op jit(solution)/shard_map/ppermute | solution.py:19
  17.0 7.2 %collective-permute-done.3 = bf16[1024,128]{1,0:T(8,128)(2,1)S(1)} collective-permute-done((bf16[1024,128]{1,0:T(8,128)(2,1)}, bf16[1024,128]{1,0:T(8,128)(2,1)S(1)}, u32[]{:S(2)}, u32[]{:S(2)}) %collective-permute-start.3) | collective-permute-done | bytes 262176 | tf_op jit(solution)/shard_map/ppermute | solution.py:19
  24.2 1.0 %add.14 = bf16[1024,128]{1,0:T(8,128)(2,1)S(1)} add(bf16[1024,128]{1,0:T(8,128)(2,1)} %shard_map.67, bf16[1024,128]{1,0:T(8,128)(2,1)S(1)} %collective-permute-done.3) | non-fusion elementwise | flops 131072 | bytes 786432 | tf_op jit(solution)/shard_map/add | solution.py:119
  25.2 1.9 %collective-permute-start.4 = (bf16[1024,128]{1,0:T(8,128)(2,1)S(1)}, bf16[1024,128]{1,0:T(8,128)(2,1)S(1)}, u32[]{:S(2)}, u32[]{:S(2)}) collective-permute-start(bf16[1024,128]{1,0:T(8,128)(2,1)S(1)} %add.14), channel_id=1, source_target_pairs={{0,8},{4,12},{8,0},{12,4},{16,24},{20,28},{24,16},{28,20},{1,9},{5... | collective-permute-start | bytes 786440 | tf_op jit(solution)/shard_map/ppermute | solution.py:19
  27.1 6.2 %collective-permute-done.4 = bf16[1024,128]{1,0:T(8,128)(2,1)S(1)} collective-permute-done((bf16[1024,128]{1,0:T(8,128)(2,1)S(1)}, bf16[1024,128]{1,0:T(8,128)(2,1)S(1)}, u32[]{:S(2)}, u32[]{:S(2)}) %collective-permute-start.4) | collective-permute-done | bytes 262176 | tf_op jit(solution)/shard_map/ppermute | solution.py:19
  33.3 0.1 add.15.refs_0_
  33.4 0.0 copy-start
  33.4 2.8 %collective-permute-start.5 = (bf16[1024,128]{1,0:T(8,128)(2,1)S(1)}, bf16[1024,128]{1,0:T(8,128)(2,1)S(1)}, u32[]{:S(2)}, u32[]{:S(2)}) collective-permute-start(bf16[1024,128]{1,0:T(8,128)(2,1)S(1)} %add.15.refs_0_), channel_id=1, source_target_pairs={{0,16},{4,20},{8,24},{12,28},{16,0},{20,4},{24,8},{28,12},{1,17},{... | collective-permute-start | bytes 786440 | tf_op jit(solution)/shard_map/ppermute | solution.py:19
  36.2 10.9 %collective-permute-done.5.refs_1_ = bf16[1024,128]{1,0:T(8,128)(2,1)S(1)} collective-permute-done((bf16[1024,128]{1,0:T(8,128)(2,1)S(1)}, bf16[1024,128]{1,0:T(8,128)(2,1)S(1)}, u32[]{:S(2)}, u32[]{:S(2)}) %collective-permute-start.5) | collective-permute-done | bytes 262176 | tf_op jit(solution)/shard_map/ppermute | solution.py:19
  47.1 0.0 copy-start.4
  47.1 0.0 copy-done
  47.1 0.7 %copy-done.4 = bf16[1024,128]{1,0:T(8,128)(2,1)} copy-done((bf16[1024,128]{1,0:T(8,128)(2,1)}, bf16[1024,128]{1,0:T(8,128)(2,1)S(1)}, u32[]{:S(2)}) %copy-start.4) | copy-done | bytes 262168
  47.8 4.0 %shard_map.68 = (bf16[512,128]{1,0:T(8,128)(2,1)}, bf16[2,64,128]{2,1,0:T(8,128)(2,1)}, f32[1,128]{1,0:T(1,128)}) custom-call(s32[4]{0:T(128)} %get-tuple-element.10.spots, bf16[2,1,64,64]{3,2,1,0:T(8,128)(2,1)} %inverses.1, bf16[1024,128]{1,0:T(8,128)(2,1)} %signals.1, bf16[1024,128]{1,0:T(8,128)(2,1)} %copy-done, bf16[1024,128]{1,0:T(8,128)(2,1)} %copy-done.4, ...), custom_call_target="tpu_custom_call" | custom-call | tf_op jit(solution)/shard_map/pallas_call | solution.py:92
  51.8 0.0 copy-start.6
  51.8 0.7 %copy-done.6 = f32[1,128]{1,0:T(1,128)S(1)} copy-done((f32[1,128]{1,0:T(1,128)S(1)}, f32[1,128]{1,0:T(1,128)}, u32[]{:S(2)}) %copy-start.6) | copy-done | bytes 536
  52.5 1.6 %collective-permute-start.6 = (f32[1,128]{1,0:T(1,128)S(1)}, f32[1,128]{1,0:T(1,128)S(1)}, u32[]{:S(2)}, u32[]{:S(2)}) collective-permute-start(f32[1,128]{1,0:T(1,128)S(1)} %copy-done.6), channel_id=1, source_target_pairs={{0,4},{4,0},{8,12},{12,8},{16,20},{20,16},{24,28},{28,24},{1,5},{5... | collective-permute-start | bytes 1544 | tf_op jit(solution)/shard_map/ppermute | solution.py:19
  54.1 2.0 %collective-permute-done.6 = f32[1,128]{1,0:T(1,128)S(1)} collective-permute-done((f32[1,128]{1,0:T(1,128)S(1)}, f32[1,128]{1,0:T(1,128)S(1)}, u32[]{:S(2)}, u32[]{:S(2)}) %collective-permute-start.6) | collective-permute-done | bytes 544 | tf_op jit(solution)/shard_map/ppermute | solution.py:19
  56.0 0.7 %collective-permute-start.7 = (f32[1,128]{1,0:T(1,128)S(1)}, f32[1,128]{1,0:T(1,128)S(1)}, u32[]{:S(2)}, u32[]{:S(2)}) collective-permute-start(f32[1,128]{1,0:T(1,128)S(1)} %max.9), channel_id=1, source_target_pairs={{0,8},{4,12},{8,0},{12,4},{16,24},{20,28},{24,16},{28,20},{1,9},{5... | collective-permute-start | bytes 1544 | tf_op jit(solution)/shard_map/ppermute | solution.py:19
  56.7 2.8 %collective-permute-done.7 = f32[1,128]{1,0:T(1,128)S(1)} collective-permute-done((f32[1,128]{1,0:T(1,128)S(1)}, f32[1,128]{1,0:T(1,128)S(1)}, u32[]{:S(2)}, u32[]{:S(2)}) %collective-permute-start.7) | collective-permute-done | bytes 544 | tf_op jit(solution)/shard_map/ppermute | solution.py:19
  59.6 2.1 %collective-permute-start.8 = (f32[1,128]{1,0:T(1,128)S(1)}, f32[1,128]{1,0:T(1,128)S(1)}, u32[]{:S(2)}, u32[]{:S(2)}) collective-permute-start(f32[1,128]{1,0:T(1,128)S(1)} %max.10), channel_id=1, source_target_pairs={{0,16},{4,20},{8,24},{12,28},{16,0},{20,4},{24,8},{28,12},{1,17},{... | collective-permute-start | bytes 1544 | tf_op jit(solution)/shard_map/ppermute | solution.py:19
  61.7 2.4 %collective-permute-done.8 = f32[1,128]{1,0:T(1,128)S(1)} collective-permute-done((f32[1,128]{1,0:T(1,128)S(1)}, f32[1,128]{1,0:T(1,128)S(1)}, u32[]{:S(2)}, u32[]{:S(2)}) %collective-permute-start.8) | collective-permute-done | bytes 544 | tf_op jit(solution)/shard_map/ppermute | solution.py:19
  64.0 0.5 maximum_bitcast_fusion
  (2 shorter events, 0.0 us)
Async XLA Ops:
  0.6 9.5 %collective-permute-start.1 = (bf16[1024,128]{1,0:T(8,128)(2,1)}, bf16[1024,128]{1,0:T(8,128)(2,1)S(1)}, u32[]{:S(2)}, u32[]{:S(2)}) collective-permute-start(bf16[1024,128]{1,0:T(8,128)(2,1)} %refs_2_.1), channel_id=1, source_target_pairs={{0,2},{1,3},{2,0},{3,1},{4,6},{5,7},{6,4},{7,5},{8,10},{9,11},{10,... | collective-permute-start | bytes 786440 | tf_op jit(solution)/shard_map/ppermute | solution.py:19
  3.6 8.5 %collective-permute-start = (bf16[1024,128]{1,0:T(8,128)(2,1)}, bf16[1024,128]{1,0:T(8,128)(2,1)S(1)}, u32[]{:S(2)}, u32[]{:S(2)}) collective-permute-start(bf16[1024,128]{1,0:T(8,128)(2,1)} %refs_2_.1), channel_id=1, source_target_pairs={{0,1},{1,0},{2,3},{3,2},{4,5},{5,4},{6,7},{7,6},{8,9},{9,8},{10,11... | collective-permute-start | bytes 786440 | tf_op jit(solution)/shard_map/ppermute | solution.py:19
  10.2 2.0 %copy-start.1 = (bf16[1024,128]{1,0:T(8,128)(2,1)}, bf16[1024,128]{1,0:T(8,128)(2,1)S(1)}, u32[]{:S(2)}) copy-start(bf16[1024,128]{1,0:T(8,128)(2,1)S(1)} %collective-permute-done.1.refs_2_.refs_4_) | copy-start | bytes 786436
  10.2 2.0 %collective-permute-start.2 = (bf16[1024,128]{1,0:T(8,128)(2,1)S(1)}, bf16[1024,128]{1,0:T(8,128)(2,1)S(1)}, u32[]{:S(2)}, u32[]{:S(2)}) collective-permute-start(bf16[1024,128]{1,0:T(8,128)(2,1)S(1)} %collective-permute-done.1.refs_2_.refs_4_), channel_id=1, source_target_pairs={{0,1},{1,0},{2,3},{3,2},{4,5},{5,4},{6,7},{7,6},{8,9},{9,8},{10,11... | collective-permute-start | bytes 786440 | tf_op jit(solution)/shard_map/ppermute | solution.py:19
  10.2 0.7 %copy-start.5 = (s32[2,1]{0,1:T(1,128)S(1)}, s32[2,1]{0,1:T(1,128)}, u32[]{:S(2)}) copy-start(s32[2,1]{0,1:T(1,128)} %param.6) | copy-start | bytes 28
  12.1 0.7 %copy-start.2 = (bf16[1024,128]{1,0:T(8,128)(2,1)}, bf16[1024,128]{1,0:T(8,128)(2,1)S(1)}, u32[]{:S(2)}) copy-start(bf16[1024,128]{1,0:T(8,128)(2,1)S(1)} %collective-permute-done.refs_1_.refs_3_) | copy-start | bytes 786436
  12.1 0.8 %copy-start.3 = (bf16[1024,128]{1,0:T(8,128)(2,1)}, bf16[1024,128]{1,0:T(8,128)(2,1)S(1)}, u32[]{:S(2)}) copy-start(bf16[1024,128]{1,0:T(8,128)(2,1)S(1)} %collective-permute-done.2.refs_3_.refs_5_) | copy-start | bytes 786436
  15.3 9.0 %collective-permute-start.3 = (bf16[1024,128]{1,0:T(8,128)(2,1)}, bf16[1024,128]{1,0:T(8,128)(2,1)S(1)}, u32[]{:S(2)}, u32[]{:S(2)}) collective-permute-start(bf16[1024,128]{1,0:T(8,128)(2,1)} %shard_map.67), channel_id=1, source_target_pairs={{0,4},{4,0},{8,12},{12,8},{16,20},{20,16},{24,28},{28,24},{1,5},{5... | collective-permute-start | bytes 786440 | tf_op jit(solution)/shard_map/ppermute | solution.py:19
  25.2 8.1 %collective-permute-start.4 = (bf16[1024,128]{1,0:T(8,128)(2,1)S(1)}, bf16[1024,128]{1,0:T(8,128)(2,1)S(1)}, u32[]{:S(2)}, u32[]{:S(2)}) collective-permute-start(bf16[1024,128]{1,0:T(8,128)(2,1)S(1)} %add.14), channel_id=1, source_target_pairs={{0,8},{4,12},{8,0},{12,4},{16,24},{20,28},{24,16},{28,20},{1,9},{5... | collective-permute-start | bytes 786440 | tf_op jit(solution)/shard_map/ppermute | solution.py:19
  33.4 13.8 %copy-start = (bf16[1024,128]{1,0:T(8,128)(2,1)}, bf16[1024,128]{1,0:T(8,128)(2,1)S(1)}, u32[]{:S(2)}) copy-start(bf16[1024,128]{1,0:T(8,128)(2,1)S(1)} %add.15.refs_0_) | copy-start | bytes 786436
  33.4 13.7 %collective-permute-start.5 = (bf16[1024,128]{1,0:T(8,128)(2,1)S(1)}, bf16[1024,128]{1,0:T(8,128)(2,1)S(1)}, u32[]{:S(2)}, u32[]{:S(2)}) collective-permute-start(bf16[1024,128]{1,0:T(8,128)(2,1)S(1)} %add.15.refs_0_), channel_id=1, source_target_pairs={{0,16},{4,20},{8,24},{12,28},{16,0},{20,4},{24,8},{28,12},{1,17},{... | collective-permute-start | bytes 786440 | tf_op jit(solution)/shard_map/ppermute | solution.py:19
  47.1 0.7 %copy-start.4 = (bf16[1024,128]{1,0:T(8,128)(2,1)}, bf16[1024,128]{1,0:T(8,128)(2,1)S(1)}, u32[]{:S(2)}) copy-start(bf16[1024,128]{1,0:T(8,128)(2,1)S(1)} %collective-permute-done.5.refs_1_) | copy-start | bytes 786436
  51.8 0.7 %copy-start.6 = (f32[1,128]{1,0:T(1,128)S(1)}, f32[1,128]{1,0:T(1,128)}, u32[]{:S(2)}) copy-start(f32[1,128]{1,0:T(1,128)} %get-tuple-element.8) | copy-start | bytes 1540
  52.5 3.5 %collective-permute-start.6 = (f32[1,128]{1,0:T(1,128)S(1)}, f32[1,128]{1,0:T(1,128)S(1)}, u32[]{:S(2)}, u32[]{:S(2)}) collective-permute-start(f32[1,128]{1,0:T(1,128)S(1)} %copy-done.6), channel_id=1, source_target_pairs={{0,4},{4,0},{8,12},{12,8},{16,20},{20,16},{24,28},{28,24},{1,5},{5... | collective-permute-start | bytes 1544 | tf_op jit(solution)/shard_map/ppermute | solution.py:19
  56.0 3.5 %collective-permute-start.7 = (f32[1,128]{1,0:T(1,128)S(1)}, f32[1,128]{1,0:T(1,128)S(1)}, u32[]{:S(2)}, u32[]{:S(2)}) collective-permute-start(f32[1,128]{1,0:T(1,128)S(1)} %max.9), channel_id=1, source_target_pairs={{0,8},{4,12},{8,0},{12,4},{16,24},{20,28},{24,16},{28,20},{1,9},{5... | collective-permute-start | bytes 1544 | tf_op jit(solution)/shard_map/ppermute | solution.py:19
  59.6 4.4 %collective-permute-start.8 = (f32[1,128]{1,0:T(1,128)S(1)}, f32[1,128]{1,0:T(1,128)S(1)}, u32[]{:S(2)}, u32[]{:S(2)}) collective-permute-start(f32[1,128]{1,0:T(1,128)S(1)} %max.10), channel_id=1, source_target_pairs={{0,16},{4,20},{8,24},{12,28},{16,0},{20,4},{24,8},{28,12},{1,17},{... | collective-permute-start | bytes 1544 | tf_op jit(solution)/shard_map/ppermute | solution.py:19

commit v2 on v1

v2 whole, which is shorter than its diff:
```python
import functools

import jax
import jax.numpy as jnp
from jax import lax
from jax.experimental import pallas as pl
from jax.experimental.pallas import tpu as pltpu
from jax.sharding import PartitionSpec as P

BLK = 64
SB = 128
STEPS = 2

VMEM = pl.BlockSpec(memory_space=pltpu.VMEM)
SMEM = pl.BlockSpec(memory_space=pltpu.SMEM)


def swap(block, axis, size, mask):
    return lax.ppermute(block, axis, [(i, i ^ mask) for i in range(size)])


def near(array):
    return pltpu.with_memory_space_constraint(array, pltpu.VMEM)


def matmul(a, b):
    return jnp.dot(a, b, preferred_element_type=jnp.float32)


def pick_kernel(n_sig, masks, selected, *refs):
    pieces, out = refs[:-1], refs[-1]
    row = lax.broadcasted_iota(jnp.int32, (SB, STEPS * BLK), 0)
    column = lax.broadcasted_iota(jnp.int32, (SB, STEPS * BLK), 1)
    wanted = jnp.where(column < BLK, selected[0, 0] * BLK, selected[1, 0] * BLK - BLK) + column
    me, group = lax.axis_index("sig"), lax.axis_index("atoms")
    total = jnp.zeros(out.shape, jnp.float32)
    for (side, mask), piece in zip(masks, pieces):
        home = (group ^ side) * n_sig + (me ^ mask)
        hot = (row + home * SB == wanted).astype(jnp.float32).astype(jnp.bfloat16)
        total += matmul(piece[...], hot)
    out[...] = total.astype(jnp.bfloat16)


def pick(n_sig, selected, masks, pieces):
    return pl.pallas_call(
        functools.partial(pick_kernel, n_sig, masks),
        out_shape=pltpu.VMEM((pieces[0].shape[0], STEPS * BLK), jnp.bfloat16),
        in_specs=[SMEM] + [VMEM] * len(pieces),
        out_specs=VMEM,
    )(selected, *[near(piece) for piece in pieces])


def exact(matrix, rows):
    high = rows.astype(jnp.bfloat16)
    rest = rows - high.astype(jnp.float32)
    middle = rest.astype(jnp.bfloat16)
    low = (rest - middle.astype(jnp.float32)).astype(jnp.bfloat16)
    return matmul(matrix, low) + matmul(matrix, middle) + matmul(matrix, high)


def finish_kernel(shape, own, inverses, signals, *refs):
    n_halves, n_terms, n_pieces = shape
    terms = [refs[h * n_terms : (h + 1) * n_terms] for h in range(n_halves)]
    rest = refs[n_terms * n_halves : -3]
    pieces = [rest[i * n_halves : (i + 1) * n_halves] for i in range(n_pieces)]
    corr_out, coef_out, peak_out = refs[-3:]
    rows = gram = None
    lefts, start = [], 0
    for parts in terms:
        chosen = parts[0][...]
        for term in parts[1:]:
            chosen = chosen + term[...]
        depth = chosen.shape[0]
        chosen_t = chosen.T
        here = signals[start : start + depth]
        right = matmul(chosen_t, jnp.concatenate([here, chosen], 1))
        rows = right if rows is None else rows + right
        lefts.append(jnp.concatenate([here.T, chosen_t], 0))
        start += depth
    gram = rows[:, SB:].astype(jnp.bfloat16)
    rows = rows[:, :SB]
    first = exact(inverses[0, 0], rows[:BLK]).astype(jnp.bfloat16)
    rows_next = rows[BLK:] - matmul(gram[BLK:, :BLK], first)
    second = exact(inverses[1, 0], rows_next).astype(jnp.bfloat16)
    coef_out[0] = first
    coef_out[1] = second
    weights_t = jnp.concatenate([first, second], 0).T
    me = lax.axis_index("sig")
    best = jnp.zeros((SB, SB), jnp.float32)
    for i, piece in enumerate(pieces):
        both = matmul(lefts[0], piece[0][...])
        for left, part in zip(lefts[1:], piece[1:]):
            both += matmul(left, part[...])
        panel_t = both[SB:].astype(jnp.bfloat16)
        corr_t = both[:SB] - matmul(weights_t, panel_t)
        if i < own:
            at = pl.multiple_of((me ^ i) * SB, SB)
            corr_out[pl.ds(at, SB), :] = corr_t.T.astype(jnp.bfloat16)
        best = jnp.maximum(best, jnp.abs(corr_t))
    peak_out[...] = jnp.max(best.T, axis=0, keepdims=True)


def finish(inverses, signals, terms, pieces, own):
    shape = (len(terms), len(terms[0]), len(pieces))
    flat = [term for parts in terms for term in parts] + [part for piece in pieces for part in piece]
    return pl.pallas_call(
        functools.partial(finish_kernel, shape, own),
        out_shape=(
            jax.ShapeDtypeStruct((own * SB, SB), jnp.bfloat16),
            jax.ShapeDtypeStruct((STEPS, BLK, SB), jnp.bfloat16),
            pltpu.VMEM((1, SB), jnp.float32),
        ),
        in_specs=[VMEM] * (2 + len(flat)),
        out_specs=(VMEM, VMEM, VMEM),
    )(inverses, near(signals), *[near(array) for array in flat])


CHUNKS = 2
MERGE = True
ALTERNATE = True


def shards(n_atoms, n_sig, signals, dictionary, selected, inverses):
    depth = dictionary.shape[0] // CHUNKS
    parts = [dictionary[h * depth : (h + 1) * depth] for h in range(CHUNKS)]
    top = n_atoms // 2
    bits = []
    bit = 1
    while bit < (top if MERGE else n_atoms):
        bits.append(bit)
        bit *= 2
    sides = [0, top] if MERGE else [0]
    masks = list(range(n_sig))
    order_of = [(side, mask) for side in sides for mask in masks]
    held, terms = [], []
    for h, part in enumerate(parts):
        have = {}
        for side in reversed(sides):
            pieces = {0: swap(part, "atoms", n_atoms, side) if side else part}
            bit = n_sig // 2
            while bit:
                for mask in list(pieces):
                    pieces[mask | bit] = swap(pieces[mask], "sig", n_sig, bit)
                bit //= 2
            have[side] = pieces
        listed = [have[side][mask] for side in sides for mask in masks]
        held.append(listed)
        chosen = pick(n_sig, selected, order_of, listed)
        order = list(bits)
        if ALTERNATE and h % 2 and len(order) > 1:
            order[0], order[1] = order[1], order[0]
        for bit in order[:-1]:
            chosen = chosen + swap(chosen, "atoms", n_atoms, bit)
        terms.append([chosen, swap(chosen, "atoms", n_atoms, order[-1])])
    pieces = [[held[h][i] for h in range(CHUNKS)] for i in range(len(held[0]))]
    correlations, coefficients, peak = finish(inverses, signals, terms, pieces, n_sig)
    for bit in bits:
        peak = jnp.maximum(peak, swap(peak, "atoms", n_atoms, bit))
    return correlations, coefficients, peak[0]


def solution(mesh):
    placed = (P(None, "sig"), P(None, ("atoms", "sig")), P(None, "sig"), P(None, "sig", None, None))
    return jax.shard_map(
        functools.partial(shards, mesh.shape["atoms"], mesh.shape["sig"]),
        mesh=mesh,
        in_specs=placed,
        out_specs=(P("atoms", "sig"), P(None, None, "sig"), P("sig")),
        check_vma=False,
    )
```

time: 64.7 us -> 50.2 us (0.78)
  waiting for transfers between devices: 38 us -> 22.3 us
  starting transfers between devices: 13.8 us -> 18.1 us
  local copies, waits for them, and re-layouts: 3.45 us -> 1.65 us
  other arithmetic: 2.27 us -> 0.59 us
    ppermute x9 -> x20, waiting for transfers between devices: 38 us -> 22.3 us  [swap(): return lax.ppermute(block, axis, [(i, i ^ mask) for i in range(size)])]
    ppermute x9 -> x20, starting transfers between devices: 13.8 us -> 18.1 us  [swap(): return lax.ppermute(block, axis, [(i, i ^ mask) for i in range(size)])]
    unnamed x15 -> x5, local copies, waits for them, and re-layouts: 3.45 us -> 0.66 us
    add x2, other arithmetic: 1.1 us -> 0.08 us  [shards(): chosen = chosen + swap(chosen, 'atoms', n_atoms, bit)]
    slice x0 -> x1, local copies, waits for them, and re-layouts: none -> 0.99 us  [shards(): parts = [dictionary[h * depth:(h + 1) * depth] for h in range(CHUNKS)]]
    add x1 -> x0, other arithmetic: 0.66 us -> none  [shards(): chosen = pick(selected, group * n_sig + spots, list(range(n_sig)), listed)]
    pallas_call x2 -> x3, Pallas kernels: 6.32 us -> 6.65 us  [the longest x1 4.41 us: finish(): pl.pallas_call(functools.partial(finish_kernel, shape, own), out_shape=(j...]
  transfers between devices with their start and end apart: 9 -> 20, of which waited for: 7 -> 8; matrix products, arithmetic and copies ran while one was open for 2% -> 1% of each run, Pallas kernels for 0% -> 4%
where the time goes in v2:
time: 50.2 us; the launch traced here: 50 us
  waiting for transfers between devices  22.3 us (44%)
  starting transfers between devices  18.1 us (36%)
  Pallas kernels  6.65 us (13%)
  local copies, waits for them, and re-layouts  1.65 us (3%)
  between operations  0.71 us (1%)
  other arithmetic  0.59 us (1%)
    ppermute x20, waiting for transfers between devices, swap(): return lax.ppermute(block, axis, [(i, i ^ mask) for i in range(size)])  22.3 us
    ppermute x20, starting transfers between devices, swap(): return lax.ppermute(block, axis, [(i, i ^ mask) for i in range(size)])  18.1 us
    pallas_call x1, Pallas kernels, finish(): pl.pallas_call(functools.partial(finish_kernel, shape, own), out_shape=(j...  4.41 us
    pallas_call x2, Pallas kernels, pick(): pl.pallas_call(functools.partial(pick_kernel, n_sig, masks), out_shape=pl...  2.24 us
  transfers between devices with their start and end apart: 20, of which 8 were waited for; matrix products, arithmetic and copies ran while one was open for 1% of the time, Pallas kernels for 4%

profile of v2, /device:TPU:0, one launch (start us, length us, event | category | flops | bytes accessed | tf_op | source)
XLA Modules:
  0.0 50.0 jit_solution(414508538298275720)
XLA Ops:
  0.6 1.0 %fusion = (bf16[512,128]{1,0:T(8,128)(2,1)S(1)}, bf16[512,128]{1,0:T(8,128)(2,1)S(1)}) fusion(bf16[1024,128]{1,0:T(8,128)(2,1)} %param.5), kind=kLoop, calls=%fused_computation.1 | loop fusion | bytes 524288 | tf_op jit(solution)/shard_map/slice | solution.py:125
  1.6 0.0 copy-start.1
  1.6 4.1 %collective-permute-start.12 = (bf16[512,128]{1,0:T(8,128)(2,1)S(1)}, bf16[512,128]{1,0:T(8,128)(2,1)S(1)}, u32[]{:S(2)}, u32[]{:S(2)}) collective-permute-start(bf16[512,128]{1,0:T(8,128)(2,1)S(1)} %get-tuple-element.9.refs_0_.refs_5_), channel_id=1, source_target_pairs={{0,16},{4,20},{8,24},{12,28},{16,0},{20,4},{24,8},{28,12},{1,17},{... | collective-permute-start | bytes 393224 | tf_op jit(solution)/shard_map/ppermute | solution.py:19
  5.7 1.5 %collective-permute-start.10 = (bf16[512,128]{1,0:T(8,128)(2,1)S(1)}, bf16[512,128]{1,0:T(8,128)(2,1)S(1)}, u32[]{:S(2)}, u32[]{:S(2)}) collective-permute-start(bf16[512,128]{1,0:T(8,128)(2,1)S(1)} %get-tuple-element.9.refs_0_.refs_5_), channel_id=1, source_target_pairs={{0,2},{1,3},{2,0},{3,1},{4,6},{5,7},{6,4},{7,5},{8,10},{9,11},{10,... | collective-permute-start | bytes 393224 | tf_op jit(solution)/shard_map/ppermute | solution.py:19
  7.2 0.0 collective-permute-start.9
  7.2 0.3 collective-permute-start.3
  7.6 0.3 collective-permute-start.1
  7.8 7.7 %collective-permute-done.12.refs_4_.refs_13_ = bf16[512,128]{1,0:T(8,128)(2,1)S(1)} collective-permute-done((bf16[512,128]{1,0:T(8,128)(2,1)S(1)}, bf16[512,128]{1,0:T(8,128)(2,1)S(1)}, u32[]{:S(2)}, u32[]{:S(2)}) %collective-permute-start.12) | collective-permute-done | bytes 131104 | tf_op jit(solution)/shard_map/ppermute | solution.py:19
  15.6 1.9 %collective-permute-start.14 = (bf16[512,128]{1,0:T(8,128)(2,1)S(1)}, bf16[512,128]{1,0:T(8,128)(2,1)S(1)}, u32[]{:S(2)}, u32[]{:S(2)}) collective-permute-start(bf16[512,128]{1,0:T(8,128)(2,1)S(1)} %collective-permute-done.12.refs_4_.refs_13_), channel_id=1, source_target_pairs={{0,2},{1,3},{2,0},{3,1},{4,6},{5,7},{6,4},{7,5},{8,10},{9,11},{10,... | collective-permute-start | bytes 393224 | tf_op jit(solution)/shard_map/ppermute | solution.py:19
  17.5 0.0 collective-permute-done.10.refs_2_.refs_9_
  17.5 0.0 collective-permute-start.13
  17.5 0.0 collective-permute-done.9.refs_1_.refs_7_
  17.5 0.5 %collective-permute-start.11 = (bf16[512,128]{1,0:T(8,128)(2,1)S(1)}, bf16[512,128]{1,0:T(8,128)(2,1)S(1)}, u32[]{:S(2)}, u32[]{:S(2)}) collective-permute-start(bf16[512,128]{1,0:T(8,128)(2,1)S(1)} %collective-permute-done.10.refs_2_.refs_9_), channel_id=1, source_target_pairs={{0,1},{1,0},{2,3},{3,2},{4,5},{5,4},{6,7},{7,6},{8,9},{9,8},{10,11... | collective-permute-start | bytes 393224 | tf_op jit(solution)/shard_map/ppermute | solution.py:19
  18.0 0.0 collective-permute-done.3.refs_4_.refs_12_
  18.0 1.2 %collective-permute-start.5 = (bf16[512,128]{1,0:T(8,128)(2,1)S(1)}, bf16[512,128]{1,0:T(8,128)(2,1)S(1)}, u32[]{:S(2)}, u32[]{:S(2)}) collective-permute-start(bf16[512,128]{1,0:T(8,128)(2,1)S(1)} %collective-permute-done.3.refs_4_.refs_12_), channel_id=1, source_target_pairs={{0,2},{1,3},{2,0},{3,1},{4,6},{5,7},{6,4},{7,5},{8,10},{9,11},{10,... | collective-permute-start | bytes 393224 | tf_op jit(solution)/shard_map/ppermute | solution.py:19
  19.2 0.0 collective-permute-done.1.refs_2_.refs_8_
  19.2 0.0 collective-permute-start
  19.2 2.1 %collective-permute-done.14.refs_6_.refs_17_ = bf16[512,128]{1,0:T(8,128)(2,1)S(1)} collective-permute-done((bf16[512,128]{1,0:T(8,128)(2,1)S(1)}, bf16[512,128]{1,0:T(8,128)(2,1)S(1)}, u32[]{:S(2)}, u32[]{:S(2)}) %collective-permute-start.14) | collective-permute-done | bytes 131104 | tf_op jit(solution)/shard_map/ppermute | solution.py:19
  21.3 0.0 collective-permute-start.15
  21.3 0.0 collective-permute-done.13.refs_5_.refs_15_
  21.3 0.5 %collective-permute-start.4 = (bf16[512,128]{1,0:T(8,128)(2,1)S(1)}, bf16[512,128]{1,0:T(8,128)(2,1)S(1)}, u32[]{:S(2)}, u32[]{:S(2)}) collective-permute-start(bf16[512,128]{1,0:T(8,128)(2,1)S(1)} %collective-permute-done.3.refs_4_.refs_12_), channel_id=1, source_target_pairs={{0,1},{1,0},{2,3},{3,2},{4,5},{5,4},{6,7},{7,6},{8,9},{9,8},{10,11... | collective-permute-start | bytes 393224 | tf_op jit(solution)/shard_map/ppermute | solution.py:19
  21.8 0.0 collective-permute-done.11.refs_3_.refs_11_
  21.8 0.1 collective-permute-start.2
  21.9 1.6 %collective-permute-done.5.refs_6_.refs_16_ = bf16[512,128]{1,0:T(8,128)(2,1)S(1)} collective-permute-done((bf16[512,128]{1,0:T(8,128)(2,1)S(1)}, bf16[512,128]{1,0:T(8,128)(2,1)S(1)}, u32[]{:S(2)}, u32[]{:S(2)}) %collective-permute-start.5) | collective-permute-done | bytes 131104 | tf_op jit(solution)/shard_map/ppermute | solution.py:19
  23.5 0.0 collective-permute-start.6
  23.5 0.6 %copy.7.selected = s32[2,1]{1,0:T(2,128)} copy(s32[2,1]{0,1:T(1,128)S(1)} %copy-done.1) | data formatting | bytes 16 | tf_op args[2]
  24.2 0.0 collective-permute-done.15.refs_7_.refs_19_
  24.2 1.1 %shard_map.68 = bf16[512,128]{1,0:T(8,128)(2,1)S(1)} custom-call(s32[2,1]{1,0:T(2,128)} %copy.7.selected, bf16[512,128]{1,0:T(8,128)(2,1)S(1)} %get-tuple-element.9.refs_0_.refs_5_, bf16[512,128]{1,0:T(8,128)(2,1)S(1)} %collective-permute-done.9.refs_1_.refs_7_, bf16[512,128]{1,0:T(8,128)(2,1)S(1)} %collective-permute-done.10.refs_2_.refs_9_, ...), custom_call_target="tpu_custom_call" | custom-call | tf_op jit(solution)/shard_map/pallas_call | solution.py:45
  25.3 0.4 collective-permute-start.16
  25.6 0.0 collective-permute-done.refs_1_.refs_6_
  25.7 0.0 collective-permute-done.4.refs_5_.refs_14_
  25.7 0.0 collective-permute-done.2.refs_3_.refs_10_
  25.7 0.0 collective-permute-done.6.refs_7_.refs_18_
  25.7 1.1 %shard_map.67 = bf16[512,128]{1,0:T(8,128)(2,1)S(1)} custom-call(s32[2,1]{1,0:T(2,128)} %copy.7.selected, bf16[512,128]{1,0:T(8,128)(2,1)S(1)} %get-tuple-element.10.refs_0_.refs_4_, bf16[512,128]{1,0:T(8,128)(2,1)S(1)} %collective-permute-done.refs_1_.refs_6_, bf16[512,128]{1,0:T(8,128)(2,1)S(1)} %collective-permute-done.1.refs_2_.refs_8_, ...), custom_call_target="tpu_custom_call" | custom-call | tf_op jit(solution)/shard_map/pallas_call | solution.py:45
  26.8 1.6 %collective-permute-start.7 = (bf16[512,128]{1,0:T(8,128)(2,1)S(1)}, bf16[512,128]{1,0:T(8,128)(2,1)S(1)}, u32[]{:S(2)}, u32[]{:S(2)}) collective-permute-start(bf16[512,128]{1,0:T(8,128)(2,1)S(1)} %shard_map.67), channel_id=1, source_target_pairs={{0,4},{4,0},{8,12},{12,8},{16,20},{20,16},{24,28},{28,24},{1,5},{5... | collective-permute-start | bytes 393224 | tf_op jit(solution)/shard_map/ppermute | solution.py:19
  28.4 2.9 %collective-permute-done.16 = bf16[512,128]{1,0:T(8,128)(2,1)S(1)} collective-permute-done((bf16[512,128]{1,0:T(8,128)(2,1)S(1)}, bf16[512,128]{1,0:T(8,128)(2,1)S(1)}, u32[]{:S(2)}, u32[]{:S(2)}) %collective-permute-start.16) | collective-permute-done | bytes 131104 | tf_op jit(solution)/shard_map/ppermute | solution.py:19
  31.3 0.0 copy-start
  31.3 1.6 %collective-permute-start.17 = (bf16[512,128]{1,0:T(8,128)(2,1)S(1)}, bf16[512,128]{1,0:T(8,128)(2,1)S(1)}, u32[]{:S(2)}, u32[]{:S(2)}) collective-permute-start(bf16[512,128]{1,0:T(8,128)(2,1)S(1)} %add.7.refs_2_), channel_id=1, source_target_pairs={{0,4},{4,0},{8,12},{12,8},{16,20},{20,16},{24,28},{28,24},{1,5},{5... | collective-permute-start | bytes 393224 | tf_op jit(solution)/shard_map/ppermute | solution.py:19
  32.9 0.0 collective-permute-done.7
  33.0 1.6 %collective-permute-start.8 = (bf16[512,128]{1,0:T(8,128)(2,1)S(1)}, bf16[512,128]{1,0:T(8,128)(2,1)S(1)}, u32[]{:S(2)}, u32[]{:S(2)}) collective-permute-start(bf16[512,128]{1,0:T(8,128)(2,1)S(1)} %add.6.refs_0_), channel_id=1, source_target_pairs={{0,8},{4,12},{8,0},{12,4},{16,24},{20,28},{24,16},{28,20},{1,9},{5... | collective-permute-start | bytes 393224 | tf_op jit(solution)/shard_map/ppermute | solution.py:19
  34.5 2.0 %collective-permute-done.17.refs_3_ = bf16[512,128]{1,0:T(8,128)(2,1)S(1)} collective-permute-done((bf16[512,128]{1,0:T(8,128)(2,1)S(1)}, bf16[512,128]{1,0:T(8,128)(2,1)S(1)}, u32[]{:S(2)}, u32[]{:S(2)}) %collective-permute-start.17) | collective-permute-done | bytes 131104 | tf_op jit(solution)/shard_map/ppermute | solution.py:19
  36.5 1.5 %collective-permute-done.8.refs_1_ = bf16[512,128]{1,0:T(8,128)(2,1)S(1)} collective-permute-done((bf16[512,128]{1,0:T(8,128)(2,1)S(1)}, bf16[512,128]{1,0:T(8,128)(2,1)S(1)}, u32[]{:S(2)}, u32[]{:S(2)}) %collective-permute-start.8) | collective-permute-done | bytes 131104 | tf_op jit(solution)/shard_map/ppermute | solution.py:19
  38.0 4.4 %shard_map.69 = (bf16[512,128]{1,0:T(8,128)(2,1)}, bf16[2,64,128]{2,1,0:T(8,128)(2,1)}, f32[1,128]{1,0:T(1,128)S(1)}) custom-call(bf16[2,1,64,64]{3,2,1,0:T(8,128)(2,1)} %inverses.1, bf16[1024,128]{1,0:T(8,128)(2,1)S(1)} %copy-done, bf16[512,128]{1,0:T(8,128)(2,1)S(1)} %add.6.refs_0_, bf16[512,128]{1,0:T(8,128)(2,1)S(1)} %collective-permute-done.8.refs_1_, ...), custom_call_target="tpu_custom_call" | custom-call | tf_op jit(solution)/shard_map/pallas_call | solution.py:106
  42.4 1.1 %collective-permute-start.18 = (f32[1,128]{1,0:T(1,128)S(1)}, f32[1,128]{1,0:T(1,128)S(1)}, u32[]{:S(2)}, u32[]{:S(2)}) collective-permute-start(f32[1,128]{1,0:T(1,128)S(1)} %get-tuple-element.8), channel_id=1, source_target_pairs={{0,4},{4,0},{8,12},{12,8},{16,20},{20,16},{24,28},{28,24},{1,5},{5... | collective-permute-start | bytes 1544 | tf_op jit(solution)/shard_map/ppermute | solution.py:19
  43.5 2.4 %collective-permute-done.18 = f32[1,128]{1,0:T(1,128)S(1)} collective-permute-done((f32[1,128]{1,0:T(1,128)S(1)}, f32[1,128]{1,0:T(1,128)S(1)}, u32[]{:S(2)}, u32[]{:S(2)}) %collective-permute-start.18) | collective-permute-done | bytes 544 | tf_op jit(solution)/shard_map/ppermute | solution.py:19
  45.9 1.5 %collective-permute-start.19 = (f32[1,128]{1,0:T(1,128)S(1)}, f32[1,128]{1,0:T(1,128)S(1)}, u32[]{:S(2)}, u32[]{:S(2)}) collective-permute-start(f32[1,128]{1,0:T(1,128)S(1)} %max.6), channel_id=1, source_target_pairs={{0,8},{4,12},{8,0},{12,4},{16,24},{20,28},{24,16},{28,20},{1,9},{5... | collective-permute-start | bytes 1544 | tf_op jit(solution)/shard_map/ppermute | solution.py:19
  47.4 2.1 %collective-permute-done.19 = f32[1,128]{1,0:T(1,128)S(1)} collective-permute-done((f32[1,128]{1,0:T(1,128)S(1)}, f32[1,128]{1,0:T(1,128)S(1)}, u32[]{:S(2)}, u32[]{:S(2)}) %collective-permute-start.19) | collective-permute-done | bytes 544 | tf_op jit(solution)/shard_map/ppermute | solution.py:19
  49.5 0.5 %maximum_bitcast_fusion = f32[128]{0:T(128)} fusion(f32[1,128]{1,0:T(1,128)S(1)} %max.6, f32[1,128]{1,0:T(1,128)S(1)} %collective-permute-done.19), kind=kLoop, calls=%fused_computation | loop fusion | flops 128 | bytes 1536 | tf_op jit(solution)/shard_map/squeeze | solution.py:159
  (5 shorter events, 0.1 us)
Async XLA Ops:
  1.6 21.9 %copy-start.1 = (s32[2,1]{0,1:T(1,128)S(1)}, s32[2,1]{0,1:T(1,128)}, u32[]{:S(2)}) copy-start(s32[2,1]{0,1:T(1,128)} %param.6) | copy-start | bytes 28
  1.6 14.0 %collective-permute-start.12 = (bf16[512,128]{1,0:T(8,128)(2,1)S(1)}, bf16[512,128]{1,0:T(8,128)(2,1)S(1)}, u32[]{:S(2)}, u32[]{:S(2)}) collective-permute-start(bf16[512,128]{1,0:T(8,128)(2,1)S(1)} %get-tuple-element.9.refs_0_.refs_5_), channel_id=1, source_target_pairs={{0,16},{4,20},{8,24},{12,28},{16,0},{20,4},{24,8},{28,12},{1,17},{... | collective-permute-start | bytes 393224 | tf_op jit(solution)/shard_map/ppermute | solution.py:19
  5.7 11.8 %collective-permute-start.10 = (bf16[512,128]{1,0:T(8,128)(2,1)S(1)}, bf16[512,128]{1,0:T(8,128)(2,1)S(1)}, u32[]{:S(2)}, u32[]{:S(2)}) collective-permute-start(bf16[512,128]{1,0:T(8,128)(2,1)S(1)} %get-tuple-element.9.refs_0_.refs_5_), channel_id=1, source_target_pairs={{0,2},{1,3},{2,0},{3,1},{4,6},{5,7},{6,4},{7,5},{8,10},{9,11},{10,... | collective-permute-start | bytes 393224 | tf_op jit(solution)/shard_map/ppermute | solution.py:19
  7.2 10.3 %collective-permute-start.9 = (bf16[512,128]{1,0:T(8,128)(2,1)S(1)}, bf16[512,128]{1,0:T(8,128)(2,1)S(1)}, u32[]{:S(2)}, u32[]{:S(2)}) collective-permute-start(bf16[512,128]{1,0:T(8,128)(2,1)S(1)} %get-tuple-element.9.refs_0_.refs_5_), channel_id=1, source_target_pairs={{0,1},{1,0},{2,3},{3,2},{4,5},{5,4},{6,7},{7,6},{8,9},{9,8},{10,11... | collective-permute-start | bytes 393224 | tf_op jit(solution)/shard_map/ppermute | solution.py:19
  7.2 10.8 %collective-permute-start.3 = (bf16[512,128]{1,0:T(8,128)(2,1)S(1)}, bf16[512,128]{1,0:T(8,128)(2,1)S(1)}, u32[]{:S(2)}, u32[]{:S(2)}) collective-permute-start(bf16[512,128]{1,0:T(8,128)(2,1)S(1)} %get-tuple-element.10.refs_0_.refs_4_), channel_id=1, source_target_pairs={{0,16},{4,20},{8,24},{12,28},{16,0},{20,4},{24,8},{28,12},{1,17},{... | collective-permute-start | bytes 393224 | tf_op jit(solution)/shard_map/ppermute | solution.py:19
  7.6 11.6 %collective-permute-start.1 = (bf16[512,128]{1,0:T(8,128)(2,1)S(1)}, bf16[512,128]{1,0:T(8,128)(2,1)S(1)}, u32[]{:S(2)}, u32[]{:S(2)}) collective-permute-start(bf16[512,128]{1,0:T(8,128)(2,1)S(1)} %get-tuple-element.10.refs_0_.refs_4_), channel_id=1, source_target_pairs={{0,2},{1,3},{2,0},{3,1},{4,6},{5,7},{6,4},{7,5},{8,10},{9,11},{10,... | collective-permute-start | bytes 393224 | tf_op jit(solution)/shard_map/ppermute | solution.py:19
  15.6 5.7 %collective-permute-start.14 = (bf16[512,128]{1,0:T(8,128)(2,1)S(1)}, bf16[512,128]{1,0:T(8,128)(2,1)S(1)}, u32[]{:S(2)}, u32[]{:S(2)}) collective-permute-start(bf16[512,128]{1,0:T(8,128)(2,1)S(1)} %collective-permute-done.12.refs_4_.refs_13_), channel_id=1, source_target_pairs={{0,2},{1,3},{2,0},{3,1},{4,6},{5,7},{6,4},{7,5},{8,10},{9,11},{10,... | collective-permute-start | bytes 393224 | tf_op jit(solution)/shard_map/ppermute | solution.py:19
  17.5 3.8 %collective-permute-start.13 = (bf16[512,128]{1,0:T(8,128)(2,1)S(1)}, bf16[512,128]{1,0:T(8,128)(2,1)S(1)}, u32[]{:S(2)}, u32[]{:S(2)}) collective-permute-start(bf16[512,128]{1,0:T(8,128)(2,1)S(1)} %collective-permute-done.12.refs_4_.refs_13_), channel_id=1, source_target_pairs={{0,1},{1,0},{2,3},{3,2},{4,5},{5,4},{6,7},{7,6},{8,9},{9,8},{10,11... | collective-permute-start | bytes 393224 | tf_op jit(solution)/shard_map/ppermute | solution.py:19
  17.5 4.3 %collective-permute-start.11 = (bf16[512,128]{1,0:T(8,128)(2,1)S(1)}, bf16[512,128]{1,0:T(8,128)(2,1)S(1)}, u32[]{:S(2)}, u32[]{:S(2)}) collective-permute-start(bf16[512,128]{1,0:T(8,128)(2,1)S(1)} %collective-permute-done.10.refs_2_.refs_9_), channel_id=1, source_target_pairs={{0,1},{1,0},{2,3},{3,2},{4,5},{5,4},{6,7},{7,6},{8,9},{9,8},{10,11... | collective-permute-start | bytes 393224 | tf_op jit(solution)/shard_map/ppermute | solution.py:19
  18.0 5.5 %collective-permute-start.5 = (bf16[512,128]{1,0:T(8,128)(2,1)S(1)}, bf16[512,128]{1,0:T(8,128)(2,1)S(1)}, u32[]{:S(2)}, u32[]{:S(2)}) collective-permute-start(bf16[512,128]{1,0:T(8,128)(2,1)S(1)} %collective-permute-done.3.refs_4_.refs_12_), channel_id=1, source_target_pairs={{0,2},{1,3},{2,0},{3,1},{4,6},{5,7},{6,4},{7,5},{8,10},{9,11},{10,... | collective-permute-start | bytes 393224 | tf_op jit(solution)/shard_map/ppermute | solution.py:19
  19.2 6.4 %collective-permute-start = (bf16[512,128]{1,0:T(8,128)(2,1)S(1)}, bf16[512,128]{1,0:T(8,128)(2,1)S(1)}, u32[]{:S(2)}, u32[]{:S(2)}) collective-permute-start(bf16[512,128]{1,0:T(8,128)(2,1)S(1)} %get-tuple-element.10.refs_0_.refs_4_), channel_id=1, source_target_pairs={{0,1},{1,0},{2,3},{3,2},{4,5},{5,4},{6,7},{7,6},{8,9},{9,8},{10,11... | collective-permute-start | bytes 393224 | tf_op jit(solution)/shard_map/ppermute | solution.py:19
  21.3 2.9 %collective-permute-start.15 = (bf16[512,128]{1,0:T(8,128)(2,1)S(1)}, bf16[512,128]{1,0:T(8,128)(2,1)S(1)}, u32[]{:S(2)}, u32[]{:S(2)}) collective-permute-start(bf16[512,128]{1,0:T(8,128)(2,1)S(1)} %collective-permute-done.14.refs_6_.refs_17_), channel_id=1, source_target_pairs={{0,1},{1,0},{2,3},{3,2},{4,5},{5,4},{6,7},{7,6},{8,9},{9,8},{10,11... | collective-permute-start | bytes 393224 | tf_op jit(solution)/shard_map/ppermute | solution.py:19
  21.3 4.3 %collective-permute-start.4 = (bf16[512,128]{1,0:T(8,128)(2,1)S(1)}, bf16[512,128]{1,0:T(8,128)(2,1)S(1)}, u32[]{:S(2)}, u32[]{:S(2)}) collective-permute-start(bf16[512,128]{1,0:T(8,128)(2,1)S(1)} %collective-permute-done.3.refs_4_.refs_12_), channel_id=1, source_target_pairs={{0,1},{1,0},{2,3},{3,2},{4,5},{5,4},{6,7},{7,6},{8,9},{9,8},{10,11... | collective-permute-start | bytes 393224 | tf_op jit(solution)/shard_map/ppermute | solution.py:19
  21.8 3.8 %collective-permute-start.2 = (bf16[512,128]{1,0:T(8,128)(2,1)S(1)}, bf16[512,128]{1,0:T(8,128)(2,1)S(1)}, u32[]{:S(2)}, u32[]{:S(2)}) collective-permute-start(bf16[512,128]{1,0:T(8,128)(2,1)S(1)} %collective-permute-done.1.refs_2_.refs_8_), channel_id=1, source_target_pairs={{0,1},{1,0},{2,3},{3,2},{4,5},{5,4},{6,7},{7,6},{8,9},{9,8},{10,11... | collective-permute-start | bytes 393224 | tf_op jit(solution)/shard_map/ppermute | solution.py:19
  23.5 2.2 %collective-permute-start.6 = (bf16[512,128]{1,0:T(8,128)(2,1)S(1)}, bf16[512,128]{1,0:T(8,128)(2,1)S(1)}, u32[]{:S(2)}, u32[]{:S(2)}) collective-permute-start(bf16[512,128]{1,0:T(8,128)(2,1)S(1)} %collective-permute-done.5.refs_6_.refs_16_), channel_id=1, source_target_pairs={{0,1},{1,0},{2,3},{3,2},{4,5},{5,4},{6,7},{7,6},{8,9},{9,8},{10,11... | collective-permute-start | bytes 393224 | tf_op jit(solution)/shard_map/ppermute | solution.py:19
  25.3 6.0 %collective-permute-start.16 = (bf16[512,128]{1,0:T(8,128)(2,1)S(1)}, bf16[512,128]{1,0:T(8,128)(2,1)S(1)}, u32[]{:S(2)}, u32[]{:S(2)}) collective-permute-start(bf16[512,128]{1,0:T(8,128)(2,1)S(1)} %shard_map.68), channel_id=1, source_target_pairs={{0,8},{4,12},{8,0},{12,4},{16,24},{20,28},{24,16},{28,20},{1,9},{5... | collective-permute-start | bytes 393224 | tf_op jit(solution)/shard_map/ppermute | solution.py:19
  26.8 6.1 %collective-permute-start.7 = (bf16[512,128]{1,0:T(8,128)(2,1)S(1)}, bf16[512,128]{1,0:T(8,128)(2,1)S(1)}, u32[]{:S(2)}, u32[]{:S(2)}) collective-permute-start(bf16[512,128]{1,0:T(8,128)(2,1)S(1)} %shard_map.67), channel_id=1, source_target_pairs={{0,4},{4,0},{8,12},{12,8},{16,20},{20,16},{24,28},{28,24},{1,5},{5... | collective-permute-start | bytes 393224 | tf_op jit(solution)/shard_map/ppermute | solution.py:19
  31.3 6.7 %copy-start = (bf16[1024,128]{1,0:T(8,128)(2,1)S(1)}, bf16[1024,128]{1,0:T(8,128)(2,1)}, u32[]{:S(2)}) copy-start(bf16[1024,128]{1,0:T(8,128)(2,1)} %signals.1) | copy-start | bytes 786436
  31.3 5.2 %collective-permute-start.17 = (bf16[512,128]{1,0:T(8,128)(2,1)S(1)}, bf16[512,128]{1,0:T(8,128)(2,1)S(1)}, u32[]{:S(2)}, u32[]{:S(2)}) collective-permute-start(bf16[512,128]{1,0:T(8,128)(2,1)S(1)} %add.7.refs_2_), channel_id=1, source_target_pairs={{0,4},{4,0},{8,12},{12,8},{16,20},{20,16},{24,28},{28,24},{1,5},{5... | collective-permute-start | bytes 393224 | tf_op jit(solution)/shard_map/ppermute | solution.py:19
  33.0 5.0 %collective-permute-start.8 = (bf16[512,128]{1,0:T(8,128)(2,1)S(1)}, bf16[512,128]{1,0:T(8,128)(2,1)S(1)}, u32[]{:S(2)}, u32[]{:S(2)}) collective-permute-start(bf16[512,128]{1,0:T(8,128)(2,1)S(1)} %add.6.refs_0_), channel_id=1, source_target_pairs={{0,8},{4,12},{8,0},{12,4},{16,24},{20,28},{24,16},{28,20},{1,9},{5... | collective-permute-start | bytes 393224 | tf_op jit(solution)/shard_map/ppermute | solution.py:19
  42.4 3.5 %collective-permute-start.18 = (f32[1,128]{1,0:T(1,128)S(1)}, f32[1,128]{1,0:T(1,128)S(1)}, u32[]{:S(2)}, u32[]{:S(2)}) collective-permute-start(f32[1,128]{1,0:T(1,128)S(1)} %get-tuple-element.8), channel_id=1, source_target_pairs={{0,4},{4,0},{8,12},{12,8},{16,20},{20,16},{24,28},{28,24},{1,5},{5... | collective-permute-start | bytes 1544 | tf_op jit(solution)/shard_map/ppermute | solution.py:19
  45.9 3.5 %collective-permute-start.19 = (f32[1,128]{1,0:T(1,128)S(1)}, f32[1,128]{1,0:T(1,128)S(1)}, u32[]{:S(2)}, u32[]{:S(2)}) collective-permute-start(f32[1,128]{1,0:T(1,128)S(1)} %max.6), channel_id=1, source_target_pairs={{0,8},{4,12},{8,0},{12,4},{16,24},{20,28},{24,16},{28,20},{1,9},{5... | collective-permute-start | bytes 1544 | tf_op jit(solution)/shard_map/ppermute | solution.py:19

commit v3 on v1

v3 whole, which is shorter than its diff:
```python
import functools

import jax
import jax.numpy as jnp
from jax import lax
from jax.experimental import pallas as pl
from jax.experimental.pallas import tpu as pltpu
from jax.sharding import PartitionSpec as P

BLK = 64
SB = 128
STEPS = 2

VMEM = pl.BlockSpec(memory_space=pltpu.VMEM)
SMEM = pl.BlockSpec(memory_space=pltpu.SMEM)
HBM = pl.BlockSpec(memory_space=pltpu.HBM)
PARAMS = pltpu.CompilerParams(vmem_limit_bytes=8 << 20)


def swap(block, axis, size, mask):
    return lax.ppermute(block, axis, [(i, i ^ mask) for i in range(size)])


def matmul(a, b):
    return jnp.dot(a, b, preferred_element_type=jnp.float32)


def near(array):
    return pltpu.with_memory_space_constraint(array, pltpu.VMEM)


def after(array, *others):
    return lax.optimization_barrier((array, *others))[0]


def hot_rows(n_sig, tags, selected):
    me, group = lax.axis_index("sig"), lax.axis_index("atoms")
    place = lax.broadcasted_iota(jnp.int32, (SB, STEPS * BLK), 0)
    column = lax.broadcasted_iota(jnp.int32, (SB, STEPS * BLK), 1)
    wanted = jnp.where(column < BLK, selected[0] * BLK, selected[1] * BLK - BLK) + column - place
    hot = []
    for side, mask in tags:
        home = ((group ^ side) * n_sig + (me ^ mask)) * SB
        hot.append((wanted == home).astype(jnp.float32).astype(jnp.bfloat16))
    return jnp.concatenate(hot, 0)


def fetch_kernel(n_sig, selected, own, mine, out):
    mine[...] = own[...]
    out[...] = matmul(own[...], hot_rows(n_sig, [(0, 0)], selected)).astype(jnp.bfloat16)


def fetch(n_sig, selected, own):
    return pl.pallas_call(
        functools.partial(fetch_kernel, n_sig),
        out_shape=(pltpu.VMEM(own.shape, jnp.bfloat16), pltpu.VMEM((own.shape[0], STEPS * BLK), jnp.bfloat16)),
        in_specs=[SMEM, VMEM],
        out_specs=(VMEM, VMEM),
        name="fetch",
        compiler_params=PARAMS,
    )(selected, own)


def pick_kernel(n_sig, selected, base, *refs):
    pieces, outs = refs[: n_sig - 1], refs[n_sig - 1 :]
    rows = jnp.concatenate([piece[...] for piece in pieces], 1)
    total = matmul(rows, hot_rows(n_sig, [(0, mask) for mask in range(1, n_sig)], selected))
    total = total.astype(jnp.bfloat16) + base[...]
    at = 0
    for out in outs:
        out[...] = total[at : at + out.shape[0]]
        at += out.shape[0]


def pick(n_sig, selected, base, pieces, depths):
    return pl.pallas_call(
        functools.partial(pick_kernel, n_sig),
        out_shape=tuple(pltpu.VMEM((depth, STEPS * BLK), jnp.bfloat16) for depth in depths),
        in_specs=[SMEM] + [VMEM] * n_sig,
        out_specs=(VMEM,) * len(depths),
        name="pick",
        compiler_params=PARAMS,
    )(selected, near(base), *[near(piece) for piece in pieces])


def ready_kernel(counts, signals, *refs):
    parts, turned, first = refs[:-2], refs[-2], refs[-1]
    at = 0
    for i, count in enumerate(counts):
        piece = jnp.concatenate([part[...] for part in parts[at : at + count]], 0).T
        at += count
        turned[i * SB : (i + 1) * SB] = piece
        first[i * SB : (i + 1) * SB] = matmul(piece, signals[...])


def ready(signals, pieces):
    parts = [near(part) for piece in pieces for part in piece]
    width = len(pieces) * SB
    return pl.pallas_call(
        functools.partial(ready_kernel, [len(piece) for piece in pieces]),
        out_shape=(
            pltpu.VMEM((width, signals.shape[0]), jnp.bfloat16),
            pltpu.VMEM((width, SB), jnp.float32),
        ),
        in_specs=[VMEM] * (1 + len(parts)),
        out_specs=(VMEM, VMEM),
        name="ready",
        compiler_params=PARAMS,
    )(near(signals), *parts)


def exact(matrix, rows):
    high = rows.astype(jnp.bfloat16)
    rest = rows - high.astype(jnp.float32)
    middle = rest.astype(jnp.bfloat16)
    low = (rest - middle.astype(jnp.float32)).astype(jnp.bfloat16)
    terms = matmul(matrix, jnp.concatenate([low, middle, high], 1))
    return terms[:, :SB] + terms[:, SB : 2 * SB] + terms[:, 2 * SB :]


def finish_kernel(n_sig, n_halves, n_sides, inverses, signals, *refs):
    corr_out, coef_out, peak_out = refs[-3:]
    halves, at = [], 0
    for count in n_halves:
        half = refs[at][...]
        for more in refs[at + 1 : at + count]:
            half = half + more[...]
        halves.append(half)
        at += count
    sides = refs[at:-3]
    chosen = jnp.concatenate(halves, 0)
    right = matmul(chosen.T, jnp.concatenate([signals[...], chosen], 1))
    rows, gram = right[:, :SB], right[:, SB:].astype(jnp.bfloat16)
    one = exact(inverses[0, 0], rows[:BLK]).astype(jnp.bfloat16)
    two = exact(inverses[1, 0], rows[BLK:] - matmul(gram[BLK:, :BLK], one)).astype(jnp.bfloat16)
    coef_out[0] = one
    coef_out[1] = two
    weights = jnp.concatenate([one, two], 0)
    me = lax.axis_index("sig")
    best = None
    for side in range(n_sides):
        turned, first = sides[2 * side], sides[2 * side + 1]
        panel = matmul(turned[...], chosen).astype(jnp.bfloat16)
        corr = first[...] - matmul(panel, weights)
        if side == 0:
            for i in range(n_sig):
                at = pl.multiple_of((me ^ i) * SB, SB)
                corr_out[pl.ds(at, SB), :] = corr[i * SB : (i + 1) * SB].astype(jnp.bfloat16)
        most = jnp.max(jnp.abs(corr), axis=0, keepdims=True)
        best = most if best is None else jnp.maximum(best, most)
    peak_out[...] = best


def finish(n_sig, inverses, signals, terms, sides):
    flat = [near(array) for group in [*terms, *sides] for array in group]
    return pl.pallas_call(
        functools.partial(finish_kernel, n_sig, [len(term) for term in terms], len(sides)),
        out_shape=(
            pltpu.VMEM((n_sig * SB, SB), jnp.bfloat16),
            pltpu.VMEM((STEPS, BLK, SB), jnp.bfloat16),
            pltpu.VMEM((1, SB), jnp.float32),
        ),
        in_specs=[VMEM] * (2 + len(flat)),
        out_specs=(VMEM, VMEM, VMEM),
        name="finish",
        compiler_params=PARAMS,
    )(near(inverses), near(signals), *flat)


def shards(n_atoms, n_sig, signals, dictionary, selected, inverses):
    selected = selected[:, 0]
    depth = dictionary.shape[0] // 2
    bits = []
    bit = 1
    while bit < n_atoms:
        bits.append(bit)
        bit *= 2
    top, twin = bits[-1], bits[0]

    def gather(piece, local):
        pieces = {0: piece}
        bit = n_sig // 2
        while bit:
            for mask in list(pieces):
                pieces[mask | bit] = swap(pieces[mask], "sig", n_sig, bit)
            pieces[0] = local
            bit //= 2
        return [pieces[mask] for mask in range(n_sig)]

    mine, base = fetch(n_sig, selected, dictionary)
    here = gather(dictionary, mine)
    beside = swap(dictionary, "atoms", n_atoms, twin)
    first, second = pick(n_sig, selected, base, here[1:], [depth, depth])
    there = gather(beside, beside)
    blocks = [first, second]
    orders = [[top] + bits[:-1], list(bits)]
    arrived = [swap(blocks[h], "atoms", n_atoms, orders[h][0]) for h in range(2)]
    for i in range(1, len(bits)):
        for h in (1, 0):
            come = after(arrived[h], blocks[1 - h]) if i > 1 or h == 0 else arrived[h]
            blocks[h] = blocks[h] + come
            arrived[h] = swap(blocks[h], "atoms", n_atoms, orders[h][i])
    sides = [ready(signals, [[piece] for piece in pieces]) for pieces in (here, there)]
    correlations, coefficients, peak = finish(n_sig, inverses, signals, [(blocks[0], arrived[0]), (blocks[1] + arrived[1],)], sides)
    for bit in bits:
        if bit != twin:
            peak = jnp.maximum(peak, swap(peak, "atoms", n_atoms, bit))
    return correlations, coefficients, peak[0]


def solution(mesh):
    placed = (P(None, "sig"), P(None, ("atoms", "sig")), P(None, "sig"), P(None, "sig", None, None))
    return jax.shard_map(
        functools.partial(shards, mesh.shape["atoms"], mesh.shape["sig"]),
        mesh=mesh,
        in_specs=placed,
        out_specs=(P("atoms", "sig"), P(None, None, "sig"), P("sig")),
        check_vma=False,
    )
```

time: 64.7 us -> 46.2 us (0.71)
  waiting for transfers between devices: 38 us -> 17.4 us
  starting transfers between devices: 13.8 us -> 20.2 us
  Pallas kernels: 6.32 us -> 4.71 us
  other arithmetic: 2.27 us -> 0.71 us
  local copies, waits for them, and re-layouts: 3.45 us -> 2.27 us
    ppermute x9 -> x15, waiting for transfers between devices: 38 us -> 17.4 us  [swap(): return lax.ppermute(block, axis, [(i, i ^ mask) for i in range(size)])]
    ppermute x9 -> x15, starting transfers between devices: 13.8 us -> 20.2 us  [swap(): return lax.ppermute(block, axis, [(i, i ^ mask) for i in range(size)])]
    pallas_call x2 -> x5, Pallas kernels: 6.32 us -> 4.71 us  [the longest x1 2.03 us: finish(): pl.pallas_call(functools.partial(finish_kernel, n_sig, [len(term) for ter...]
    add x3 -> x5, other arithmetic: 1.75 us -> 0.19 us  [the longest x4 0.15 us: shards(): blocks[h] = blocks[h] + come]
    unnamed x15 -> x10, local copies, waits for them, and re-layouts: 3.45 us -> 2.27 us
  transfers between devices with their start and end apart: 9 -> 15, of which waited for: 7 -> 10; matrix products, arithmetic and copies ran while one was open for 2% -> 3% of each run, Pallas kernels for 0% -> 6%
where the time goes in v3:
time: 46.2 us; the launch traced here: 46 us
  starting transfers between devices  20.2 us (44%)
  waiting for transfers between devices  17.4 us (38%)
  Pallas kernels  4.71 us (10%)
  local copies, waits for them, and re-layouts  2.27 us (5%)
  between operations  0.74 us (2%)
  other arithmetic  0.71 us (2%)
    ppermute x15, starting transfers between devices, swap(): return lax.ppermute(block, axis, [(i, i ^ mask) for i in range(size)])  20.2 us
    ppermute x15, waiting for transfers between devices, swap(): return lax.ppermute(block, axis, [(i, i ^ mask) for i in range(size)])  17.4 us
    unnamed x10, local copies, waits for them, and re-layouts  2.27 us
    pallas_call x1, Pallas kernels, finish(): pl.pallas_call(functools.partial(finish_kernel, n_sig, [len(term) for ter...  2.03 us
    pallas_call x2, Pallas kernels, ready(): pl.pallas_call(functools.partial(ready_kernel, [len(piece) for piece in p...  0.95 us
    pallas_call x1, Pallas kernels, pick(): pl.pallas_call(functools.partial(pick_kernel, n_sig), out_shape=tuple((pl...  0.92 us
  transfers between devices with their start and end apart: 15, of which 10 were waited for; matrix products, arithmetic and copies ran while one was open for 3% of the time, Pallas kernels for 6%

profile of v3, /device:TPU:0, one launch (start us, length us, event | category | flops | bytes accessed | tf_op | source)
XLA Modules:
  0.0 46.0 jit_solution(1284176493036844625)
XLA Ops:
  0.6 0.0 copy-start.3
  0.6 3.0 %collective-permute-start.1 = (bf16[1024,128]{1,0:T(8,128)(2,1)}, bf16[1024,128]{1,0:T(8,128)(2,1)S(1)}, u32[]{:S(2)}, u32[]{:S(2)}) collective-permute-start(bf16[1024,128]{1,0:T(8,128)(2,1)} %own.1), channel_id=1, source_target_pairs={{0,2},{1,3},{2,0},{3,1},{4,6},{5,7},{6,4},{7,5},{8,10},{9,11},{10,... | collective-permute-start | bytes 786440 | tf_op jit(solution)/shard_map/ppermute | solution.py:21
  3.6 1.5 %collective-permute-start.9 = (bf16[1024,128]{1,0:T(8,128)(2,1)}, bf16[1024,128]{1,0:T(8,128)(2,1)S(1)}, u32[]{:S(2)}, u32[]{:S(2)}) collective-permute-start(bf16[1024,128]{1,0:T(8,128)(2,1)} %own.1), channel_id=1, source_target_pairs={{0,4},{4,0},{8,12},{12,8},{16,20},{20,16},{24,28},{28,24},{1,5},{5... | collective-permute-start | bytes 786440 | tf_op jit(solution)/shard_map/ppermute | solution.py:21
  5.2 0.0 copy-done.3
  5.2 0.0 copy-start.1
  5.2 1.0 %copy-done.1 = bf16[1024,128]{1,0:T(8,128)(2,1)S(1)} copy-done((bf16[1024,128]{1,0:T(8,128)(2,1)S(1)}, bf16[1024,128]{1,0:T(8,128)(2,1)}, u32[]{:S(2)}) %copy-start.1) | copy-done | bytes 262168
  6.1 0.8 %fetch.1 = (bf16[1024,128]{1,0:T(8,128)(2,1)S(1)}, bf16[1024,128]{1,0:T(8,128)(2,1)S(1)}) custom-call(s32[2]{0:T(128)S(1)} %bitcast.3, bf16[1024,128]{1,0:T(8,128)(2,1)S(1)} %copy-done.1), custom_call_target="tpu_custom_call" | custom-call | tf_op jit(solution)/shard_map/fetch/pallas_call | solution.py:54
  7.0 0.1 collective-permute-start
  7.0 3.1 %collective-permute-done.1.refs_1_.refs_2_ = bf16[1024,128]{1,0:T(8,128)(2,1)S(1)} collective-permute-done((bf16[1024,128]{1,0:T(8,128)(2,1)}, bf16[1024,128]{1,0:T(8,128)(2,1)S(1)}, u32[]{:S(2)}, u32[]{:S(2)}) %collective-permute-start.1) | collective-permute-done | bytes 262176 | tf_op jit(solution)/shard_map/ppermute | solution.py:21
  10.2 0.0 collective-permute-start.2
  10.2 1.5 %collective-permute-done.9.refs_0_ = bf16[1024,128]{1,0:T(8,128)(2,1)S(1)} collective-permute-done((bf16[1024,128]{1,0:T(8,128)(2,1)}, bf16[1024,128]{1,0:T(8,128)(2,1)S(1)}, u32[]{:S(2)}, u32[]{:S(2)}) %collective-permute-start.9) | collective-permute-done | bytes 262176 | tf_op jit(solution)/shard_map/ppermute | solution.py:21
  11.6 0.4 collective-permute-start.11
  12.0 0.0 collective-permute-done.refs_0_.refs_1_
  12.0 0.0 collective-permute-done.2.refs_2_.refs_3_
  12.0 0.9 %pick.1 = (bf16[512,128]{1,0:T(8,128)(2,1)S(1)}, bf16[512,128]{1,0:T(8,128)(2,1)S(1)}) custom-call(s32[2]{0:T(128)S(1)} %bitcast.4, bf16[1024,128]{1,0:T(8,128)(2,1)S(1)} %get-tuple-element.17.base, bf16[1024,128]{1,0:T(8,128)(2,1)S(1)} %collective-permute-done.refs_0_.refs_1_, bf16[1024,128]{1,0:T(8,128)(2,1)S(1)} %collective-permute-done.1.refs_1_.refs_2_, ...), custom_call_target="tpu_custom_call" | custom-call | tf_op jit(solution)/shard_map/pick/pallas_call | solution.py:76
  12.9 1.7 %collective-permute-start.4 = (bf16[512,128]{1,0:T(8,128)(2,1)S(1)}, bf16[512,128]{1,0:T(8,128)(2,1)S(1)}, u32[]{:S(2)}, u32[]{:S(2)}) collective-permute-start(bf16[512,128]{1,0:T(8,128)(2,1)S(1)} %get-tuple-element.20), channel_id=1, source_target_pairs={{0,4},{4,0},{8,12},{12,8},{16,20},{20,16},{24,28},{28,24},{1,5},{5... | collective-permute-start | bytes 393224 | tf_op jit(solution)/shard_map/ppermute | solution.py:21
  14.7 2.6 %collective-permute-start.3 = (bf16[512,128]{1,0:T(8,128)(2,1)S(1)}, bf16[512,128]{1,0:T(8,128)(2,1)S(1)}, u32[]{:S(2)}, u32[]{:S(2)}) collective-permute-start(bf16[512,128]{1,0:T(8,128)(2,1)S(1)} %get-tuple-element.19), channel_id=1, source_target_pairs={{0,16},{4,20},{8,24},{12,28},{16,0},{20,4},{24,8},{28,12},{1,17},{... | collective-permute-start | bytes 393224 | tf_op jit(solution)/shard_map/ppermute | solution.py:21
  17.3 0.0 collective-permute-start.10
  17.3 1.3 %collective-permute-done.4 = bf16[512,128]{1,0:T(8,128)(2,1)S(1)} collective-permute-done((bf16[512,128]{1,0:T(8,128)(2,1)S(1)}, bf16[512,128]{1,0:T(8,128)(2,1)S(1)}, u32[]{:S(2)}, u32[]{:S(2)}) %collective-permute-start.4) | collective-permute-done | bytes 131104 | tf_op jit(solution)/shard_map/ppermute | solution.py:21
  18.6 1.6 %collective-permute-start.6 = (bf16[512,128]{1,0:T(8,128)(2,1)S(1)}, bf16[512,128]{1,0:T(8,128)(2,1)S(1)}, u32[]{:S(2)}, u32[]{:S(2)}) collective-permute-start(bf16[512,128]{1,0:T(8,128)(2,1)S(1)} %add.15), channel_id=1, source_target_pairs={{0,8},{4,12},{8,0},{12,4},{16,24},{20,28},{24,16},{28,20},{1,9},{5... | collective-permute-start | bytes 393224 | tf_op jit(solution)/shard_map/ppermute | solution.py:21
  20.2 3.4 %collective-permute-done.3 = bf16[512,128]{1,0:T(8,128)(2,1)S(1)} collective-permute-done((bf16[512,128]{1,0:T(8,128)(2,1)S(1)}, bf16[512,128]{1,0:T(8,128)(2,1)S(1)}, u32[]{:S(2)}, u32[]{:S(2)}) %collective-permute-start.3) | collective-permute-done | bytes 131104 | tf_op jit(solution)/shard_map/ppermute | solution.py:21
  23.6 0.6 %collective-permute-start.5 = (bf16[512,128]{1,0:T(8,128)(2,1)S(1)}, bf16[512,128]{1,0:T(8,128)(2,1)S(1)}, u32[]{:S(2)}, u32[]{:S(2)}) collective-permute-start(bf16[512,128]{1,0:T(8,128)(2,1)S(1)} %add.16), channel_id=1, source_target_pairs={{0,4},{4,0},{8,12},{12,8},{16,20},{20,16},{24,28},{28,24},{1,5},{5... | collective-permute-start | bytes 393224 | tf_op jit(solution)/shard_map/ppermute | solution.py:21
  24.2 0.0 collective-permute-done.11.refs_2_
  24.2 0.0 collective-permute-start.12
  24.2 0.8 %collective-permute-done.6 = bf16[512,128]{1,0:T(8,128)(2,1)S(1)} collective-permute-done((bf16[512,128]{1,0:T(8,128)(2,1)S(1)}, bf16[512,128]{1,0:T(8,128)(2,1)S(1)}, u32[]{:S(2)}, u32[]{:S(2)}) %collective-permute-start.6) | collective-permute-done | bytes 131104 | tf_op jit(solution)/shard_map/ppermute | solution.py:21
  25.1 0.0 copy-start
  25.1 2.6 %collective-permute-start.8 = (bf16[512,128]{1,0:T(8,128)(2,1)S(1)}, bf16[512,128]{1,0:T(8,128)(2,1)S(1)}, u32[]{:S(2)}, u32[]{:S(2)}) collective-permute-start(bf16[512,128]{1,0:T(8,128)(2,1)S(1)} %add.17), channel_id=1, source_target_pairs={{0,16},{4,20},{8,24},{12,28},{16,0},{20,4},{24,8},{28,12},{1,17},{... | collective-permute-start | bytes 393224 | tf_op jit(solution)/shard_map/ppermute | solution.py:21
  27.7 1.0 %collective-permute-done.5 = bf16[512,128]{1,0:T(8,128)(2,1)S(1)} collective-permute-done((bf16[512,128]{1,0:T(8,128)(2,1)S(1)}, bf16[512,128]{1,0:T(8,128)(2,1)S(1)}, u32[]{:S(2)}, u32[]{:S(2)}) %collective-permute-start.5) | collective-permute-done | bytes 131104 | tf_op jit(solution)/shard_map/ppermute | solution.py:21
  28.7 1.6 %collective-permute-start.7 = (bf16[512,128]{1,0:T(8,128)(2,1)S(1)}, bf16[512,128]{1,0:T(8,128)(2,1)S(1)}, u32[]{:S(2)}, u32[]{:S(2)}) collective-permute-start(bf16[512,128]{1,0:T(8,128)(2,1)S(1)} %add.18.refs_0_), channel_id=1, source_target_pairs={{0,8},{4,12},{8,0},{12,4},{16,24},{20,28},{24,16},{28,20},{1,9},{5... | collective-permute-start | bytes 393224 | tf_op jit(solution)/shard_map/ppermute | solution.py:21
  30.3 0.0 copy-done
  30.3 0.5 %ready.2 = (bf16[512,1024]{1,0:T(8,128)(2,1)S(1)}, f32[512,128]{1,0:T(8,128)S(1)}) custom-call(bf16[1024,128]{1,0:T(8,128)(2,1)S(1)} %copy-done, bf16[1024,128]{1,0:T(8,128)(2,1)S(1)} %get-tuple-element.18.refs_0_, bf16[1024,128]{1,0:T(8,128)(2,1)S(1)} %collective-permute-done.refs_0_.refs_1_, bf16[1024,128]{1,0:T(8,128)(2,1)S(1)} %collective-permute-done.1.refs_1_.refs_2_, ...), custom_call_target="tpu_custom_call" | custom-call | tf_op jit(solution)/shard_map/ready/pallas_call | solution.py:99
  30.8 0.0 collective-permute-done.10.refs_1_
  30.8 0.0 collective-permute-done.12.refs_3_
  30.8 0.5 %ready.3 = (bf16[512,1024]{1,0:T(8,128)(2,1)S(1)}, f32[512,128]{1,0:T(8,128)S(1)}) custom-call(bf16[1024,128]{1,0:T(8,128)(2,1)S(1)} %copy-done, bf16[1024,128]{1,0:T(8,128)(2,1)S(1)} %collective-permute-done.9.refs_0_, bf16[1024,128]{1,0:T(8,128)(2,1)S(1)} %collective-permute-done.10.refs_1_, bf16[1024,128]{1,0:T(8,128)(2,1)S(1)} %collective-permute-done.11.refs_2_, ...), custom_call_target="tpu_custom_call" | custom-call | tf_op jit(solution)/shard_map/ready/pallas_call | solution.py:99
  31.3 0.0 copy-start.2
  31.3 2.8 %collective-permute-done.8 = bf16[512,128]{1,0:T(8,128)(2,1)S(1)} collective-permute-done((bf16[512,128]{1,0:T(8,128)(2,1)S(1)}, bf16[512,128]{1,0:T(8,128)(2,1)S(1)}, u32[]{:S(2)}, u32[]{:S(2)}) %collective-permute-start.8) | collective-permute-done | bytes 131104 | tf_op jit(solution)/shard_map/ppermute | solution.py:21
  34.1 0.6 %collective-permute-done.7.refs_1_ = bf16[512,128]{1,0:T(8,128)(2,1)S(1)} collective-permute-done((bf16[512,128]{1,0:T(8,128)(2,1)S(1)}, bf16[512,128]{1,0:T(8,128)(2,1)S(1)}, u32[]{:S(2)}, u32[]{:S(2)}) %collective-permute-start.7) | collective-permute-done | bytes 131104 | tf_op jit(solution)/shard_map/ppermute | solution.py:21
  34.7 0.0 copy-done.2
  34.7 2.0 %finish.1 = (bf16[512,128]{1,0:T(8,128)(2,1)S(1)}, bf16[2,64,128]{2,1,0:T(8,128)(2,1)S(1)}, f32[1,128]{1,0:T(1,128)S(1)}) custom-call(bf16[2,1,64,64]{3,2,1,0:T(8,128)(2,1)S(1)} %copy-done.2, bf16[1024,128]{1,0:T(8,128)(2,1)S(1)} %copy-done, bf16[512,128]{1,0:T(8,128)(2,1)S(1)} %add.18.refs_0_, bf16[512,128]{1,0:T(8,128)(2,1)S(1)} %collective-permute-done.7.refs_1_, ...), custom_call_target="tpu_custom_call" | custom-call | tf_op jit(solution)/shard_map/finish/pallas_call | solution.py:156
  36.7 0.9 %collective-permute-start.13 = (f32[1,128]{1,0:T(1,128)S(1)}, f32[1,128]{1,0:T(1,128)S(1)}, u32[]{:S(2)}, u32[]{:S(2)}) collective-permute-start(f32[1,128]{1,0:T(1,128)S(1)} %get-tuple-element.30), channel_id=1, source_target_pairs={{0,8},{4,12},{8,0},{12,4},{16,24},{20,28},{24,16},{28,20},{1,9},{5... | collective-permute-start | bytes 1544 | tf_op jit(solution)/shard_map/ppermute | solution.py:21
  37.6 2.7 %collective-permute-done.13 = f32[1,128]{1,0:T(1,128)S(1)} collective-permute-done((f32[1,128]{1,0:T(1,128)S(1)}, f32[1,128]{1,0:T(1,128)S(1)}, u32[]{:S(2)}, u32[]{:S(2)}) %collective-permute-start.13) | collective-permute-done | bytes 544 | tf_op jit(solution)/shard_map/ppermute | solution.py:21
  40.3 3.6 %collective-permute-start.14 = (f32[1,128]{1,0:T(1,128)S(1)}, f32[1,128]{1,0:T(1,128)S(1)}, u32[]{:S(2)}, u32[]{:S(2)}) collective-permute-start(f32[1,128]{1,0:T(1,128)S(1)} %max.6), channel_id=1, source_target_pairs={{0,16},{4,20},{8,24},{12,28},{16,0},{20,4},{24,8},{28,12},{1,17},{... | collective-permute-start | bytes 1544 | tf_op jit(solution)/shard_map/ppermute | solution.py:21
  44.0 0.7 %copy.7 = bf16[512,128]{1,0:T(8,128)(2,1)} copy(bf16[512,128]{1,0:T(8,128)(2,1)S(1)} %get-tuple-element.31) | data formatting | bytes 262144
  44.6 0.6 %copy.8 = bf16[2,64,128]{2,1,0:T(8,128)(2,1)} copy(bf16[2,64,128]{2,1,0:T(8,128)(2,1)S(1)} %get-tuple-element.32) | data formatting | bytes 65536
  45.3 0.2 collective-permute-done.14
  45.5 0.5 %maximum_bitcast_fusion = f32[128]{0:T(128)} fusion(f32[1,128]{1,0:T(1,128)S(1)} %max.6, f32[1,128]{1,0:T(1,128)S(1)} %collective-permute-done.14), kind=kLoop, calls=%fused_computation | loop fusion | flops 128 | bytes 1536 | tf_op jit(solution)/shard_map/squeeze | solution.py:208
  (6 shorter events, 0.2 us)
Async XLA Ops:
  0.6 4.5 %copy-start.3 = (s32[2,1]{0,1:T(1,128)S(1)}, s32[2,1]{0,1:T(1,128)}, u32[]{:S(2)}) copy-start(s32[2,1]{0,1:T(1,128)} %param.6) | copy-start | bytes 28
  0.6 9.5 %collective-permute-start.1 = (bf16[1024,128]{1,0:T(8,128)(2,1)}, bf16[1024,128]{1,0:T(8,128)(2,1)S(1)}, u32[]{:S(2)}, u32[]{:S(2)}) collective-permute-start(bf16[1024,128]{1,0:T(8,128)(2,1)} %own.1), channel_id=1, source_target_pairs={{0,2},{1,3},{2,0},{3,1},{4,6},{5,7},{6,4},{7,5},{8,10},{9,11},{10,... | collective-permute-start | bytes 786440 | tf_op jit(solution)/shard_map/ppermute | solution.py:21
  3.6 8.0 %collective-permute-start.9 = (bf16[1024,128]{1,0:T(8,128)(2,1)}, bf16[1024,128]{1,0:T(8,128)(2,1)S(1)}, u32[]{:S(2)}, u32[]{:S(2)}) collective-permute-start(bf16[1024,128]{1,0:T(8,128)(2,1)} %own.1), channel_id=1, source_target_pairs={{0,4},{4,0},{8,12},{12,8},{16,20},{20,16},{24,28},{28,24},{1,5},{5... | collective-permute-start | bytes 786440 | tf_op jit(solution)/shard_map/ppermute | solution.py:21
  5.2 1.0 %copy-start.1 = (bf16[1024,128]{1,0:T(8,128)(2,1)S(1)}, bf16[1024,128]{1,0:T(8,128)(2,1)}, u32[]{:S(2)}) copy-start(bf16[1024,128]{1,0:T(8,128)(2,1)} %own.1) | copy-start | bytes 786436
  7.0 5.0 %collective-permute-start = (bf16[1024,128]{1,0:T(8,128)(2,1)S(1)}, bf16[1024,128]{1,0:T(8,128)(2,1)S(1)}, u32[]{:S(2)}, u32[]{:S(2)}) collective-permute-start(bf16[1024,128]{1,0:T(8,128)(2,1)S(1)} %get-tuple-element.18.refs_0_), channel_id=1, source_target_pairs={{0,1},{1,0},{2,3},{3,2},{4,5},{5,4},{6,7},{7,6},{8,9},{9,8},{10,11... | collective-permute-start | bytes 786440 | tf_op jit(solution)/shard_map/ppermute | solution.py:21
  10.2 1.8 %collective-permute-start.2 = (bf16[1024,128]{1,0:T(8,128)(2,1)S(1)}, bf16[1024,128]{1,0:T(8,128)(2,1)S(1)}, u32[]{:S(2)}, u32[]{:S(2)}) collective-permute-start(bf16[1024,128]{1,0:T(8,128)(2,1)S(1)} %collective-permute-done.1.refs_1_.refs_2_), channel_id=1, source_target_pairs={{0,1},{1,0},{2,3},{3,2},{4,5},{5,4},{6,7},{7,6},{8,9},{9,8},{10,11... | collective-permute-start | bytes 786440 | tf_op jit(solution)/shard_map/ppermute | solution.py:21
  11.6 12.6 %collective-permute-start.11 = (bf16[1024,128]{1,0:T(8,128)(2,1)S(1)}, bf16[1024,128]{1,0:T(8,128)(2,1)S(1)}, u32[]{:S(2)}, u32[]{:S(2)}) collective-permute-start(bf16[1024,128]{1,0:T(8,128)(2,1)S(1)} %collective-permute-done.9.refs_0_), channel_id=1, source_target_pairs={{0,2},{1,3},{2,0},{3,1},{4,6},{5,7},{6,4},{7,5},{8,10},{9,11},{10,... | collective-permute-start | bytes 786440 | tf_op jit(solution)/shard_map/ppermute | solution.py:21
  12.9 5.6 %collective-permute-start.4 = (bf16[512,128]{1,0:T(8,128)(2,1)S(1)}, bf16[512,128]{1,0:T(8,128)(2,1)S(1)}, u32[]{:S(2)}, u32[]{:S(2)}) collective-permute-start(bf16[512,128]{1,0:T(8,128)(2,1)S(1)} %get-tuple-element.20), channel_id=1, source_target_pairs={{0,4},{4,0},{8,12},{12,8},{16,20},{20,16},{24,28},{28,24},{1,5},{5... | collective-permute-start | bytes 393224 | tf_op jit(solution)/shard_map/ppermute | solution.py:21
  14.7 8.9 %collective-permute-start.3 = (bf16[512,128]{1,0:T(8,128)(2,1)S(1)}, bf16[512,128]{1,0:T(8,128)(2,1)S(1)}, u32[]{:S(2)}, u32[]{:S(2)}) collective-permute-start(bf16[512,128]{1,0:T(8,128)(2,1)S(1)} %get-tuple-element.19), channel_id=1, source_target_pairs={{0,16},{4,20},{8,24},{12,28},{16,0},{20,4},{24,8},{28,12},{1,17},{... | collective-permute-start | bytes 393224 | tf_op jit(solution)/shard_map/ppermute | solution.py:21
  17.3 13.5 %collective-permute-start.10 = (bf16[1024,128]{1,0:T(8,128)(2,1)S(1)}, bf16[1024,128]{1,0:T(8,128)(2,1)S(1)}, u32[]{:S(2)}, u32[]{:S(2)}) collective-permute-start(bf16[1024,128]{1,0:T(8,128)(2,1)S(1)} %collective-permute-done.9.refs_0_), channel_id=1, source_target_pairs={{0,1},{1,0},{2,3},{3,2},{4,5},{5,4},{6,7},{7,6},{8,9},{9,8},{10,11... | collective-permute-start | bytes 786440 | tf_op jit(solution)/shard_map/ppermute | solution.py:21
  18.6 6.5 %collective-permute-start.6 = (bf16[512,128]{1,0:T(8,128)(2,1)S(1)}, bf16[512,128]{1,0:T(8,128)(2,1)S(1)}, u32[]{:S(2)}, u32[]{:S(2)}) collective-permute-start(bf16[512,128]{1,0:T(8,128)(2,1)S(1)} %add.15), channel_id=1, source_target_pairs={{0,8},{4,12},{8,0},{12,4},{16,24},{20,28},{24,16},{28,20},{1,9},{5... | collective-permute-start | bytes 393224 | tf_op jit(solution)/shard_map/ppermute | solution.py:21
  23.6 5.0 %collective-permute-start.5 = (bf16[512,128]{1,0:T(8,128)(2,1)S(1)}, bf16[512,128]{1,0:T(8,128)(2,1)S(1)}, u32[]{:S(2)}, u32[]{:S(2)}) collective-permute-start(bf16[512,128]{1,0:T(8,128)(2,1)S(1)} %add.16), channel_id=1, source_target_pairs={{0,4},{4,0},{8,12},{12,8},{16,20},{20,16},{24,28},{28,24},{1,5},{5... | collective-permute-start | bytes 393224 | tf_op jit(solution)/shard_map/ppermute | solution.py:21
  24.2 6.5 %collective-permute-start.12 = (bf16[1024,128]{1,0:T(8,128)(2,1)S(1)}, bf16[1024,128]{1,0:T(8,128)(2,1)S(1)}, u32[]{:S(2)}, u32[]{:S(2)}) collective-permute-start(bf16[1024,128]{1,0:T(8,128)(2,1)S(1)} %collective-permute-done.11.refs_2_), channel_id=1, source_target_pairs={{0,1},{1,0},{2,3},{3,2},{4,5},{5,4},{6,7},{7,6},{8,9},{9,8},{10,11... | collective-permute-start | bytes 786440 | tf_op jit(solution)/shard_map/ppermute | solution.py:21
  25.1 5.2 %copy-start = (bf16[1024,128]{1,0:T(8,128)(2,1)S(1)}, bf16[1024,128]{1,0:T(8,128)(2,1)}, u32[]{:S(2)}) copy-start(bf16[1024,128]{1,0:T(8,128)(2,1)} %signals.5) | copy-start | bytes 786436
  25.1 8.9 %collective-permute-start.8 = (bf16[512,128]{1,0:T(8,128)(2,1)S(1)}, bf16[512,128]{1,0:T(8,128)(2,1)S(1)}, u32[]{:S(2)}, u32[]{:S(2)}) collective-permute-start(bf16[512,128]{1,0:T(8,128)(2,1)S(1)} %add.17), channel_id=1, source_target_pairs={{0,16},{4,20},{8,24},{12,28},{16,0},{20,4},{24,8},{28,12},{1,17},{... | collective-permute-start | bytes 393224 | tf_op jit(solution)/shard_map/ppermute | solution.py:21
  28.7 6.0 %collective-permute-start.7 = (bf16[512,128]{1,0:T(8,128)(2,1)S(1)}, bf16[512,128]{1,0:T(8,128)(2,1)S(1)}, u32[]{:S(2)}, u32[]{:S(2)}) collective-permute-start(bf16[512,128]{1,0:T(8,128)(2,1)S(1)} %add.18.refs_0_), channel_id=1, source_target_pairs={{0,8},{4,12},{8,0},{12,4},{16,24},{20,28},{24,16},{28,20},{1,9},{5... | collective-permute-start | bytes 393224 | tf_op jit(solution)/shard_map/ppermute | solution.py:21
  31.3 3.4 %copy-start.2 = (bf16[2,1,64,64]{3,2,1,0:T(8,128)(2,1)S(1)}, bf16[2,1,64,64]{3,2,1,0:T(8,128)(2,1)}, u32[]{:S(2)}) copy-start(bf16[2,1,64,64]{3,2,1,0:T(8,128)(2,1)} %inverses.1) | copy-start | bytes 49156
  36.7 3.6 %collective-permute-start.13 = (f32[1,128]{1,0:T(1,128)S(1)}, f32[1,128]{1,0:T(1,128)S(1)}, u32[]{:S(2)}, u32[]{:S(2)}) collective-permute-start(f32[1,128]{1,0:T(1,128)S(1)} %get-tuple-element.30), channel_id=1, source_target_pairs={{0,8},{4,12},{8,0},{12,4},{16,24},{20,28},{24,16},{28,20},{1,9},{5... | collective-permute-start | bytes 1544 | tf_op jit(solution)/shard_map/ppermute | solution.py:21
  40.3 5.2 %collective-permute-start.14 = (f32[1,128]{1,0:T(1,128)S(1)}, f32[1,128]{1,0:T(1,128)S(1)}, u32[]{:S(2)}, u32[]{:S(2)}) collective-permute-start(f32[1,128]{1,0:T(1,128)S(1)} %max.6), channel_id=1, source_target_pairs={{0,16},{4,20},{8,24},{12,28},{16,0},{20,4},{24,8},{28,12},{1,17},{... | collective-permute-start | bytes 1544 | tf_op jit(solution)/shard_map/ppermute | solution.py:21

commit v4 on v3

--- a/solution.py
+++ b/solution.py
@@ -129,6 +129,7 @@
         at += count
     sides = refs[at:-3]
     chosen = jnp.concatenate(halves, 0)
+    panels = [matmul(turned[...], chosen).astype(jnp.bfloat16) for turned in sides[::2]]
     right = matmul(chosen.T, jnp.concatenate([signals[...], chosen], 1))
     rows, gram = right[:, :SB], right[:, SB:].astype(jnp.bfloat16)
     one = exact(inverses[0, 0], rows[:BLK]).astype(jnp.bfloat16)
@@ -139,9 +140,7 @@
     me = lax.axis_index("sig")
     best = None
     for side in range(n_sides):
-        turned, first = sides[2 * side], sides[2 * side + 1]
-        panel = matmul(turned[...], chosen).astype(jnp.bfloat16)
-        corr = first[...] - matmul(panel, weights)
+        corr = sides[2 * side + 1][...] - matmul(panels[side], weights)
         if side == 0:
             for i in range(n_sig):
                 at = pl.multiple_of((me ^ i) * SB, SB)
@@ -193,7 +192,7 @@
     first, second = pick(n_sig, selected, base, here[1:], [depth, depth])
     there = gather(beside, beside)
     blocks = [first, second]
-    orders = [[top] + bits[:-1], list(bits)]
+    orders = [[top] + bits[-2::-1], bits[-2::-1] + [top]]
     arrived = [swap(blocks[h], "atoms", n_atoms, orders[h][0]) for h in range(2)]
     for i in range(1, len(bits)):
         for h in (1, 0):

time: 46.2 us -> 45 us (0.974)
  starting transfers between devices: 20.2 us -> 15.8 us
  waiting for transfers between devices: 17.4 us -> 21.1 us
  Pallas kernels: 4.71 us -> 4.12 us
    ppermute x15, starting transfers between devices: 20.2 us -> 15.8 us  [swap(): return lax.ppermute(block, axis, [(i, i ^ mask) for i in range(size)])]
    ppermute x15, waiting for transfers between devices: 17.4 us -> 21.1 us  [swap(): return lax.ppermute(block, axis, [(i, i ^ mask) for i in range(size)])]
    pallas_call x1, Pallas kernels: 2.03 us -> 1.44 us  [finish(): pl.pallas_call(functools.partial(finish_kernel, n_sig, [len(term) for ter...]
where the time goes in v4:
time: 45 us; the launch traced here: 44.8 us
  waiting for transfers between devices  21.1 us (47%)
  starting transfers between devices  15.8 us (35%)
  Pallas kernels  4.12 us (9%)
  local copies, waits for them, and re-layouts  2.27 us (5%)
  between operations  0.75 us (2%)
  other arithmetic  0.71 us (2%)
    ppermute x15, waiting for transfers between devices, swap(): return lax.ppermute(block, axis, [(i, i ^ mask) for i in range(size)])  21.1 us
    ppermute x15, starting transfers between devices, swap(): return lax.ppermute(block, axis, [(i, i ^ mask) for i in range(size)])  15.8 us
    unnamed x10, local copies, waits for them, and re-layouts  2.27 us
    pallas_call x1, Pallas kernels, finish(): pl.pallas_call(functools.partial(finish_kernel, n_sig, [len(term) for ter...  1.44 us
    pallas_call x2, Pallas kernels, ready(): pl.pallas_call(functools.partial(ready_kernel, [len(piece) for piece in p...  0.95 us
    pallas_call x1, Pallas kernels, pick(): pl.pallas_call(functools.partial(pick_kernel, n_sig), out_shape=tuple((pl...  0.92 us
  transfers between devices with their start and end apart: 15, of which 10 were waited for; matrix products, arithmetic and copies ran while one was open for 3% of the time, Pallas kernels for 6%

profile of v4, /device:TPU:0, one launch (start us, length us, event | category | flops | bytes accessed | tf_op | source)
XLA Modules:
  0.0 44.8 jit_solution(11793371188484510072)
XLA Ops:
  0.6 0.0 copy-start.3
  0.6 3.0 %collective-permute-start.1 = (bf16[1024,128]{1,0:T(8,128)(2,1)}, bf16[1024,128]{1,0:T(8,128)(2,1)S(1)}, u32[]{:S(2)}, u32[]{:S(2)}) collective-permute-start(bf16[1024,128]{1,0:T(8,128)(2,1)} %own.1), channel_id=1, source_target_pairs={{0,2},{1,3},{2,0},{3,1},{4,6},{5,7},{6,4},{7,5},{8,10},{9,11},{10,... | collective-permute-start | bytes 786440 | tf_op jit(solution)/shard_map/ppermute | solution.py:21
  3.6 1.5 %collective-permute-start.9 = (bf16[1024,128]{1,0:T(8,128)(2,1)}, bf16[1024,128]{1,0:T(8,128)(2,1)S(1)}, u32[]{:S(2)}, u32[]{:S(2)}) collective-permute-start(bf16[1024,128]{1,0:T(8,128)(2,1)} %own.1), channel_id=1, source_target_pairs={{0,4},{4,0},{8,12},{12,8},{16,20},{20,16},{24,28},{28,24},{1,5},{5... | collective-permute-start | bytes 786440 | tf_op jit(solution)/shard_map/ppermute | solution.py:21
  5.2 0.0 copy-done.3
  5.2 0.0 copy-start.1
  5.2 1.0 %copy-done.1 = bf16[1024,128]{1,0:T(8,128)(2,1)S(1)} copy-done((bf16[1024,128]{1,0:T(8,128)(2,1)S(1)}, bf16[1024,128]{1,0:T(8,128)(2,1)}, u32[]{:S(2)}) %copy-start.1) | copy-done | bytes 262168
  6.1 0.8 %fetch.1 = (bf16[1024,128]{1,0:T(8,128)(2,1)S(1)}, bf16[1024,128]{1,0:T(8,128)(2,1)S(1)}) custom-call(s32[2]{0:T(128)S(1)} %bitcast.3, bf16[1024,128]{1,0:T(8,128)(2,1)S(1)} %copy-done.1), custom_call_target="tpu_custom_call" | custom-call | tf_op jit(solution)/shard_map/fetch/pallas_call | solution.py:54
  7.0 0.1 collective-permute-start
  7.0 3.1 %collective-permute-done.1.refs_1_.refs_2_ = bf16[1024,128]{1,0:T(8,128)(2,1)S(1)} collective-permute-done((bf16[1024,128]{1,0:T(8,128)(2,1)}, bf16[1024,128]{1,0:T(8,128)(2,1)S(1)}, u32[]{:S(2)}, u32[]{:S(2)}) %collective-permute-start.1) | collective-permute-done | bytes 262176 | tf_op jit(solution)/shard_map/ppermute | solution.py:21
  10.2 0.0 collective-permute-start.2
  10.2 1.5 %collective-permute-done.9.refs_0_ = bf16[1024,128]{1,0:T(8,128)(2,1)S(1)} collective-permute-done((bf16[1024,128]{1,0:T(8,128)(2,1)}, bf16[1024,128]{1,0:T(8,128)(2,1)S(1)}, u32[]{:S(2)}, u32[]{:S(2)}) %collective-permute-start.9) | collective-permute-done | bytes 262176 | tf_op jit(solution)/shard_map/ppermute | solution.py:21
  11.6 0.4 collective-permute-start.11
  12.0 0.0 collective-permute-done.refs_0_.refs_1_
  12.0 0.0 collective-permute-done.2.refs_2_.refs_3_
  12.0 0.9 %pick.1 = (bf16[512,128]{1,0:T(8,128)(2,1)S(1)}, bf16[512,128]{1,0:T(8,128)(2,1)S(1)}) custom-call(s32[2]{0:T(128)S(1)} %bitcast.4, bf16[1024,128]{1,0:T(8,128)(2,1)S(1)} %get-tuple-element.17.base, bf16[1024,128]{1,0:T(8,128)(2,1)S(1)} %collective-permute-done.refs_0_.refs_1_, bf16[1024,128]{1,0:T(8,128)(2,1)S(1)} %collective-permute-done.1.refs_1_.refs_2_, ...), custom_call_target="tpu_custom_call" | custom-call | tf_op jit(solution)/shard_map/pick/pallas_call | solution.py:76
  12.9 1.8 %collective-permute-start.4 = (bf16[512,128]{1,0:T(8,128)(2,1)S(1)}, bf16[512,128]{1,0:T(8,128)(2,1)S(1)}, u32[]{:S(2)}, u32[]{:S(2)}) collective-permute-start(bf16[512,128]{1,0:T(8,128)(2,1)S(1)} %get-tuple-element.20), channel_id=1, source_target_pairs={{0,8},{4,12},{8,0},{12,4},{16,24},{20,28},{24,16},{28,20},{1,9},{5... | collective-permute-start | bytes 393224 | tf_op jit(solution)/shard_map/ppermute | solution.py:21
  14.7 2.6 %collective-permute-start.3 = (bf16[512,128]{1,0:T(8,128)(2,1)S(1)}, bf16[512,128]{1,0:T(8,128)(2,1)S(1)}, u32[]{:S(2)}, u32[]{:S(2)}) collective-permute-start(bf16[512,128]{1,0:T(8,128)(2,1)S(1)} %get-tuple-element.19), channel_id=1, source_target_pairs={{0,16},{4,20},{8,24},{12,28},{16,0},{20,4},{24,8},{28,12},{1,17},{... | collective-permute-start | bytes 393224 | tf_op jit(solution)/shard_map/ppermute | solution.py:21
  17.3 0.0 collective-permute-start.10
  17.3 3.4 %collective-permute-done.4 = bf16[512,128]{1,0:T(8,128)(2,1)S(1)} collective-permute-done((bf16[512,128]{1,0:T(8,128)(2,1)S(1)}, bf16[512,128]{1,0:T(8,128)(2,1)S(1)}, u32[]{:S(2)}, u32[]{:S(2)}) %collective-permute-start.4) | collective-permute-done | bytes 131104 | tf_op jit(solution)/shard_map/ppermute | solution.py:21
  20.8 1.5 %collective-permute-start.6 = (bf16[512,128]{1,0:T(8,128)(2,1)S(1)}, bf16[512,128]{1,0:T(8,128)(2,1)S(1)}, u32[]{:S(2)}, u32[]{:S(2)}) collective-permute-start(bf16[512,128]{1,0:T(8,128)(2,1)S(1)} %add.15), channel_id=1, source_target_pairs={{0,4},{4,0},{8,12},{12,8},{16,20},{20,16},{24,28},{28,24},{1,5},{5... | collective-permute-start | bytes 393224 | tf_op jit(solution)/shard_map/ppermute | solution.py:21
  22.3 1.3 %collective-permute-done.3 = bf16[512,128]{1,0:T(8,128)(2,1)S(1)} collective-permute-done((bf16[512,128]{1,0:T(8,128)(2,1)S(1)}, bf16[512,128]{1,0:T(8,128)(2,1)S(1)}, u32[]{:S(2)}, u32[]{:S(2)}) %collective-permute-start.3) | collective-permute-done | bytes 131104 | tf_op jit(solution)/shard_map/ppermute | solution.py:21
  23.6 0.5 %collective-permute-start.5 = (bf16[512,128]{1,0:T(8,128)(2,1)S(1)}, bf16[512,128]{1,0:T(8,128)(2,1)S(1)}, u32[]{:S(2)}, u32[]{:S(2)}) collective-permute-start(bf16[512,128]{1,0:T(8,128)(2,1)S(1)} %add.16), channel_id=1, source_target_pairs={{0,8},{4,12},{8,0},{12,4},{16,24},{20,28},{24,16},{28,20},{1,9},{5... | collective-permute-start | bytes 393224 | tf_op jit(solution)/shard_map/ppermute | solution.py:21
  24.1 0.0 collective-permute-done.11.refs_2_
  24.1 0.0 collective-permute-start.12
  24.1 1.7 %collective-permute-done.6 = bf16[512,128]{1,0:T(8,128)(2,1)S(1)} collective-permute-done((bf16[512,128]{1,0:T(8,128)(2,1)S(1)}, bf16[512,128]{1,0:T(8,128)(2,1)S(1)}, u32[]{:S(2)}, u32[]{:S(2)}) %collective-permute-start.6) | collective-permute-done | bytes 131104 | tf_op jit(solution)/shard_map/ppermute | solution.py:21
  25.9 0.0 copy-start
  25.9 1.4 %collective-permute-start.8 = (bf16[512,128]{1,0:T(8,128)(2,1)S(1)}, bf16[512,128]{1,0:T(8,128)(2,1)S(1)}, u32[]{:S(2)}, u32[]{:S(2)}) collective-permute-start(bf16[512,128]{1,0:T(8,128)(2,1)S(1)} %add.17), channel_id=1, source_target_pairs={{0,16},{4,20},{8,24},{12,28},{16,0},{20,4},{24,8},{28,12},{1,17},{... | collective-permute-start | bytes 393224 | tf_op jit(solution)/shard_map/ppermute | solution.py:21
  27.3 2.4 %collective-permute-done.5 = bf16[512,128]{1,0:T(8,128)(2,1)S(1)} collective-permute-done((bf16[512,128]{1,0:T(8,128)(2,1)S(1)}, bf16[512,128]{1,0:T(8,128)(2,1)S(1)}, u32[]{:S(2)}, u32[]{:S(2)}) %collective-permute-start.5) | collective-permute-done | bytes 131104 | tf_op jit(solution)/shard_map/ppermute | solution.py:21
  29.8 1.6 %collective-permute-start.7 = (bf16[512,128]{1,0:T(8,128)(2,1)S(1)}, bf16[512,128]{1,0:T(8,128)(2,1)S(1)}, u32[]{:S(2)}, u32[]{:S(2)}) collective-permute-start(bf16[512,128]{1,0:T(8,128)(2,1)S(1)} %add.18.refs_0_), channel_id=1, source_target_pairs={{0,4},{4,0},{8,12},{12,8},{16,20},{20,16},{24,28},{28,24},{1,5},{5... | collective-permute-start | bytes 393224 | tf_op jit(solution)/shard_map/ppermute | solution.py:21
  31.4 0.0 copy-done
  31.4 0.5 %ready.2 = (bf16[512,1024]{1,0:T(8,128)(2,1)S(1)}, f32[512,128]{1,0:T(8,128)S(1)}) custom-call(bf16[1024,128]{1,0:T(8,128)(2,1)S(1)} %copy-done, bf16[1024,128]{1,0:T(8,128)(2,1)S(1)} %get-tuple-element.18.refs_0_, bf16[1024,128]{1,0:T(8,128)(2,1)S(1)} %collective-permute-done.refs_0_.refs_1_, bf16[1024,128]{1,0:T(8,128)(2,1)S(1)} %collective-permute-done.1.refs_1_.refs_2_, ...), custom_call_target="tpu_custom_call" | custom-call | tf_op jit(solution)/shard_map/ready/pallas_call | solution.py:99
  31.8 0.0 collective-permute-done.10.refs_1_
  31.9 0.0 collective-permute-done.12.refs_3_
  31.9 0.5 %ready.3 = (bf16[512,1024]{1,0:T(8,128)(2,1)S(1)}, f32[512,128]{1,0:T(8,128)S(1)}) custom-call(bf16[1024,128]{1,0:T(8,128)(2,1)S(1)} %copy-done, bf16[1024,128]{1,0:T(8,128)(2,1)S(1)} %collective-permute-done.9.refs_0_, bf16[1024,128]{1,0:T(8,128)(2,1)S(1)} %collective-permute-done.10.refs_1_, bf16[1024,128]{1,0:T(8,128)(2,1)S(1)} %collective-permute-done.11.refs_2_, ...), custom_call_target="tpu_custom_call" | custom-call | tf_op jit(solution)/shard_map/ready/pallas_call | solution.py:99
  32.3 0.0 copy-start.2
  32.4 1.6 %collective-permute-done.8 = bf16[512,128]{1,0:T(8,128)(2,1)S(1)} collective-permute-done((bf16[512,128]{1,0:T(8,128)(2,1)S(1)}, bf16[512,128]{1,0:T(8,128)(2,1)S(1)}, u32[]{:S(2)}, u32[]{:S(2)}) %collective-permute-start.8) | collective-permute-done | bytes 131104 | tf_op jit(solution)/shard_map/ppermute | solution.py:21
  34.0 0.8 %collective-permute-done.7.refs_1_ = bf16[512,128]{1,0:T(8,128)(2,1)S(1)} collective-permute-done((bf16[512,128]{1,0:T(8,128)(2,1)S(1)}, bf16[512,128]{1,0:T(8,128)(2,1)S(1)}, u32[]{:S(2)}, u32[]{:S(2)}) %collective-permute-start.7) | collective-permute-done | bytes 131104 | tf_op jit(solution)/shard_map/ppermute | solution.py:21
  34.8 0.0 copy-done.2
  34.8 1.4 %finish.1 = (bf16[512,128]{1,0:T(8,128)(2,1)S(1)}, bf16[2,64,128]{2,1,0:T(8,128)(2,1)S(1)}, f32[1,128]{1,0:T(1,128)S(1)}) custom-call(bf16[2,1,64,64]{3,2,1,0:T(8,128)(2,1)S(1)} %copy-done.2, bf16[1024,128]{1,0:T(8,128)(2,1)S(1)} %copy-done, bf16[512,128]{1,0:T(8,128)(2,1)S(1)} %add.18.refs_0_, bf16[512,128]{1,0:T(8,128)(2,1)S(1)} %collective-permute-done.7.refs_1_, ...), custom_call_target="tpu_custom_call" | custom-call | tf_op jit(solution)/shard_map/finish/pallas_call | solution.py:155
  36.3 0.1 collective-permute-start.13
  36.3 3.5 %collective-permute-done.13 = f32[1,128]{1,0:T(1,128)S(1)} collective-permute-done((f32[1,128]{1,0:T(1,128)S(1)}, f32[1,128]{1,0:T(1,128)S(1)}, u32[]{:S(2)}, u32[]{:S(2)}) %collective-permute-start.13) | collective-permute-done | bytes 544 | tf_op jit(solution)/shard_map/ppermute | solution.py:21
  39.9 1.3 %collective-permute-start.14 = (f32[1,128]{1,0:T(1,128)S(1)}, f32[1,128]{1,0:T(1,128)S(1)}, u32[]{:S(2)}, u32[]{:S(2)}) collective-permute-start(f32[1,128]{1,0:T(1,128)S(1)} %max.6), channel_id=1, source_target_pairs={{0,16},{4,20},{8,24},{12,28},{16,0},{20,4},{24,8},{28,12},{1,17},{... | collective-permute-start | bytes 1544 | tf_op jit(solution)/shard_map/ppermute | solution.py:21
  41.2 0.7 %copy.7 = bf16[512,128]{1,0:T(8,128)(2,1)} copy(bf16[512,128]{1,0:T(8,128)(2,1)S(1)} %get-tuple-element.31) | data formatting | bytes 262144
  41.9 0.6 %copy.8 = bf16[2,64,128]{2,1,0:T(8,128)(2,1)} copy(bf16[2,64,128]{2,1,0:T(8,128)(2,1)S(1)} %get-tuple-element.32) | data formatting | bytes 65536
  42.5 1.8 %collective-permute-done.14 = f32[1,128]{1,0:T(1,128)S(1)} collective-permute-done((f32[1,128]{1,0:T(1,128)S(1)}, f32[1,128]{1,0:T(1,128)S(1)}, u32[]{:S(2)}, u32[]{:S(2)}) %collective-permute-start.14) | collective-permute-done | bytes 544 | tf_op jit(solution)/shard_map/ppermute | solution.py:21
  44.3 0.5 %maximum_bitcast_fusion = f32[128]{0:T(128)} fusion(f32[1,128]{1,0:T(1,128)S(1)} %max.6, f32[1,128]{1,0:T(1,128)S(1)} %collective-permute-done.14), kind=kLoop, calls=%fused_computation | loop fusion | flops 128 | bytes 1536 | tf_op jit(solution)/shard_map/squeeze | solution.py:207
  (6 shorter events, 0.2 us)
Async XLA Ops:
  0.6 4.5 %copy-start.3 = (s32[2,1]{0,1:T(1,128)S(1)}, s32[2,1]{0,1:T(1,128)}, u32[]{:S(2)}) copy-start(s32[2,1]{0,1:T(1,128)} %param.6) | copy-start | bytes 28
  0.6 9.5 %collective-permute-start.1 = (bf16[1024,128]{1,0:T(8,128)(2,1)}, bf16[1024,128]{1,0:T(8,128)(2,1)S(1)}, u32[]{:S(2)}, u32[]{:S(2)}) collective-permute-start(bf16[1024,128]{1,0:T(8,128)(2,1)} %own.1), channel_id=1, source_target_pairs={{0,2},{1,3},{2,0},{3,1},{4,6},{5,7},{6,4},{7,5},{8,10},{9,11},{10,... | collective-permute-start | bytes 786440 | tf_op jit(solution)/shard_map/ppermute | solution.py:21
  3.6 8.0 %collective-permute-start.9 = (bf16[1024,128]{1,0:T(8,128)(2,1)}, bf16[1024,128]{1,0:T(8,128)(2,1)S(1)}, u32[]{:S(2)}, u32[]{:S(2)}) collective-permute-start(bf16[1024,128]{1,0:T(8,128)(2,1)} %own.1), channel_id=1, source_target_pairs={{0,4},{4,0},{8,12},{12,8},{16,20},{20,16},{24,28},{28,24},{1,5},{5... | collective-permute-start | bytes 786440 | tf_op jit(solution)/shard_map/ppermute | solution.py:21
  5.2 1.0 %copy-start.1 = (bf16[1024,128]{1,0:T(8,128)(2,1)S(1)}, bf16[1024,128]{1,0:T(8,128)(2,1)}, u32[]{:S(2)}) copy-start(bf16[1024,128]{1,0:T(8,128)(2,1)} %own.1) | copy-start | bytes 786436
  7.0 5.0 %collective-permute-start = (bf16[1024,128]{1,0:T(8,128)(2,1)S(1)}, bf16[1024,128]{1,0:T(8,128)(2,1)S(1)}, u32[]{:S(2)}, u32[]{:S(2)}) collective-permute-start(bf16[1024,128]{1,0:T(8,128)(2,1)S(1)} %get-tuple-element.18.refs_0_), channel_id=1, source_target_pairs={{0,1},{1,0},{2,3},{3,2},{4,5},{5,4},{6,7},{7,6},{8,9},{9,8},{10,11... | collective-permute-start | bytes 786440 | tf_op jit(solution)/shard_map/ppermute | solution.py:21
  10.2 1.8 %collective-permute-start.2 = (bf16[1024,128]{1,0:T(8,128)(2,1)S(1)}, bf16[1024,128]{1,0:T(8,128)(2,1)S(1)}, u32[]{:S(2)}, u32[]{:S(2)}) collective-permute-start(bf16[1024,128]{1,0:T(8,128)(2,1)S(1)} %collective-permute-done.1.refs_1_.refs_2_), channel_id=1, source_target_pairs={{0,1},{1,0},{2,3},{3,2},{4,5},{5,4},{6,7},{7,6},{8,9},{9,8},{10,11... | collective-permute-start | bytes 786440 | tf_op jit(solution)/shard_map/ppermute | solution.py:21
  11.6 12.5 %collective-permute-start.11 = (bf16[1024,128]{1,0:T(8,128)(2,1)S(1)}, bf16[1024,128]{1,0:T(8,128)(2,1)S(1)}, u32[]{:S(2)}, u32[]{:S(2)}) collective-permute-start(bf16[1024,128]{1,0:T(8,128)(2,1)S(1)} %collective-permute-done.9.refs_0_), channel_id=1, source_target_pairs={{0,2},{1,3},{2,0},{3,1},{4,6},{5,7},{6,4},{7,5},{8,10},{9,11},{10,... | collective-permute-start | bytes 786440 | tf_op jit(solution)/shard_map/ppermute | solution.py:21
  12.9 7.8 %collective-permute-start.4 = (bf16[512,128]{1,0:T(8,128)(2,1)S(1)}, bf16[512,128]{1,0:T(8,128)(2,1)S(1)}, u32[]{:S(2)}, u32[]{:S(2)}) collective-permute-start(bf16[512,128]{1,0:T(8,128)(2,1)S(1)} %get-tuple-element.20), channel_id=1, source_target_pairs={{0,8},{4,12},{8,0},{12,4},{16,24},{20,28},{24,16},{28,20},{1,9},{5... | collective-permute-start | bytes 393224 | tf_op jit(solution)/shard_map/ppermute | solution.py:21
  14.7 8.9 %collective-permute-start.3 = (bf16[512,128]{1,0:T(8,128)(2,1)S(1)}, bf16[512,128]{1,0:T(8,128)(2,1)S(1)}, u32[]{:S(2)}, u32[]{:S(2)}) collective-permute-start(bf16[512,128]{1,0:T(8,128)(2,1)S(1)} %get-tuple-element.19), channel_id=1, source_target_pairs={{0,16},{4,20},{8,24},{12,28},{16,0},{20,4},{24,8},{28,12},{1,17},{... | collective-permute-start | bytes 393224 | tf_op jit(solution)/shard_map/ppermute | solution.py:21
  17.3 14.5 %collective-permute-start.10 = (bf16[1024,128]{1,0:T(8,128)(2,1)S(1)}, bf16[1024,128]{1,0:T(8,128)(2,1)S(1)}, u32[]{:S(2)}, u32[]{:S(2)}) collective-permute-start(bf16[1024,128]{1,0:T(8,128)(2,1)S(1)} %collective-permute-done.9.refs_0_), channel_id=1, source_target_pairs={{0,1},{1,0},{2,3},{3,2},{4,5},{5,4},{6,7},{7,6},{8,9},{9,8},{10,11... | collective-permute-start | bytes 786440 | tf_op jit(solution)/shard_map/ppermute | solution.py:21
  20.8 5.0 %collective-permute-start.6 = (bf16[512,128]{1,0:T(8,128)(2,1)S(1)}, bf16[512,128]{1,0:T(8,128)(2,1)S(1)}, u32[]{:S(2)}, u32[]{:S(2)}) collective-permute-start(bf16[512,128]{1,0:T(8,128)(2,1)S(1)} %add.15), channel_id=1, source_target_pairs={{0,4},{4,0},{8,12},{12,8},{16,20},{20,16},{24,28},{28,24},{1,5},{5... | collective-permute-start | bytes 393224 | tf_op jit(solution)/shard_map/ppermute | solution.py:21
  23.6 6.1 %collective-permute-start.5 = (bf16[512,128]{1,0:T(8,128)(2,1)S(1)}, bf16[512,128]{1,0:T(8,128)(2,1)S(1)}, u32[]{:S(2)}, u32[]{:S(2)}) collective-permute-start(bf16[512,128]{1,0:T(8,128)(2,1)S(1)} %add.16), channel_id=1, source_target_pairs={{0,8},{4,12},{8,0},{12,4},{16,24},{20,28},{24,16},{28,20},{1,9},{5... | collective-permute-start | bytes 393224 | tf_op jit(solution)/shard_map/ppermute | solution.py:21
  24.1 7.7 %collective-permute-start.12 = (bf16[1024,128]{1,0:T(8,128)(2,1)S(1)}, bf16[1024,128]{1,0:T(8,128)(2,1)S(1)}, u32[]{:S(2)}, u32[]{:S(2)}) collective-permute-start(bf16[1024,128]{1,0:T(8,128)(2,1)S(1)} %collective-permute-done.11.refs_2_), channel_id=1, source_target_pairs={{0,1},{1,0},{2,3},{3,2},{4,5},{5,4},{6,7},{7,6},{8,9},{9,8},{10,11... | collective-permute-start | bytes 786440 | tf_op jit(solution)/shard_map/ppermute | solution.py:21
  25.9 5.5 %copy-start = (bf16[1024,128]{1,0:T(8,128)(2,1)S(1)}, bf16[1024,128]{1,0:T(8,128)(2,1)}, u32[]{:S(2)}) copy-start(bf16[1024,128]{1,0:T(8,128)(2,1)} %signals.5) | copy-start | bytes 786436
  25.9 8.1 %collective-permute-start.8 = (bf16[512,128]{1,0:T(8,128)(2,1)S(1)}, bf16[512,128]{1,0:T(8,128)(2,1)S(1)}, u32[]{:S(2)}, u32[]{:S(2)}) collective-permute-start(bf16[512,128]{1,0:T(8,128)(2,1)S(1)} %add.17), channel_id=1, source_target_pairs={{0,16},{4,20},{8,24},{12,28},{16,0},{20,4},{24,8},{28,12},{1,17},{... | collective-permute-start | bytes 393224 | tf_op jit(solution)/shard_map/ppermute | solution.py:21
  29.8 5.0 %collective-permute-start.7 = (bf16[512,128]{1,0:T(8,128)(2,1)S(1)}, bf16[512,128]{1,0:T(8,128)(2,1)S(1)}, u32[]{:S(2)}, u32[]{:S(2)}) collective-permute-start(bf16[512,128]{1,0:T(8,128)(2,1)S(1)} %add.18.refs_0_), channel_id=1, source_target_pairs={{0,4},{4,0},{8,12},{12,8},{16,20},{20,16},{24,28},{28,24},{1,5},{5... | collective-permute-start | bytes 393224 | tf_op jit(solution)/shard_map/ppermute | solution.py:21
  32.3 2.5 %copy-start.2 = (bf16[2,1,64,64]{3,2,1,0:T(8,128)(2,1)S(1)}, bf16[2,1,64,64]{3,2,1,0:T(8,128)(2,1)}, u32[]{:S(2)}) copy-start(bf16[2,1,64,64]{3,2,1,0:T(8,128)(2,1)} %inverses.1) | copy-start | bytes 49156
  36.3 3.6 %collective-permute-start.13 = (f32[1,128]{1,0:T(1,128)S(1)}, f32[1,128]{1,0:T(1,128)S(1)}, u32[]{:S(2)}, u32[]{:S(2)}) collective-permute-start(f32[1,128]{1,0:T(1,128)S(1)} %get-tuple-element.30), channel_id=1, source_target_pairs={{0,8},{4,12},{8,0},{12,4},{16,24},{20,28},{24,16},{28,20},{1,9},{5... | collective-permute-start | bytes 1544 | tf_op jit(solution)/shard_map/ppermute | solution.py:21
  39.9 4.4 %collective-permute-start.14 = (f32[1,128]{1,0:T(1,128)S(1)}, f32[1,128]{1,0:T(1,128)S(1)}, u32[]{:S(2)}, u32[]{:S(2)}) collective-permute-start(f32[1,128]{1,0:T(1,128)S(1)} %max.6), channel_id=1, source_target_pairs={{0,16},{4,20},{8,24},{12,28},{16,0},{20,4},{24,8},{28,12},{1,17},{... | collective-permute-start | bytes 1544 | tf_op jit(solution)/shard_map/ppermute | solution.py:21

commit v5 on v4

--- a/solution.py
+++ b/solution.py
@@ -45,42 +45,41 @@
     return jnp.concatenate(hot, 0)
 
 
-def fetch_kernel(n_sig, selected, own, mine, out):
+def fetch_kernel(n_sig, selected, own, mine, out, hot):
     mine[...] = own[...]
     out[...] = matmul(own[...], hot_rows(n_sig, [(0, 0)], selected)).astype(jnp.bfloat16)
+    hot[...] = hot_rows(n_sig, [(0, mask) for mask in range(1, n_sig)], selected)
 
 
 def fetch(n_sig, selected, own):
+    shapes = (own.shape, (own.shape[0], STEPS * BLK), ((n_sig - 1) * SB, STEPS * BLK))
     return pl.pallas_call(
         functools.partial(fetch_kernel, n_sig),
-        out_shape=(pltpu.VMEM(own.shape, jnp.bfloat16), pltpu.VMEM((own.shape[0], STEPS * BLK), jnp.bfloat16)),
+        out_shape=tuple(pltpu.VMEM(shape, jnp.bfloat16) for shape in shapes),
         in_specs=[SMEM, VMEM],
-        out_specs=(VMEM, VMEM),
+        out_specs=(VMEM,) * 3,
         name="fetch",
         compiler_params=PARAMS,
     )(selected, own)
 
 
-def pick_kernel(n_sig, selected, base, *refs):
-    pieces, outs = refs[: n_sig - 1], refs[n_sig - 1 :]
-    rows = jnp.concatenate([piece[...] for piece in pieces], 1)
-    total = matmul(rows, hot_rows(n_sig, [(0, mask) for mask in range(1, n_sig)], selected))
-    total = total.astype(jnp.bfloat16) + base[...]
-    at = 0
-    for out in outs:
-        out[...] = total[at : at + out.shape[0]]
-        at += out.shape[0]
-
-
-def pick(n_sig, selected, base, pieces, depths):
-    return pl.pallas_call(
-        functools.partial(pick_kernel, n_sig),
+def pick_kernel(starts, hot, base, *refs):
+    pieces, outs = refs[: -len(starts)], refs[-len(starts) :]
+    for at, out in zip(starts, outs):
+        rows = slice(at, at + out.shape[0])
+        total = matmul(jnp.concatenate([piece[rows] for piece in pieces], 1), hot[...])
+        out[...] = total.astype(jnp.bfloat16) + base[rows]
+
+
+def pick(hot, base, pieces, starts, depths):
+    return pl.pallas_call(
+        functools.partial(pick_kernel, starts),
         out_shape=tuple(pltpu.VMEM((depth, STEPS * BLK), jnp.bfloat16) for depth in depths),
-        in_specs=[SMEM] + [VMEM] * n_sig,
+        in_specs=[VMEM] * (2 + len(pieces)),
         out_specs=(VMEM,) * len(depths),
         name="pick",
         compiler_params=PARAMS,
-    )(selected, near(base), *[near(piece) for piece in pieces])
+    )(near(hot), near(base), *[near(piece) for piece in pieces])
 
 
 def ready_kernel(counts, signals, *refs):
@@ -186,10 +185,10 @@
             bit //= 2
         return [pieces[mask] for mask in range(n_sig)]
 
-    mine, base = fetch(n_sig, selected, dictionary)
+    mine, base, hot = fetch(n_sig, selected, dictionary)
     here = gather(dictionary, mine)
     beside = swap(dictionary, "atoms", n_atoms, twin)
-    first, second = pick(n_sig, selected, base, here[1:], [depth, depth])
+    first, second = pick(hot, base, here[1:], [0, depth], [depth, depth])
     there = gather(beside, beside)
     blocks = [first, second]
     orders = [[top] + bits[-2::-1], bits[-2::-1] + [top]]

time: 45 us -> 44.4 us (0.987)
  Pallas kernels: 4.12 us -> 3.52 us
    pallas_call x2, Pallas kernels: 1.73 us -> 1.12 us  [the longest x1 0.76 us: fetch(): pl.pallas_call(functools.partial(fetch_kernel, n_sig), out_shape=tuple((p...]
  transfers between devices with their start and end apart: 15 -> 15, of which waited for: 10 -> 10; matrix products, arithmetic and copies ran while one was open for 3% -> 3% of each run, Pallas kernels for 6% -> 5%
where the time goes in v5:
time: 44.4 us; the launch traced here: 44.3 us
  waiting for transfers between devices  21.2 us (48%)
  starting transfers between devices  15.9 us (36%)
  Pallas kernels  3.52 us (8%)
  local copies, waits for them, and re-layouts  2.27 us (5%)
  between operations  0.75 us (2%)
  other arithmetic  0.71 us (2%)
    ppermute x15, waiting for transfers between devices, swap(): return lax.ppermute(block, axis, [(i, i ^ mask) for i in range(size)])  21.2 us
    ppermute x15, starting transfers between devices, swap(): return lax.ppermute(block, axis, [(i, i ^ mask) for i in range(size)])  15.9 us
    unnamed x10, local copies, waits for them, and re-layouts  2.27 us
    pallas_call x1, Pallas kernels, finish(): pl.pallas_call(functools.partial(finish_kernel, n_sig, [len(term) for ter...  1.45 us
    pallas_call x2, Pallas kernels, ready(): pl.pallas_call(functools.partial(ready_kernel, [len(piece) for piece in p...  0.95 us
  transfers between devices with their start and end apart: 15, of which 10 were waited for; matrix products, arithmetic and copies ran while one was open for 3% of the time, Pallas kernels for 5%

profile of v5, /device:TPU:0, one launch (start us, length us, event | category | flops | bytes accessed | tf_op | source)
XLA Modules:
  0.0 44.3 jit_solution(7421951813859121423)
XLA Ops:
  0.6 0.0 copy-start.3
  0.6 3.0 %collective-permute-start.1 = (bf16[1024,128]{1,0:T(8,128)(2,1)}, bf16[1024,128]{1,0:T(8,128)(2,1)S(1)}, u32[]{:S(2)}, u32[]{:S(2)}) collective-permute-start(bf16[1024,128]{1,0:T(8,128)(2,1)} %own.1), channel_id=1, source_target_pairs={{0,2},{1,3},{2,0},{3,1},{4,6},{5,7},{6,4},{7,5},{8,10},{9,11},{10,... | collective-permute-start | bytes 786440 | tf_op jit(solution)/shard_map/ppermute | solution.py:21
  3.6 1.5 %collective-permute-start.9 = (bf16[1024,128]{1,0:T(8,128)(2,1)}, bf16[1024,128]{1,0:T(8,128)(2,1)S(1)}, u32[]{:S(2)}, u32[]{:S(2)}) collective-permute-start(bf16[1024,128]{1,0:T(8,128)(2,1)} %own.1), channel_id=1, source_target_pairs={{0,4},{4,0},{8,12},{12,8},{16,20},{20,16},{24,28},{28,24},{1,5},{5... | collective-permute-start | bytes 786440 | tf_op jit(solution)/shard_map/ppermute | solution.py:21
  5.2 0.0 copy-done.3
  5.2 0.0 copy-start.1
  5.2 1.0 %copy-done.1 = bf16[1024,128]{1,0:T(8,128)(2,1)S(1)} copy-done((bf16[1024,128]{1,0:T(8,128)(2,1)S(1)}, bf16[1024,128]{1,0:T(8,128)(2,1)}, u32[]{:S(2)}) %copy-start.1) | copy-done | bytes 262168
  6.1 0.8 %fetch.1 = (bf16[1024,128]{1,0:T(8,128)(2,1)S(1)}, bf16[1024,128]{1,0:T(8,128)(2,1)S(1)}, bf16[384,128]{1,0:T(8,128)(2,1)S(1)}) custom-call(s32[2]{0:T(128)S(1)} %bitcast.3, bf16[1024,128]{1,0:T(8,128)(2,1)S(1)} %copy-done.1), custom_call_target="tpu_custom_call" | custom-call | tf_op jit(solution)/shard_map/fetch/pallas_call | solution.py:56
  6.9 0.1 collective-permute-start
  7.0 3.2 %collective-permute-done.1.refs_1_.refs_2_ = bf16[1024,128]{1,0:T(8,128)(2,1)S(1)} collective-permute-done((bf16[1024,128]{1,0:T(8,128)(2,1)}, bf16[1024,128]{1,0:T(8,128)(2,1)S(1)}, u32[]{:S(2)}, u32[]{:S(2)}) %collective-permute-start.1) | collective-permute-done | bytes 262176 | tf_op jit(solution)/shard_map/ppermute | solution.py:21
  10.2 0.0 collective-permute-start.2
  10.2 1.5 %collective-permute-done.9.refs_0_ = bf16[1024,128]{1,0:T(8,128)(2,1)S(1)} collective-permute-done((bf16[1024,128]{1,0:T(8,128)(2,1)}, bf16[1024,128]{1,0:T(8,128)(2,1)S(1)}, u32[]{:S(2)}, u32[]{:S(2)}) %collective-permute-start.9) | collective-permute-done | bytes 262176 | tf_op jit(solution)/shard_map/ppermute | solution.py:21
  11.6 0.4 collective-permute-start.11
  12.0 0.0 collective-permute-done.refs_0_.refs_1_
  12.0 0.0 collective-permute-done.2.refs_2_.refs_3_
  12.0 0.4 pick.1
  12.4 1.8 %collective-permute-start.4 = (bf16[512,128]{1,0:T(8,128)(2,1)S(1)}, bf16[512,128]{1,0:T(8,128)(2,1)S(1)}, u32[]{:S(2)}, u32[]{:S(2)}) collective-permute-start(bf16[512,128]{1,0:T(8,128)(2,1)S(1)} %get-tuple-element.22), channel_id=1, source_target_pairs={{0,8},{4,12},{8,0},{12,4},{16,24},{20,28},{24,16},{28,20},{1,9},{5... | collective-permute-start | bytes 393224 | tf_op jit(solution)/shard_map/ppermute | solution.py:21
  14.2 2.6 %collective-permute-start.3 = (bf16[512,128]{1,0:T(8,128)(2,1)S(1)}, bf16[512,128]{1,0:T(8,128)(2,1)S(1)}, u32[]{:S(2)}, u32[]{:S(2)}) collective-permute-start(bf16[512,128]{1,0:T(8,128)(2,1)S(1)} %get-tuple-element.21), channel_id=1, source_target_pairs={{0,16},{4,20},{8,24},{12,28},{16,0},{20,4},{24,8},{28,12},{1,17},{... | collective-permute-start | bytes 393224 | tf_op jit(solution)/shard_map/ppermute | solution.py:21
  16.8 0.0 collective-permute-start.10
  16.8 3.4 %collective-permute-done.4 = bf16[512,128]{1,0:T(8,128)(2,1)S(1)} collective-permute-done((bf16[512,128]{1,0:T(8,128)(2,1)S(1)}, bf16[512,128]{1,0:T(8,128)(2,1)S(1)}, u32[]{:S(2)}, u32[]{:S(2)}) %collective-permute-start.4) | collective-permute-done | bytes 131104 | tf_op jit(solution)/shard_map/ppermute | solution.py:21
  20.2 1.6 %collective-permute-start.6 = (bf16[512,128]{1,0:T(8,128)(2,1)S(1)}, bf16[512,128]{1,0:T(8,128)(2,1)S(1)}, u32[]{:S(2)}, u32[]{:S(2)}) collective-permute-start(bf16[512,128]{1,0:T(8,128)(2,1)S(1)} %add.15), channel_id=1, source_target_pairs={{0,4},{4,0},{8,12},{12,8},{16,20},{20,16},{24,28},{28,24},{1,5},{5... | collective-permute-start | bytes 393224 | tf_op jit(solution)/shard_map/ppermute | solution.py:21
  21.8 1.3 %collective-permute-done.3 = bf16[512,128]{1,0:T(8,128)(2,1)S(1)} collective-permute-done((bf16[512,128]{1,0:T(8,128)(2,1)S(1)}, bf16[512,128]{1,0:T(8,128)(2,1)S(1)}, u32[]{:S(2)}, u32[]{:S(2)}) %collective-permute-start.3) | collective-permute-done | bytes 131104 | tf_op jit(solution)/shard_map/ppermute | solution.py:21
  23.1 0.5 %collective-permute-start.5 = (bf16[512,128]{1,0:T(8,128)(2,1)S(1)}, bf16[512,128]{1,0:T(8,128)(2,1)S(1)}, u32[]{:S(2)}, u32[]{:S(2)}) collective-permute-start(bf16[512,128]{1,0:T(8,128)(2,1)S(1)} %add.16), channel_id=1, source_target_pairs={{0,8},{4,12},{8,0},{12,4},{16,24},{20,28},{24,16},{28,20},{1,9},{5... | collective-permute-start | bytes 393224 | tf_op jit(solution)/shard_map/ppermute | solution.py:21
  23.6 0.0 collective-permute-done.11.refs_2_
  23.6 0.0 collective-permute-start.12
  23.6 1.7 %collective-permute-done.6 = bf16[512,128]{1,0:T(8,128)(2,1)S(1)} collective-permute-done((bf16[512,128]{1,0:T(8,128)(2,1)S(1)}, bf16[512,128]{1,0:T(8,128)(2,1)S(1)}, u32[]{:S(2)}, u32[]{:S(2)}) %collective-permute-start.6) | collective-permute-done | bytes 131104 | tf_op jit(solution)/shard_map/ppermute | solution.py:21
  25.3 0.0 copy-start
  25.3 1.4 %collective-permute-start.8 = (bf16[512,128]{1,0:T(8,128)(2,1)S(1)}, bf16[512,128]{1,0:T(8,128)(2,1)S(1)}, u32[]{:S(2)}, u32[]{:S(2)}) collective-permute-start(bf16[512,128]{1,0:T(8,128)(2,1)S(1)} %add.17), channel_id=1, source_target_pairs={{0,16},{4,20},{8,24},{12,28},{16,0},{20,4},{24,8},{28,12},{1,17},{... | collective-permute-start | bytes 393224 | tf_op jit(solution)/shard_map/ppermute | solution.py:21
  26.7 2.4 %collective-permute-done.5 = bf16[512,128]{1,0:T(8,128)(2,1)S(1)} collective-permute-done((bf16[512,128]{1,0:T(8,128)(2,1)S(1)}, bf16[512,128]{1,0:T(8,128)(2,1)S(1)}, u32[]{:S(2)}, u32[]{:S(2)}) %collective-permute-start.5) | collective-permute-done | bytes 131104 | tf_op jit(solution)/shard_map/ppermute | solution.py:21
  29.2 1.6 %collective-permute-start.7 = (bf16[512,128]{1,0:T(8,128)(2,1)S(1)}, bf16[512,128]{1,0:T(8,128)(2,1)S(1)}, u32[]{:S(2)}, u32[]{:S(2)}) collective-permute-start(bf16[512,128]{1,0:T(8,128)(2,1)S(1)} %add.18.refs_0_), channel_id=1, source_target_pairs={{0,4},{4,0},{8,12},{12,8},{16,20},{20,16},{24,28},{28,24},{1,5},{5... | collective-permute-start | bytes 393224 | tf_op jit(solution)/shard_map/ppermute | solution.py:21
  30.8 0.0 copy-done
  30.8 0.5 %ready.2 = (bf16[512,1024]{1,0:T(8,128)(2,1)S(1)}, f32[512,128]{1,0:T(8,128)S(1)}) custom-call(bf16[1024,128]{1,0:T(8,128)(2,1)S(1)} %copy-done, bf16[1024,128]{1,0:T(8,128)(2,1)S(1)} %get-tuple-element.20.refs_0_, bf16[1024,128]{1,0:T(8,128)(2,1)S(1)} %collective-permute-done.refs_0_.refs_1_, bf16[1024,128]{1,0:T(8,128)(2,1)S(1)} %collective-permute-done.1.refs_1_.refs_2_, ...), custom_call_target="tpu_custom_call" | custom-call | tf_op jit(solution)/shard_map/ready/pallas_call | solution.py:98
  31.3 0.0 collective-permute-done.10.refs_1_
  31.3 0.0 collective-permute-done.12.refs_3_
  31.3 0.5 %ready.3 = (bf16[512,1024]{1,0:T(8,128)(2,1)S(1)}, f32[512,128]{1,0:T(8,128)S(1)}) custom-call(bf16[1024,128]{1,0:T(8,128)(2,1)S(1)} %copy-done, bf16[1024,128]{1,0:T(8,128)(2,1)S(1)} %collective-permute-done.9.refs_0_, bf16[1024,128]{1,0:T(8,128)(2,1)S(1)} %collective-permute-done.10.refs_1_, bf16[1024,128]{1,0:T(8,128)(2,1)S(1)} %collective-permute-done.11.refs_2_, ...), custom_call_target="tpu_custom_call" | custom-call | tf_op jit(solution)/shard_map/ready/pallas_call | solution.py:98
  31.8 0.0 copy-start.2
  31.8 1.6 %collective-permute-done.8 = bf16[512,128]{1,0:T(8,128)(2,1)S(1)} collective-permute-done((bf16[512,128]{1,0:T(8,128)(2,1)S(1)}, bf16[512,128]{1,0:T(8,128)(2,1)S(1)}, u32[]{:S(2)}, u32[]{:S(2)}) %collective-permute-start.8) | collective-permute-done | bytes 131104 | tf_op jit(solution)/shard_map/ppermute | solution.py:21
  33.4 0.8 %collective-permute-done.7.refs_1_ = bf16[512,128]{1,0:T(8,128)(2,1)S(1)} collective-permute-done((bf16[512,128]{1,0:T(8,128)(2,1)S(1)}, bf16[512,128]{1,0:T(8,128)(2,1)S(1)}, u32[]{:S(2)}, u32[]{:S(2)}) %collective-permute-start.7) | collective-permute-done | bytes 131104 | tf_op jit(solution)/shard_map/ppermute | solution.py:21
  34.2 0.0 copy-done.2
  34.3 1.4 %finish.1 = (bf16[512,128]{1,0:T(8,128)(2,1)S(1)}, bf16[2,64,128]{2,1,0:T(8,128)(2,1)S(1)}, f32[1,128]{1,0:T(1,128)S(1)}) custom-call(bf16[2,1,64,64]{3,2,1,0:T(8,128)(2,1)S(1)} %copy-done.2, bf16[1024,128]{1,0:T(8,128)(2,1)S(1)} %copy-done, bf16[512,128]{1,0:T(8,128)(2,1)S(1)} %add.18.refs_0_, bf16[512,128]{1,0:T(8,128)(2,1)S(1)} %collective-permute-done.7.refs_1_, ...), custom_call_target="tpu_custom_call" | custom-call | tf_op jit(solution)/shard_map/finish/pallas_call | solution.py:154
  35.7 0.1 collective-permute-start.13
  35.8 3.5 %collective-permute-done.13 = f32[1,128]{1,0:T(1,128)S(1)} collective-permute-done((f32[1,128]{1,0:T(1,128)S(1)}, f32[1,128]{1,0:T(1,128)S(1)}, u32[]{:S(2)}, u32[]{:S(2)}) %collective-permute-start.13) | collective-permute-done | bytes 544 | tf_op jit(solution)/shard_map/ppermute | solution.py:21
  39.3 1.3 %collective-permute-start.14 = (f32[1,128]{1,0:T(1,128)S(1)}, f32[1,128]{1,0:T(1,128)S(1)}, u32[]{:S(2)}, u32[]{:S(2)}) collective-permute-start(f32[1,128]{1,0:T(1,128)S(1)} %max.6), channel_id=1, source_target_pairs={{0,16},{4,20},{8,24},{12,28},{16,0},{20,4},{24,8},{28,12},{1,17},{... | collective-permute-start | bytes 1544 | tf_op jit(solution)/shard_map/ppermute | solution.py:21
  40.7 0.7 %copy.7 = bf16[512,128]{1,0:T(8,128)(2,1)} copy(bf16[512,128]{1,0:T(8,128)(2,1)S(1)} %get-tuple-element.33) | data formatting | bytes 262144
  41.3 0.6 %copy.8 = bf16[2,64,128]{2,1,0:T(8,128)(2,1)} copy(bf16[2,64,128]{2,1,0:T(8,128)(2,1)S(1)} %get-tuple-element.34) | data formatting | bytes 65536
  41.9 1.8 %collective-permute-done.14 = f32[1,128]{1,0:T(1,128)S(1)} collective-permute-done((f32[1,128]{1,0:T(1,128)S(1)}, f32[1,128]{1,0:T(1,128)S(1)}, u32[]{:S(2)}, u32[]{:S(2)}) %collective-permute-start.14) | collective-permute-done | bytes 544 | tf_op jit(solution)/shard_map/ppermute | solution.py:21
  43.8 0.5 %maximum_bitcast_fusion = f32[128]{0:T(128)} fusion(f32[1,128]{1,0:T(1,128)S(1)} %max.6, f32[1,128]{1,0:T(1,128)S(1)} %collective-permute-done.14), kind=kLoop, calls=%fused_computation | loop fusion | flops 128 | bytes 1536 | tf_op jit(solution)/shard_map/squeeze | solution.py:206
  (6 shorter events, 0.2 us)
Async XLA Ops:
  0.6 4.5 %copy-start.3 = (s32[2,1]{0,1:T(1,128)S(1)}, s32[2,1]{0,1:T(1,128)}, u32[]{:S(2)}) copy-start(s32[2,1]{0,1:T(1,128)} %param.6) | copy-start | bytes 28
  0.6 9.5 %collective-permute-start.1 = (bf16[1024,128]{1,0:T(8,128)(2,1)}, bf16[1024,128]{1,0:T(8,128)(2,1)S(1)}, u32[]{:S(2)}, u32[]{:S(2)}) collective-permute-start(bf16[1024,128]{1,0:T(8,128)(2,1)} %own.1), channel_id=1, source_target_pairs={{0,2},{1,3},{2,0},{3,1},{4,6},{5,7},{6,4},{7,5},{8,10},{9,11},{10,... | collective-permute-start | bytes 786440 | tf_op jit(solution)/shard_map/ppermute | solution.py:21
  3.6 8.0 %collective-permute-start.9 = (bf16[1024,128]{1,0:T(8,128)(2,1)}, bf16[1024,128]{1,0:T(8,128)(2,1)S(1)}, u32[]{:S(2)}, u32[]{:S(2)}) collective-permute-start(bf16[1024,128]{1,0:T(8,128)(2,1)} %own.1), channel_id=1, source_target_pairs={{0,4},{4,0},{8,12},{12,8},{16,20},{20,16},{24,28},{28,24},{1,5},{5... | collective-permute-start | bytes 786440 | tf_op jit(solution)/shard_map/ppermute | solution.py:21
  5.2 1.0 %copy-start.1 = (bf16[1024,128]{1,0:T(8,128)(2,1)S(1)}, bf16[1024,128]{1,0:T(8,128)(2,1)}, u32[]{:S(2)}) copy-start(bf16[1024,128]{1,0:T(8,128)(2,1)} %own.1) | copy-start | bytes 786436
  6.9 5.1 %collective-permute-start = (bf16[1024,128]{1,0:T(8,128)(2,1)S(1)}, bf16[1024,128]{1,0:T(8,128)(2,1)S(1)}, u32[]{:S(2)}, u32[]{:S(2)}) collective-permute-start(bf16[1024,128]{1,0:T(8,128)(2,1)S(1)} %get-tuple-element.20.refs_0_), channel_id=1, source_target_pairs={{0,1},{1,0},{2,3},{3,2},{4,5},{5,4},{6,7},{7,6},{8,9},{9,8},{10,11... | collective-permute-start | bytes 786440 | tf_op jit(solution)/shard_map/ppermute | solution.py:21
  10.2 1.8 %collective-permute-start.2 = (bf16[1024,128]{1,0:T(8,128)(2,1)S(1)}, bf16[1024,128]{1,0:T(8,128)(2,1)S(1)}, u32[]{:S(2)}, u32[]{:S(2)}) collective-permute-start(bf16[1024,128]{1,0:T(8,128)(2,1)S(1)} %collective-permute-done.1.refs_1_.refs_2_), channel_id=1, source_target_pairs={{0,1},{1,0},{2,3},{3,2},{4,5},{5,4},{6,7},{7,6},{8,9},{9,8},{10,11... | collective-permute-start | bytes 786440 | tf_op jit(solution)/shard_map/ppermute | solution.py:21
  11.6 12.0 %collective-permute-start.11 = (bf16[1024,128]{1,0:T(8,128)(2,1)S(1)}, bf16[1024,128]{1,0:T(8,128)(2,1)S(1)}, u32[]{:S(2)}, u32[]{:S(2)}) collective-permute-start(bf16[1024,128]{1,0:T(8,128)(2,1)S(1)} %collective-permute-done.9.refs_0_), channel_id=1, source_target_pairs={{0,2},{1,3},{2,0},{3,1},{4,6},{5,7},{6,4},{7,5},{8,10},{9,11},{10,... | collective-permute-start | bytes 786440 | tf_op jit(solution)/shard_map/ppermute | solution.py:21
  12.4 7.8 %collective-permute-start.4 = (bf16[512,128]{1,0:T(8,128)(2,1)S(1)}, bf16[512,128]{1,0:T(8,128)(2,1)S(1)}, u32[]{:S(2)}, u32[]{:S(2)}) collective-permute-start(bf16[512,128]{1,0:T(8,128)(2,1)S(1)} %get-tuple-element.22), channel_id=1, source_target_pairs={{0,8},{4,12},{8,0},{12,4},{16,24},{20,28},{24,16},{28,20},{1,9},{5... | collective-permute-start | bytes 393224 | tf_op jit(solution)/shard_map/ppermute | solution.py:21
  14.2 8.9 %collective-permute-start.3 = (bf16[512,128]{1,0:T(8,128)(2,1)S(1)}, bf16[512,128]{1,0:T(8,128)(2,1)S(1)}, u32[]{:S(2)}, u32[]{:S(2)}) collective-permute-start(bf16[512,128]{1,0:T(8,128)(2,1)S(1)} %get-tuple-element.21), channel_id=1, source_target_pairs={{0,16},{4,20},{8,24},{12,28},{16,0},{20,4},{24,8},{28,12},{1,17},{... | collective-permute-start | bytes 393224 | tf_op jit(solution)/shard_map/ppermute | solution.py:21
  16.8 14.5 %collective-permute-start.10 = (bf16[1024,128]{1,0:T(8,128)(2,1)S(1)}, bf16[1024,128]{1,0:T(8,128)(2,1)S(1)}, u32[]{:S(2)}, u32[]{:S(2)}) collective-permute-start(bf16[1024,128]{1,0:T(8,128)(2,1)S(1)} %collective-permute-done.9.refs_0_), channel_id=1, source_target_pairs={{0,1},{1,0},{2,3},{3,2},{4,5},{5,4},{6,7},{7,6},{8,9},{9,8},{10,11... | collective-permute-start | bytes 786440 | tf_op jit(solution)/shard_map/ppermute | solution.py:21
  20.2 5.0 %collective-permute-start.6 = (bf16[512,128]{1,0:T(8,128)(2,1)S(1)}, bf16[512,128]{1,0:T(8,128)(2,1)S(1)}, u32[]{:S(2)}, u32[]{:S(2)}) collective-permute-start(bf16[512,128]{1,0:T(8,128)(2,1)S(1)} %add.15), channel_id=1, source_target_pairs={{0,4},{4,0},{8,12},{12,8},{16,20},{20,16},{24,28},{28,24},{1,5},{5... | collective-permute-start | bytes 393224 | tf_op jit(solution)/shard_map/ppermute | solution.py:21
  23.1 6.1 %collective-permute-start.5 = (bf16[512,128]{1,0:T(8,128)(2,1)S(1)}, bf16[512,128]{1,0:T(8,128)(2,1)S(1)}, u32[]{:S(2)}, u32[]{:S(2)}) collective-permute-start(bf16[512,128]{1,0:T(8,128)(2,1)S(1)} %add.16), channel_id=1, source_target_pairs={{0,8},{4,12},{8,0},{12,4},{16,24},{20,28},{24,16},{28,20},{1,9},{5... | collective-permute-start | bytes 393224 | tf_op jit(solution)/shard_map/ppermute | solution.py:21
  23.6 7.7 %collective-permute-start.12 = (bf16[1024,128]{1,0:T(8,128)(2,1)S(1)}, bf16[1024,128]{1,0:T(8,128)(2,1)S(1)}, u32[]{:S(2)}, u32[]{:S(2)}) collective-permute-start(bf16[1024,128]{1,0:T(8,128)(2,1)S(1)} %collective-permute-done.11.refs_2_), channel_id=1, source_target_pairs={{0,1},{1,0},{2,3},{3,2},{4,5},{5,4},{6,7},{7,6},{8,9},{9,8},{10,11... | collective-permute-start | bytes 786440 | tf_op jit(solution)/shard_map/ppermute | solution.py:21
  25.3 5.5 %copy-start = (bf16[1024,128]{1,0:T(8,128)(2,1)S(1)}, bf16[1024,128]{1,0:T(8,128)(2,1)}, u32[]{:S(2)}) copy-start(bf16[1024,128]{1,0:T(8,128)(2,1)} %signals.5) | copy-start | bytes 786436
  25.3 8.1 %collective-permute-start.8 = (bf16[512,128]{1,0:T(8,128)(2,1)S(1)}, bf16[512,128]{1,0:T(8,128)(2,1)S(1)}, u32[]{:S(2)}, u32[]{:S(2)}) collective-permute-start(bf16[512,128]{1,0:T(8,128)(2,1)S(1)} %add.17), channel_id=1, source_target_pairs={{0,16},{4,20},{8,24},{12,28},{16,0},{20,4},{24,8},{28,12},{1,17},{... | collective-permute-start | bytes 393224 | tf_op jit(solution)/shard_map/ppermute | solution.py:21
  29.2 5.0 %collective-permute-start.7 = (bf16[512,128]{1,0:T(8,128)(2,1)S(1)}, bf16[512,128]{1,0:T(8,128)(2,1)S(1)}, u32[]{:S(2)}, u32[]{:S(2)}) collective-permute-start(bf16[512,128]{1,0:T(8,128)(2,1)S(1)} %add.18.refs_0_), channel_id=1, source_target_pairs={{0,4},{4,0},{8,12},{12,8},{16,20},{20,16},{24,28},{28,24},{1,5},{5... | collective-permute-start | bytes 393224 | tf_op jit(solution)/shard_map/ppermute | solution.py:21
  31.8 2.5 %copy-start.2 = (bf16[2,1,64,64]{3,2,1,0:T(8,128)(2,1)S(1)}, bf16[2,1,64,64]{3,2,1,0:T(8,128)(2,1)}, u32[]{:S(2)}) copy-start(bf16[2,1,64,64]{3,2,1,0:T(8,128)(2,1)} %inverses.1) | copy-start | bytes 49156
  35.7 3.6 %collective-permute-start.13 = (f32[1,128]{1,0:T(1,128)S(1)}, f32[1,128]{1,0:T(1,128)S(1)}, u32[]{:S(2)}, u32[]{:S(2)}) collective-permute-start(f32[1,128]{1,0:T(1,128)S(1)} %get-tuple-element.32), channel_id=1, source_target_pairs={{0,8},{4,12},{8,0},{12,4},{16,24},{20,28},{24,16},{28,20},{1,9},{5... | collective-permute-start | bytes 1544 | tf_op jit(solution)/shard_map/ppermute | solution.py:21
  39.3 4.4 %collective-permute-start.14 = (f32[1,128]{1,0:T(1,128)S(1)}, f32[1,128]{1,0:T(1,128)S(1)}, u32[]{:S(2)}, u32[]{:S(2)}) collective-permute-start(f32[1,128]{1,0:T(1,128)S(1)} %max.6), channel_id=1, source_target_pairs={{0,16},{4,20},{8,24},{12,28},{16,0},{20,4},{24,8},{28,12},{1,17},{... | collective-permute-start | bytes 1544 | tf_op jit(solution)/shard_map/ppermute | solution.py:21

commit v6 on v5

--- a/solution.py
+++ b/solution.py
@@ -128,10 +128,12 @@
         at += count
     sides = refs[at:-3]
     chosen = jnp.concatenate(halves, 0)
-    panels = [matmul(turned[...], chosen).astype(jnp.bfloat16) for turned in sides[::2]]
     right = matmul(chosen.T, jnp.concatenate([signals[...], chosen], 1))
     rows, gram = right[:, :SB], right[:, SB:].astype(jnp.bfloat16)
+    panels = []
+    panels.append(matmul(sides[0][...], chosen).astype(jnp.bfloat16))
     one = exact(inverses[0, 0], rows[:BLK]).astype(jnp.bfloat16)
+    panels.append(matmul(sides[2][...], chosen).astype(jnp.bfloat16))
     two = exact(inverses[1, 0], rows[BLK:] - matmul(gram[BLK:, :BLK], one)).astype(jnp.bfloat16)
     coef_out[0] = one
     coef_out[1] = two
@@ -200,7 +202,7 @@
             arrived[h] = swap(blocks[h], "atoms", n_atoms, orders[h][i])
     sides = [ready(signals, [[piece] for piece in pieces]) for pieces in (here, there)]
     correlations, coefficients, peak = finish(n_sig, inverses, signals, [(blocks[0], arrived[0]), (blocks[1] + arrived[1],)], sides)
-    for bit in bits:
+    for bit in reversed(bits):
         if bit != twin:
             peak = jnp.maximum(peak, swap(peak, "atoms", n_atoms, bit))
     return correlations, coefficients, peak[0]

time: 44.4 us -> 44.1 us (level)
  no operation moved by 1% of the time
where the time goes in v6:
time: 44.1 us; the launch traced here: 44 us
  waiting for transfers between devices  21.2 us (48%)
  starting transfers between devices  15.8 us (36%)
  Pallas kernels  3.25 us (7%)
  local copies, waits for them, and re-layouts  2.27 us (5%)
  between operations  0.74 us (2%)
  other arithmetic  0.71 us (2%)
    ppermute x15, waiting for transfers between devices, swap(): return lax.ppermute(block, axis, [(i, i ^ mask) for i in range(size)])  21.2 us
    ppermute x15, starting transfers between devices, swap(): return lax.ppermute(block, axis, [(i, i ^ mask) for i in range(size)])  15.8 us
    unnamed x10, local copies, waits for them, and re-layouts  2.27 us
    pallas_call x1, Pallas kernels, finish(): pl.pallas_call(functools.partial(finish_kernel, n_sig, [len(term) for ter...  1.17 us
    pallas_call x2, Pallas kernels, ready(): pl.pallas_call(functools.partial(ready_kernel, [len(piece) for piece in p...  0.95 us
  transfers between devices with their start and end apart: 15, of which 10 were waited for; matrix products, arithmetic and copies ran while one was open for 3% of the time, Pallas kernels for 5%

profile of v6, /device:TPU:0, one launch (start us, length us, event | category | flops | bytes accessed | tf_op | source)
XLA Modules:
  0.0 44.0 jit_solution(9901645860938171675)
XLA Ops:
  0.6 0.0 copy-start.3
  0.6 3.0 %collective-permute-start.1 = (bf16[1024,128]{1,0:T(8,128)(2,1)}, bf16[1024,128]{1,0:T(8,128)(2,1)S(1)}, u32[]{:S(2)}, u32[]{:S(2)}) collective-permute-start(bf16[1024,128]{1,0:T(8,128)(2,1)} %own.1), channel_id=1, source_target_pairs={{0,2},{1,3},{2,0},{3,1},{4,6},{5,7},{6,4},{7,5},{8,10},{9,11},{10,... | collective-permute-start | bytes 786440 | tf_op jit(solution)/shard_map/ppermute | solution.py:21
  3.6 1.5 %collective-permute-start.9 = (bf16[1024,128]{1,0:T(8,128)(2,1)}, bf16[1024,128]{1,0:T(8,128)(2,1)S(1)}, u32[]{:S(2)}, u32[]{:S(2)}) collective-permute-start(bf16[1024,128]{1,0:T(8,128)(2,1)} %own.1), channel_id=1, source_target_pairs={{0,4},{4,0},{8,12},{12,8},{16,20},{20,16},{24,28},{28,24},{1,5},{5... | collective-permute-start | bytes 786440 | tf_op jit(solution)/shard_map/ppermute | solution.py:21
  5.2 0.0 copy-done.3
  5.2 0.0 copy-start.1
  5.2 1.0 %copy-done.1 = bf16[1024,128]{1,0:T(8,128)(2,1)S(1)} copy-done((bf16[1024,128]{1,0:T(8,128)(2,1)S(1)}, bf16[1024,128]{1,0:T(8,128)(2,1)}, u32[]{:S(2)}) %copy-start.1) | copy-done | bytes 262168
  6.1 0.8 %fetch.1 = (bf16[1024,128]{1,0:T(8,128)(2,1)S(1)}, bf16[1024,128]{1,0:T(8,128)(2,1)S(1)}, bf16[384,128]{1,0:T(8,128)(2,1)S(1)}) custom-call(s32[2]{0:T(128)S(1)} %bitcast.3, bf16[1024,128]{1,0:T(8,128)(2,1)S(1)} %copy-done.1), custom_call_target="tpu_custom_call" | custom-call | tf_op jit(solution)/shard_map/fetch/pallas_call | solution.py:56
  6.9 0.1 collective-permute-start
  7.0 3.2 %collective-permute-done.1.refs_1_.refs_2_ = bf16[1024,128]{1,0:T(8,128)(2,1)S(1)} collective-permute-done((bf16[1024,128]{1,0:T(8,128)(2,1)}, bf16[1024,128]{1,0:T(8,128)(2,1)S(1)}, u32[]{:S(2)}, u32[]{:S(2)}) %collective-permute-start.1) | collective-permute-done | bytes 262176 | tf_op jit(solution)/shard_map/ppermute | solution.py:21
  10.2 0.0 collective-permute-start.2
  10.2 1.5 %collective-permute-done.9.refs_0_ = bf16[1024,128]{1,0:T(8,128)(2,1)S(1)} collective-permute-done((bf16[1024,128]{1,0:T(8,128)(2,1)}, bf16[1024,128]{1,0:T(8,128)(2,1)S(1)}, u32[]{:S(2)}, u32[]{:S(2)}) %collective-permute-start.9) | collective-permute-done | bytes 262176 | tf_op jit(solution)/shard_map/ppermute | solution.py:21
  11.6 0.4 collective-permute-start.11
  12.0 0.0 collective-permute-done.refs_0_.refs_1_
  12.0 0.0 collective-permute-done.2.refs_2_.refs_3_
  12.0 0.4 pick.1
  12.4 1.8 %collective-permute-start.4 = (bf16[512,128]{1,0:T(8,128)(2,1)S(1)}, bf16[512,128]{1,0:T(8,128)(2,1)S(1)}, u32[]{:S(2)}, u32[]{:S(2)}) collective-permute-start(bf16[512,128]{1,0:T(8,128)(2,1)S(1)} %get-tuple-element.22), channel_id=1, source_target_pairs={{0,8},{4,12},{8,0},{12,4},{16,24},{20,28},{24,16},{28,20},{1,9},{5... | collective-permute-start | bytes 393224 | tf_op jit(solution)/shard_map/ppermute | solution.py:21
  14.2 2.6 %collective-permute-start.3 = (bf16[512,128]{1,0:T(8,128)(2,1)S(1)}, bf16[512,128]{1,0:T(8,128)(2,1)S(1)}, u32[]{:S(2)}, u32[]{:S(2)}) collective-permute-start(bf16[512,128]{1,0:T(8,128)(2,1)S(1)} %get-tuple-element.21), channel_id=1, source_target_pairs={{0,16},{4,20},{8,24},{12,28},{16,0},{20,4},{24,8},{28,12},{1,17},{... | collective-permute-start | bytes 393224 | tf_op jit(solution)/shard_map/ppermute | solution.py:21
  16.8 0.0 collective-permute-start.10
  16.8 3.4 %collective-permute-done.4 = bf16[512,128]{1,0:T(8,128)(2,1)S(1)} collective-permute-done((bf16[512,128]{1,0:T(8,128)(2,1)S(1)}, bf16[512,128]{1,0:T(8,128)(2,1)S(1)}, u32[]{:S(2)}, u32[]{:S(2)}) %collective-permute-start.4) | collective-permute-done | bytes 131104 | tf_op jit(solution)/shard_map/ppermute | solution.py:21
  20.2 1.6 %collective-permute-start.6 = (bf16[512,128]{1,0:T(8,128)(2,1)S(1)}, bf16[512,128]{1,0:T(8,128)(2,1)S(1)}, u32[]{:S(2)}, u32[]{:S(2)}) collective-permute-start(bf16[512,128]{1,0:T(8,128)(2,1)S(1)} %add.15), channel_id=1, source_target_pairs={{0,4},{4,0},{8,12},{12,8},{16,20},{20,16},{24,28},{28,24},{1,5},{5... | collective-permute-start | bytes 393224 | tf_op jit(solution)/shard_map/ppermute | solution.py:21
  21.8 1.3 %collective-permute-done.3 = bf16[512,128]{1,0:T(8,128)(2,1)S(1)} collective-permute-done((bf16[512,128]{1,0:T(8,128)(2,1)S(1)}, bf16[512,128]{1,0:T(8,128)(2,1)S(1)}, u32[]{:S(2)}, u32[]{:S(2)}) %collective-permute-start.3) | collective-permute-done | bytes 131104 | tf_op jit(solution)/shard_map/ppermute | solution.py:21
  23.1 0.5 %collective-permute-start.5 = (bf16[512,128]{1,0:T(8,128)(2,1)S(1)}, bf16[512,128]{1,0:T(8,128)(2,1)S(1)}, u32[]{:S(2)}, u32[]{:S(2)}) collective-permute-start(bf16[512,128]{1,0:T(8,128)(2,1)S(1)} %add.16), channel_id=1, source_target_pairs={{0,8},{4,12},{8,0},{12,4},{16,24},{20,28},{24,16},{28,20},{1,9},{5... | collective-permute-start | bytes 393224 | tf_op jit(solution)/shard_map/ppermute | solution.py:21
  23.6 0.0 collective-permute-done.11.refs_2_
  23.6 0.0 collective-permute-start.12
  23.6 1.7 %collective-permute-done.6 = bf16[512,128]{1,0:T(8,128)(2,1)S(1)} collective-permute-done((bf16[512,128]{1,0:T(8,128)(2,1)S(1)}, bf16[512,128]{1,0:T(8,128)(2,1)S(1)}, u32[]{:S(2)}, u32[]{:S(2)}) %collective-permute-start.6) | collective-permute-done | bytes 131104 | tf_op jit(solution)/shard_map/ppermute | solution.py:21
  25.3 0.0 copy-start
  25.3 1.4 %collective-permute-start.8 = (bf16[512,128]{1,0:T(8,128)(2,1)S(1)}, bf16[512,128]{1,0:T(8,128)(2,1)S(1)}, u32[]{:S(2)}, u32[]{:S(2)}) collective-permute-start(bf16[512,128]{1,0:T(8,128)(2,1)S(1)} %add.17), channel_id=1, source_target_pairs={{0,16},{4,20},{8,24},{12,28},{16,0},{20,4},{24,8},{28,12},{1,17},{... | collective-permute-start | bytes 393224 | tf_op jit(solution)/shard_map/ppermute | solution.py:21
  26.7 2.4 %collective-permute-done.5 = bf16[512,128]{1,0:T(8,128)(2,1)S(1)} collective-permute-done((bf16[512,128]{1,0:T(8,128)(2,1)S(1)}, bf16[512,128]{1,0:T(8,128)(2,1)S(1)}, u32[]{:S(2)}, u32[]{:S(2)}) %collective-permute-start.5) | collective-permute-done | bytes 131104 | tf_op jit(solution)/shard_map/ppermute | solution.py:21
  29.2 1.6 %collective-permute-start.7 = (bf16[512,128]{1,0:T(8,128)(2,1)S(1)}, bf16[512,128]{1,0:T(8,128)(2,1)S(1)}, u32[]{:S(2)}, u32[]{:S(2)}) collective-permute-start(bf16[512,128]{1,0:T(8,128)(2,1)S(1)} %add.18.refs_0_), channel_id=1, source_target_pairs={{0,4},{4,0},{8,12},{12,8},{16,20},{20,16},{24,28},{28,24},{1,5},{5... | collective-permute-start | bytes 393224 | tf_op jit(solution)/shard_map/ppermute | solution.py:21
  30.8 0.0 copy-done
  30.8 0.5 %ready.2 = (bf16[512,1024]{1,0:T(8,128)(2,1)S(1)}, f32[512,128]{1,0:T(8,128)S(1)}) custom-call(bf16[1024,128]{1,0:T(8,128)(2,1)S(1)} %copy-done, bf16[1024,128]{1,0:T(8,128)(2,1)S(1)} %get-tuple-element.20.refs_0_, bf16[1024,128]{1,0:T(8,128)(2,1)S(1)} %collective-permute-done.refs_0_.refs_1_, bf16[1024,128]{1,0:T(8,128)(2,1)S(1)} %collective-permute-done.1.refs_1_.refs_2_, ...), custom_call_target="tpu_custom_call" | custom-call | tf_op jit(solution)/shard_map/ready/pallas_call | solution.py:98
  31.3 0.0 collective-permute-done.10.refs_1_
  31.3 0.0 collective-permute-done.12.refs_3_
  31.3 0.5 %ready.3 = (bf16[512,1024]{1,0:T(8,128)(2,1)S(1)}, f32[512,128]{1,0:T(8,128)S(1)}) custom-call(bf16[1024,128]{1,0:T(8,128)(2,1)S(1)} %copy-done, bf16[1024,128]{1,0:T(8,128)(2,1)S(1)} %collective-permute-done.9.refs_0_, bf16[1024,128]{1,0:T(8,128)(2,1)S(1)} %collective-permute-done.10.refs_1_, bf16[1024,128]{1,0:T(8,128)(2,1)S(1)} %collective-permute-done.11.refs_2_, ...), custom_call_target="tpu_custom_call" | custom-call | tf_op jit(solution)/shard_map/ready/pallas_call | solution.py:98
  31.8 0.0 copy-start.2
  31.8 1.6 %collective-permute-done.8 = bf16[512,128]{1,0:T(8,128)(2,1)S(1)} collective-permute-done((bf16[512,128]{1,0:T(8,128)(2,1)S(1)}, bf16[512,128]{1,0:T(8,128)(2,1)S(1)}, u32[]{:S(2)}, u32[]{:S(2)}) %collective-permute-start.8) | collective-permute-done | bytes 131104 | tf_op jit(solution)/shard_map/ppermute | solution.py:21
  33.4 0.8 %collective-permute-done.7.refs_1_ = bf16[512,128]{1,0:T(8,128)(2,1)S(1)} collective-permute-done((bf16[512,128]{1,0:T(8,128)(2,1)S(1)}, bf16[512,128]{1,0:T(8,128)(2,1)S(1)}, u32[]{:S(2)}, u32[]{:S(2)}) %collective-permute-start.7) | collective-permute-done | bytes 131104 | tf_op jit(solution)/shard_map/ppermute | solution.py:21
  34.2 0.0 copy-done.2
  34.3 1.2 %finish.1 = (bf16[512,128]{1,0:T(8,128)(2,1)S(1)}, bf16[2,64,128]{2,1,0:T(8,128)(2,1)S(1)}, f32[1,128]{1,0:T(1,128)S(1)}) custom-call(bf16[2,1,64,64]{3,2,1,0:T(8,128)(2,1)S(1)} %copy-done.2, bf16[1024,128]{1,0:T(8,128)(2,1)S(1)} %copy-done, bf16[512,128]{1,0:T(8,128)(2,1)S(1)} %add.18.refs_0_, bf16[512,128]{1,0:T(8,128)(2,1)S(1)} %collective-permute-done.7.refs_1_, ...), custom_call_target="tpu_custom_call" | custom-call | tf_op jit(solution)/shard_map/finish/pallas_call | solution.py:156
  35.4 1.0 %collective-permute-start.13 = (f32[1,128]{1,0:T(1,128)S(1)}, f32[1,128]{1,0:T(1,128)S(1)}, u32[]{:S(2)}, u32[]{:S(2)}) collective-permute-start(f32[1,128]{1,0:T(1,128)S(1)} %get-tuple-element.32), channel_id=1, source_target_pairs={{0,16},{4,20},{8,24},{12,28},{16,0},{20,4},{24,8},{28,12},{1,17},{... | collective-permute-start | bytes 1544 | tf_op jit(solution)/shard_map/ppermute | solution.py:21
  36.4 3.5 %collective-permute-done.13 = f32[1,128]{1,0:T(1,128)S(1)} collective-permute-done((f32[1,128]{1,0:T(1,128)S(1)}, f32[1,128]{1,0:T(1,128)S(1)}, u32[]{:S(2)}, u32[]{:S(2)}) %collective-permute-start.13) | collective-permute-done | bytes 544 | tf_op jit(solution)/shard_map/ppermute | solution.py:21
  39.9 0.4 %collective-permute-start.14 = (f32[1,128]{1,0:T(1,128)S(1)}, f32[1,128]{1,0:T(1,128)S(1)}, u32[]{:S(2)}, u32[]{:S(2)}) collective-permute-start(f32[1,128]{1,0:T(1,128)S(1)} %max.6), channel_id=1, source_target_pairs={{0,8},{4,12},{8,0},{12,4},{16,24},{20,28},{24,16},{28,20},{1,9},{5... | collective-permute-start | bytes 1544 | tf_op jit(solution)/shard_map/ppermute | solution.py:21
  40.4 0.7 %copy.7 = bf16[512,128]{1,0:T(8,128)(2,1)} copy(bf16[512,128]{1,0:T(8,128)(2,1)S(1)} %get-tuple-element.33) | data formatting | bytes 262144
  41.0 0.6 %copy.8 = bf16[2,64,128]{2,1,0:T(8,128)(2,1)} copy(bf16[2,64,128]{2,1,0:T(8,128)(2,1)S(1)} %get-tuple-element.34) | data formatting | bytes 65536
  41.7 1.8 %collective-permute-done.14 = f32[1,128]{1,0:T(1,128)S(1)} collective-permute-done((f32[1,128]{1,0:T(1,128)S(1)}, f32[1,128]{1,0:T(1,128)S(1)}, u32[]{:S(2)}, u32[]{:S(2)}) %collective-permute-start.14) | collective-permute-done | bytes 544 | tf_op jit(solution)/shard_map/ppermute | solution.py:21
  43.5 0.5 %maximum_bitcast_fusion = f32[128]{0:T(128)} fusion(f32[1,128]{1,0:T(1,128)S(1)} %max.6, f32[1,128]{1,0:T(1,128)S(1)} %collective-permute-done.14), kind=kLoop, calls=%fused_computation | loop fusion | flops 128 | bytes 1536 | tf_op jit(solution)/shard_map/squeeze | solution.py:208
  (6 shorter events, 0.2 us)
Async XLA Ops:
  0.6 4.5 %copy-start.3 = (s32[2,1]{0,1:T(1,128)S(1)}, s32[2,1]{0,1:T(1,128)}, u32[]{:S(2)}) copy-start(s32[2,1]{0,1:T(1,128)} %param.6) | copy-start | bytes 28
  0.6 9.5 %collective-permute-start.1 = (bf16[1024,128]{1,0:T(8,128)(2,1)}, bf16[1024,128]{1,0:T(8,128)(2,1)S(1)}, u32[]{:S(2)}, u32[]{:S(2)}) collective-permute-start(bf16[1024,128]{1,0:T(8,128)(2,1)} %own.1), channel_id=1, source_target_pairs={{0,2},{1,3},{2,0},{3,1},{4,6},{5,7},{6,4},{7,5},{8,10},{9,11},{10,... | collective-permute-start | bytes 786440 | tf_op jit(solution)/shard_map/ppermute | solution.py:21
  3.6 8.0 %collective-permute-start.9 = (bf16[1024,128]{1,0:T(8,128)(2,1)}, bf16[1024,128]{1,0:T(8,128)(2,1)S(1)}, u32[]{:S(2)}, u32[]{:S(2)}) collective-permute-start(bf16[1024,128]{1,0:T(8,128)(2,1)} %own.1), channel_id=1, source_target_pairs={{0,4},{4,0},{8,12},{12,8},{16,20},{20,16},{24,28},{28,24},{1,5},{5... | collective-permute-start | bytes 786440 | tf_op jit(solution)/shard_map/ppermute | solution.py:21
  5.2 1.0 %copy-start.1 = (bf16[1024,128]{1,0:T(8,128)(2,1)S(1)}, bf16[1024,128]{1,0:T(8,128)(2,1)}, u32[]{:S(2)}) copy-start(bf16[1024,128]{1,0:T(8,128)(2,1)} %own.1) | copy-start | bytes 786436
  6.9 5.1 %collective-permute-start = (bf16[1024,128]{1,0:T(8,128)(2,1)S(1)}, bf16[1024,128]{1,0:T(8,128)(2,1)S(1)}, u32[]{:S(2)}, u32[]{:S(2)}) collective-permute-start(bf16[1024,128]{1,0:T(8,128)(2,1)S(1)} %get-tuple-element.20.refs_0_), channel_id=1, source_target_pairs={{0,1},{1,0},{2,3},{3,2},{4,5},{5,4},{6,7},{7,6},{8,9},{9,8},{10,11... | collective-permute-start | bytes 786440 | tf_op jit(solution)/shard_map/ppermute | solution.py:21
  10.2 1.8 %collective-permute-start.2 = (bf16[1024,128]{1,0:T(8,128)(2,1)S(1)}, bf16[1024,128]{1,0:T(8,128)(2,1)S(1)}, u32[]{:S(2)}, u32[]{:S(2)}) collective-permute-start(bf16[1024,128]{1,0:T(8,128)(2,1)S(1)} %collective-permute-done.1.refs_1_.refs_2_), channel_id=1, source_target_pairs={{0,1},{1,0},{2,3},{3,2},{4,5},{5,4},{6,7},{7,6},{8,9},{9,8},{10,11... | collective-permute-start | bytes 786440 | tf_op jit(solution)/shard_map/ppermute | solution.py:21
  11.6 12.0 %collective-permute-start.11 = (bf16[1024,128]{1,0:T(8,128)(2,1)S(1)}, bf16[1024,128]{1,0:T(8,128)(2,1)S(1)}, u32[]{:S(2)}, u32[]{:S(2)}) collective-permute-start(bf16[1024,128]{1,0:T(8,128)(2,1)S(1)} %collective-permute-done.9.refs_0_), channel_id=1, source_target_pairs={{0,2},{1,3},{2,0},{3,1},{4,6},{5,7},{6,4},{7,5},{8,10},{9,11},{10,... | collective-permute-start | bytes 786440 | tf_op jit(solution)/shard_map/ppermute | solution.py:21
  12.4 7.8 %collective-permute-start.4 = (bf16[512,128]{1,0:T(8,128)(2,1)S(1)}, bf16[512,128]{1,0:T(8,128)(2,1)S(1)}, u32[]{:S(2)}, u32[]{:S(2)}) collective-permute-start(bf16[512,128]{1,0:T(8,128)(2,1)S(1)} %get-tuple-element.22), channel_id=1, source_target_pairs={{0,8},{4,12},{8,0},{12,4},{16,24},{20,28},{24,16},{28,20},{1,9},{5... | collective-permute-start | bytes 393224 | tf_op jit(solution)/shard_map/ppermute | solution.py:21
  14.2 8.9 %collective-permute-start.3 = (bf16[512,128]{1,0:T(8,128)(2,1)S(1)}, bf16[512,128]{1,0:T(8,128)(2,1)S(1)}, u32[]{:S(2)}, u32[]{:S(2)}) collective-permute-start(bf16[512,128]{1,0:T(8,128)(2,1)S(1)} %get-tuple-element.21), channel_id=1, source_target_pairs={{0,16},{4,20},{8,24},{12,28},{16,0},{20,4},{24,8},{28,12},{1,17},{... | collective-permute-start | bytes 393224 | tf_op jit(solution)/shard_map/ppermute | solution.py:21
  16.8 14.5 %collective-permute-start.10 = (bf16[1024,128]{1,0:T(8,128)(2,1)S(1)}, bf16[1024,128]{1,0:T(8,128)(2,1)S(1)}, u32[]{:S(2)}, u32[]{:S(2)}) collective-permute-start(bf16[1024,128]{1,0:T(8,128)(2,1)S(1)} %collective-permute-done.9.refs_0_), channel_id=1, source_target_pairs={{0,1},{1,0},{2,3},{3,2},{4,5},{5,4},{6,7},{7,6},{8,9},{9,8},{10,11... | collective-permute-start | bytes 786440 | tf_op jit(solution)/shard_map/ppermute | solution.py:21
  20.2 5.0 %collective-permute-start.6 = (bf16[512,128]{1,0:T(8,128)(2,1)S(1)}, bf16[512,128]{1,0:T(8,128)(2,1)S(1)}, u32[]{:S(2)}, u32[]{:S(2)}) collective-permute-start(bf16[512,128]{1,0:T(8,128)(2,1)S(1)} %add.15), channel_id=1, source_target_pairs={{0,4},{4,0},{8,12},{12,8},{16,20},{20,16},{24,28},{28,24},{1,5},{5... | collective-permute-start | bytes 393224 | tf_op jit(solution)/shard_map/ppermute | solution.py:21
  23.1 6.1 %collective-permute-start.5 = (bf16[512,128]{1,0:T(8,128)(2,1)S(1)}, bf16[512,128]{1,0:T(8,128)(2,1)S(1)}, u32[]{:S(2)}, u32[]{:S(2)}) collective-permute-start(bf16[512,128]{1,0:T(8,128)(2,1)S(1)} %add.16), channel_id=1, source_target_pairs={{0,8},{4,12},{8,0},{12,4},{16,24},{20,28},{24,16},{28,20},{1,9},{5... | collective-permute-start | bytes 393224 | tf_op jit(solution)/shard_map/ppermute | solution.py:21
  23.6 7.7 %collective-permute-start.12 = (bf16[1024,128]{1,0:T(8,128)(2,1)S(1)}, bf16[1024,128]{1,0:T(8,128)(2,1)S(1)}, u32[]{:S(2)}, u32[]{:S(2)}) collective-permute-start(bf16[1024,128]{1,0:T(8,128)(2,1)S(1)} %collective-permute-done.11.refs_2_), channel_id=1, source_target_pairs={{0,1},{1,0},{2,3},{3,2},{4,5},{5,4},{6,7},{7,6},{8,9},{9,8},{10,11... | collective-permute-start | bytes 786440 | tf_op jit(solution)/shard_map/ppermute | solution.py:21
  25.3 5.5 %copy-start = (bf16[1024,128]{1,0:T(8,128)(2,1)S(1)}, bf16[1024,128]{1,0:T(8,128)(2,1)}, u32[]{:S(2)}) copy-start(bf16[1024,128]{1,0:T(8,128)(2,1)} %signals.5) | copy-start | bytes 786436
  25.3 8.1 %collective-permute-start.8 = (bf16[512,128]{1,0:T(8,128)(2,1)S(1)}, bf16[512,128]{1,0:T(8,128)(2,1)S(1)}, u32[]{:S(2)}, u32[]{:S(2)}) collective-permute-start(bf16[512,128]{1,0:T(8,128)(2,1)S(1)} %add.17), channel_id=1, source_target_pairs={{0,16},{4,20},{8,24},{12,28},{16,0},{20,4},{24,8},{28,12},{1,17},{... | collective-permute-start | bytes 393224 | tf_op jit(solution)/shard_map/ppermute | solution.py:21
  29.2 5.0 %collective-permute-start.7 = (bf16[512,128]{1,0:T(8,128)(2,1)S(1)}, bf16[512,128]{1,0:T(8,128)(2,1)S(1)}, u32[]{:S(2)}, u32[]{:S(2)}) collective-permute-start(bf16[512,128]{1,0:T(8,128)(2,1)S(1)} %add.18.refs_0_), channel_id=1, source_target_pairs={{0,4},{4,0},{8,12},{12,8},{16,20},{20,16},{24,28},{28,24},{1,5},{5... | collective-permute-start | bytes 393224 | tf_op jit(solution)/shard_map/ppermute | solution.py:21
  31.8 2.5 %copy-start.2 = (bf16[2,1,64,64]{3,2,1,0:T(8,128)(2,1)S(1)}, bf16[2,1,64,64]{3,2,1,0:T(8,128)(2,1)}, u32[]{:S(2)}) copy-start(bf16[2,1,64,64]{3,2,1,0:T(8,128)(2,1)} %inverses.1) | copy-start | bytes 49156
  35.4 4.5 %collective-permute-start.13 = (f32[1,128]{1,0:T(1,128)S(1)}, f32[1,128]{1,0:T(1,128)S(1)}, u32[]{:S(2)}, u32[]{:S(2)}) collective-permute-start(f32[1,128]{1,0:T(1,128)S(1)} %get-tuple-element.32), channel_id=1, source_target_pairs={{0,16},{4,20},{8,24},{12,28},{16,0},{20,4},{24,8},{28,12},{1,17},{... | collective-permute-start | bytes 1544 | tf_op jit(solution)/shard_map/ppermute | solution.py:21
  39.9 3.5 %collective-permute-start.14 = (f32[1,128]{1,0:T(1,128)S(1)}, f32[1,128]{1,0:T(1,128)S(1)}, u32[]{:S(2)}, u32[]{:S(2)}) collective-permute-start(f32[1,128]{1,0:T(1,128)S(1)} %max.6), channel_id=1, source_target_pairs={{0,8},{4,12},{8,0},{12,4},{16,24},{20,28},{24,16},{28,20},{1,9},{5... | collective-permute-start | bytes 1544 | tf_op jit(solution)/shard_map/ppermute | solution.py:21

commit v7 on v6

--- a/solution.py
+++ b/solution.py
@@ -197,7 +197,7 @@
     arrived = [swap(blocks[h], "atoms", n_atoms, orders[h][0]) for h in range(2)]
     for i in range(1, len(bits)):
         for h in (1, 0):
-            come = after(arrived[h], blocks[1 - h]) if i > 1 or h == 0 else arrived[h]
+            come = after(arrived[h], blocks[1 - h]) if i == 1 and h == 0 else arrived[h]
             blocks[h] = blocks[h] + come
             arrived[h] = swap(blocks[h], "atoms", n_atoms, orders[h][i])
     sides = [ready(signals, [[piece] for piece in pieces]) for pieces in (here, there)]

time: 44.1 us -> 44 us (level)
  waiting for transfers between devices: 21.2 us -> 20.3 us
  starting transfers between devices: 15.8 us -> 16.6 us
    ppermute x15, waiting for transfers between devices: 21.2 us -> 20.3 us  [swap(): return lax.ppermute(block, axis, [(i, i ^ mask) for i in range(size)])]
    ppermute x15, starting transfers between devices: 15.8 us -> 16.6 us  [swap(): return lax.ppermute(block, axis, [(i, i ^ mask) for i in range(size)])]
where the time goes in v7:
time: 44 us; the launch traced here: 43.9 us
  waiting for transfers between devices  20.3 us (46%)
  starting transfers between devices  16.6 us (38%)
  Pallas kernels  3.24 us (7%)
  local copies, waits for them, and re-layouts  2.27 us (5%)
  between operations  0.76 us (2%)
  other arithmetic  0.71 us (2%)
    ppermute x15, waiting for transfers between devices, swap(): return lax.ppermute(block, axis, [(i, i ^ mask) for i in range(size)])  20.3 us
    ppermute x15, starting transfers between devices, swap(): return lax.ppermute(block, axis, [(i, i ^ mask) for i in range(size)])  16.6 us
    unnamed x10, local copies, waits for them, and re-layouts  2.27 us
    pallas_call x1, Pallas kernels, finish(): pl.pallas_call(functools.partial(finish_kernel, n_sig, [len(term) for ter...  1.17 us
    pallas_call x2, Pallas kernels, ready(): pl.pallas_call(functools.partial(ready_kernel, [len(piece) for piece in p...  0.95 us
  transfers between devices with their start and end apart: 15, of which 10 were waited for; matrix products, arithmetic and copies ran while one was open for 3% of the time, Pallas kernels for 5%

profile of v7, /device:TPU:0, one launch (start us, length us, event | category | flops | bytes accessed | tf_op | source)
XLA Modules:
  0.0 43.9 jit_solution(15111858970074348627)
XLA Ops:
  0.6 0.0 copy-start.3
  0.6 3.0 %collective-permute-start.1 = (bf16[1024,128]{1,0:T(8,128)(2,1)}, bf16[1024,128]{1,0:T(8,128)(2,1)S(1)}, u32[]{:S(2)}, u32[]{:S(2)}) collective-permute-start(bf16[1024,128]{1,0:T(8,128)(2,1)} %own.1), channel_id=1, source_target_pairs={{0,2},{1,3},{2,0},{3,1},{4,6},{5,7},{6,4},{7,5},{8,10},{9,11},{10,... | collective-permute-start | bytes 786440 | tf_op jit(solution)/shard_map/ppermute | solution.py:21
  3.6 1.5 %collective-permute-start.9 = (bf16[1024,128]{1,0:T(8,128)(2,1)}, bf16[1024,128]{1,0:T(8,128)(2,1)S(1)}, u32[]{:S(2)}, u32[]{:S(2)}) collective-permute-start(bf16[1024,128]{1,0:T(8,128)(2,1)} %own.1), channel_id=1, source_target_pairs={{0,4},{4,0},{8,12},{12,8},{16,20},{20,16},{24,28},{28,24},{1,5},{5... | collective-permute-start | bytes 786440 | tf_op jit(solution)/shard_map/ppermute | solution.py:21
  5.2 0.0 copy-done.3
  5.2 0.0 copy-start.1
  5.2 1.0 %copy-done.1 = bf16[1024,128]{1,0:T(8,128)(2,1)S(1)} copy-done((bf16[1024,128]{1,0:T(8,128)(2,1)S(1)}, bf16[1024,128]{1,0:T(8,128)(2,1)}, u32[]{:S(2)}) %copy-start.1) | copy-done | bytes 262168
  6.1 0.8 %fetch.1 = (bf16[1024,128]{1,0:T(8,128)(2,1)S(1)}, bf16[1024,128]{1,0:T(8,128)(2,1)S(1)}, bf16[384,128]{1,0:T(8,128)(2,1)S(1)}) custom-call(s32[2]{0:T(128)S(1)} %bitcast.3, bf16[1024,128]{1,0:T(8,128)(2,1)S(1)} %copy-done.1), custom_call_target="tpu_custom_call" | custom-call | tf_op jit(solution)/shard_map/fetch/pallas_call | solution.py:56
  6.9 0.1 collective-permute-start
  7.0 3.2 %collective-permute-done.1.refs_1_.refs_2_ = bf16[1024,128]{1,0:T(8,128)(2,1)S(1)} collective-permute-done((bf16[1024,128]{1,0:T(8,128)(2,1)}, bf16[1024,128]{1,0:T(8,128)(2,1)S(1)}, u32[]{:S(2)}, u32[]{:S(2)}) %collective-permute-start.1) | collective-permute-done | bytes 262176 | tf_op jit(solution)/shard_map/ppermute | solution.py:21
  10.2 0.0 collective-permute-start.2
  10.2 1.5 %collective-permute-done.9.refs_0_ = bf16[1024,128]{1,0:T(8,128)(2,1)S(1)} collective-permute-done((bf16[1024,128]{1,0:T(8,128)(2,1)}, bf16[1024,128]{1,0:T(8,128)(2,1)S(1)}, u32[]{:S(2)}, u32[]{:S(2)}) %collective-permute-start.9) | collective-permute-done | bytes 262176 | tf_op jit(solution)/shard_map/ppermute | solution.py:21
  11.6 0.4 collective-permute-start.11
  12.0 0.0 collective-permute-done.refs_0_.refs_1_
  12.0 0.0 collective-permute-done.2.refs_2_.refs_3_
  12.0 0.4 pick.1
  12.4 1.8 %collective-permute-start.4 = (bf16[512,128]{1,0:T(8,128)(2,1)S(1)}, bf16[512,128]{1,0:T(8,128)(2,1)S(1)}, u32[]{:S(2)}, u32[]{:S(2)}) collective-permute-start(bf16[512,128]{1,0:T(8,128)(2,1)S(1)} %get-tuple-element.20), channel_id=1, source_target_pairs={{0,8},{4,12},{8,0},{12,4},{16,24},{20,28},{24,16},{28,20},{1,9},{5... | collective-permute-start | bytes 393224 | tf_op jit(solution)/shard_map/ppermute | solution.py:21
  14.2 2.6 %collective-permute-start.3 = (bf16[512,128]{1,0:T(8,128)(2,1)S(1)}, bf16[512,128]{1,0:T(8,128)(2,1)S(1)}, u32[]{:S(2)}, u32[]{:S(2)}) collective-permute-start(bf16[512,128]{1,0:T(8,128)(2,1)S(1)} %get-tuple-element.19), channel_id=1, source_target_pairs={{0,16},{4,20},{8,24},{12,28},{16,0},{20,4},{24,8},{28,12},{1,17},{... | collective-permute-start | bytes 393224 | tf_op jit(solution)/shard_map/ppermute | solution.py:21
  16.8 0.0 collective-permute-start.10
  16.8 2.1 %collective-permute-done.11.refs_2_ = bf16[1024,128]{1,0:T(8,128)(2,1)S(1)} collective-permute-done((bf16[1024,128]{1,0:T(8,128)(2,1)S(1)}, bf16[1024,128]{1,0:T(8,128)(2,1)S(1)}, u32[]{:S(2)}, u32[]{:S(2)}) %collective-permute-start.11) | collective-permute-done | bytes 262176 | tf_op jit(solution)/shard_map/ppermute | solution.py:21
  18.9 0.0 collective-permute-start.12
  18.9 1.3 %collective-permute-done.4 = bf16[512,128]{1,0:T(8,128)(2,1)S(1)} collective-permute-done((bf16[512,128]{1,0:T(8,128)(2,1)S(1)}, bf16[512,128]{1,0:T(8,128)(2,1)S(1)}, u32[]{:S(2)}, u32[]{:S(2)}) %collective-permute-start.4) | collective-permute-done | bytes 131104 | tf_op jit(solution)/shard_map/ppermute | solution.py:21
  20.2 1.6 %collective-permute-start.7 = (bf16[512,128]{1,0:T(8,128)(2,1)S(1)}, bf16[512,128]{1,0:T(8,128)(2,1)S(1)}, u32[]{:S(2)}, u32[]{:S(2)}) collective-permute-start(bf16[512,128]{1,0:T(8,128)(2,1)S(1)} %add.15), channel_id=1, source_target_pairs={{0,4},{4,0},{8,12},{12,8},{16,20},{20,16},{24,28},{28,24},{1,5},{5... | collective-permute-start | bytes 393224 | tf_op jit(solution)/shard_map/ppermute | solution.py:21
  21.8 1.3 %collective-permute-done.3 = bf16[512,128]{1,0:T(8,128)(2,1)S(1)} collective-permute-done((bf16[512,128]{1,0:T(8,128)(2,1)S(1)}, bf16[512,128]{1,0:T(8,128)(2,1)S(1)}, u32[]{:S(2)}, u32[]{:S(2)}) %collective-permute-start.3) | collective-permute-done | bytes 131104 | tf_op jit(solution)/shard_map/ppermute | solution.py:21
  23.1 0.5 %collective-permute-start.5 = (bf16[512,128]{1,0:T(8,128)(2,1)S(1)}, bf16[512,128]{1,0:T(8,128)(2,1)S(1)}, u32[]{:S(2)}, u32[]{:S(2)}) collective-permute-start(bf16[512,128]{1,0:T(8,128)(2,1)S(1)} %add.16), channel_id=1, source_target_pairs={{0,8},{4,12},{8,0},{12,4},{16,24},{20,28},{24,16},{28,20},{1,9},{5... | collective-permute-start | bytes 393224 | tf_op jit(solution)/shard_map/ppermute | solution.py:21
  23.6 1.7 %collective-permute-done.7 = bf16[512,128]{1,0:T(8,128)(2,1)S(1)} collective-permute-done((bf16[512,128]{1,0:T(8,128)(2,1)S(1)}, bf16[512,128]{1,0:T(8,128)(2,1)S(1)}, u32[]{:S(2)}, u32[]{:S(2)}) %collective-permute-start.7) | collective-permute-done | bytes 131104 | tf_op jit(solution)/shard_map/ppermute | solution.py:21
  25.3 0.0 copy-start
  25.3 2.6 %collective-permute-start.8 = (bf16[512,128]{1,0:T(8,128)(2,1)S(1)}, bf16[512,128]{1,0:T(8,128)(2,1)S(1)}, u32[]{:S(2)}, u32[]{:S(2)}) collective-permute-start(bf16[512,128]{1,0:T(8,128)(2,1)S(1)} %add.18), channel_id=1, source_target_pairs={{0,16},{4,20},{8,24},{12,28},{16,0},{20,4},{24,8},{28,12},{1,17},{... | collective-permute-start | bytes 393224 | tf_op jit(solution)/shard_map/ppermute | solution.py:21
  27.9 0.2 collective-permute-done.5
  28.1 1.6 %collective-permute-start.6 = (bf16[512,128]{1,0:T(8,128)(2,1)S(1)}, bf16[512,128]{1,0:T(8,128)(2,1)S(1)}, u32[]{:S(2)}, u32[]{:S(2)}) collective-permute-start(bf16[512,128]{1,0:T(8,128)(2,1)S(1)} %add.17.refs_0_), channel_id=1, source_target_pairs={{0,4},{4,0},{8,12},{12,8},{16,20},{20,16},{24,28},{28,24},{1,5},{5... | collective-permute-start | bytes 393224 | tf_op jit(solution)/shard_map/ppermute | solution.py:21
  29.7 0.0 copy-done
  29.7 0.5 %ready.2 = (bf16[512,1024]{1,0:T(8,128)(2,1)S(1)}, f32[512,128]{1,0:T(8,128)S(1)}) custom-call(bf16[1024,128]{1,0:T(8,128)(2,1)S(1)} %copy-done, bf16[1024,128]{1,0:T(8,128)(2,1)S(1)} %get-tuple-element.18.refs_0_, bf16[1024,128]{1,0:T(8,128)(2,1)S(1)} %collective-permute-done.refs_0_.refs_1_, bf16[1024,128]{1,0:T(8,128)(2,1)S(1)} %collective-permute-done.1.refs_1_.refs_2_, ...), custom_call_target="tpu_custom_call" | custom-call | tf_op jit(solution)/shard_map/ready/pallas_call | solution.py:98
  30.2 0.0 collective-permute-done.10.refs_1_
  30.2 0.0 collective-permute-done.12.refs_3_
  30.2 0.5 %ready.3 = (bf16[512,1024]{1,0:T(8,128)(2,1)S(1)}, f32[512,128]{1,0:T(8,128)S(1)}) custom-call(bf16[1024,128]{1,0:T(8,128)(2,1)S(1)} %copy-done, bf16[1024,128]{1,0:T(8,128)(2,1)S(1)} %collective-permute-done.9.refs_0_, bf16[1024,128]{1,0:T(8,128)(2,1)S(1)} %collective-permute-done.10.refs_1_, bf16[1024,128]{1,0:T(8,128)(2,1)S(1)} %collective-permute-done.11.refs_2_, ...), custom_call_target="tpu_custom_call" | custom-call | tf_op jit(solution)/shard_map/ready/pallas_call | solution.py:98
  30.7 0.0 copy-start.2
  30.7 3.3 %collective-permute-done.8 = bf16[512,128]{1,0:T(8,128)(2,1)S(1)} collective-permute-done((bf16[512,128]{1,0:T(8,128)(2,1)S(1)}, bf16[512,128]{1,0:T(8,128)(2,1)S(1)}, u32[]{:S(2)}, u32[]{:S(2)}) %collective-permute-start.8) | collective-permute-done | bytes 131104 | tf_op jit(solution)/shard_map/ppermute | solution.py:21
  34.1 0.0 collective-permute-done.6.refs_1_
  34.1 0.0 copy-done.2
  34.1 1.2 %finish.1 = (bf16[512,128]{1,0:T(8,128)(2,1)S(1)}, bf16[2,64,128]{2,1,0:T(8,128)(2,1)S(1)}, f32[1,128]{1,0:T(1,128)S(1)}) custom-call(bf16[2,1,64,64]{3,2,1,0:T(8,128)(2,1)S(1)} %copy-done.2, bf16[1024,128]{1,0:T(8,128)(2,1)S(1)} %copy-done, bf16[512,128]{1,0:T(8,128)(2,1)S(1)} %add.17.refs_0_, bf16[512,128]{1,0:T(8,128)(2,1)S(1)} %collective-permute-done.6.refs_1_, ...), custom_call_target="tpu_custom_call" | custom-call | tf_op jit(solution)/shard_map/finish/pallas_call | solution.py:156
  35.3 0.1 collective-permute-start.13
  35.4 4.4 %collective-permute-done.13 = f32[1,128]{1,0:T(1,128)S(1)} collective-permute-done((f32[1,128]{1,0:T(1,128)S(1)}, f32[1,128]{1,0:T(1,128)S(1)}, u32[]{:S(2)}, u32[]{:S(2)}) %collective-permute-start.13) | collective-permute-done | bytes 544 | tf_op jit(solution)/shard_map/ppermute | solution.py:21
  39.8 0.8 %collective-permute-start.14 = (f32[1,128]{1,0:T(1,128)S(1)}, f32[1,128]{1,0:T(1,128)S(1)}, u32[]{:S(2)}, u32[]{:S(2)}) collective-permute-start(f32[1,128]{1,0:T(1,128)S(1)} %max.6), channel_id=1, source_target_pairs={{0,8},{4,12},{8,0},{12,4},{16,24},{20,28},{24,16},{28,20},{1,9},{5... | collective-permute-start | bytes 1544 | tf_op jit(solution)/shard_map/ppermute | solution.py:21
  40.6 0.7 %copy.7 = bf16[512,128]{1,0:T(8,128)(2,1)} copy(bf16[512,128]{1,0:T(8,128)(2,1)S(1)} %get-tuple-element.29) | data formatting | bytes 262144
  41.3 0.6 %copy.8 = bf16[2,64,128]{2,1,0:T(8,128)(2,1)} copy(bf16[2,64,128]{2,1,0:T(8,128)(2,1)S(1)} %get-tuple-element.30) | data formatting | bytes 65536
  41.9 1.4 %collective-permute-done.14 = f32[1,128]{1,0:T(1,128)S(1)} collective-permute-done((f32[1,128]{1,0:T(1,128)S(1)}, f32[1,128]{1,0:T(1,128)S(1)}, u32[]{:S(2)}, u32[]{:S(2)}) %collective-permute-start.14) | collective-permute-done | bytes 544 | tf_op jit(solution)/shard_map/ppermute | solution.py:21
  43.3 0.5 %maximum_bitcast_fusion = f32[128]{0:T(128)} fusion(f32[1,128]{1,0:T(1,128)S(1)} %max.6, f32[1,128]{1,0:T(1,128)S(1)} %collective-permute-done.14), kind=kLoop, calls=%fused_computation | loop fusion | flops 128 | bytes 1536 | tf_op jit(solution)/shard_map/squeeze | solution.py:208
  (6 shorter events, 0.2 us)
Async XLA Ops:
  0.6 4.5 %copy-start.3 = (s32[2,1]{0,1:T(1,128)S(1)}, s32[2,1]{0,1:T(1,128)}, u32[]{:S(2)}) copy-start(s32[2,1]{0,1:T(1,128)} %param.6) | copy-start | bytes 28
  0.6 9.5 %collective-permute-start.1 = (bf16[1024,128]{1,0:T(8,128)(2,1)}, bf16[1024,128]{1,0:T(8,128)(2,1)S(1)}, u32[]{:S(2)}, u32[]{:S(2)}) collective-permute-start(bf16[1024,128]{1,0:T(8,128)(2,1)} %own.1), channel_id=1, source_target_pairs={{0,2},{1,3},{2,0},{3,1},{4,6},{5,7},{6,4},{7,5},{8,10},{9,11},{10,... | collective-permute-start | bytes 786440 | tf_op jit(solution)/shard_map/ppermute | solution.py:21
  3.6 8.0 %collective-permute-start.9 = (bf16[1024,128]{1,0:T(8,128)(2,1)}, bf16[1024,128]{1,0:T(8,128)(2,1)S(1)}, u32[]{:S(2)}, u32[]{:S(2)}) collective-permute-start(bf16[1024,128]{1,0:T(8,128)(2,1)} %own.1), channel_id=1, source_target_pairs={{0,4},{4,0},{8,12},{12,8},{16,20},{20,16},{24,28},{28,24},{1,5},{5... | collective-permute-start | bytes 786440 | tf_op jit(solution)/shard_map/ppermute | solution.py:21
  5.2 1.0 %copy-start.1 = (bf16[1024,128]{1,0:T(8,128)(2,1)S(1)}, bf16[1024,128]{1,0:T(8,128)(2,1)}, u32[]{:S(2)}) copy-start(bf16[1024,128]{1,0:T(8,128)(2,1)} %own.1) | copy-start | bytes 786436
  6.9 5.1 %collective-permute-start = (bf16[1024,128]{1,0:T(8,128)(2,1)S(1)}, bf16[1024,128]{1,0:T(8,128)(2,1)S(1)}, u32[]{:S(2)}, u32[]{:S(2)}) collective-permute-start(bf16[1024,128]{1,0:T(8,128)(2,1)S(1)} %get-tuple-element.18.refs_0_), channel_id=1, source_target_pairs={{0,1},{1,0},{2,3},{3,2},{4,5},{5,4},{6,7},{7,6},{8,9},{9,8},{10,11... | collective-permute-start | bytes 786440 | tf_op jit(solution)/shard_map/ppermute | solution.py:21
  10.2 1.8 %collective-permute-start.2 = (bf16[1024,128]{1,0:T(8,128)(2,1)S(1)}, bf16[1024,128]{1,0:T(8,128)(2,1)S(1)}, u32[]{:S(2)}, u32[]{:S(2)}) collective-permute-start(bf16[1024,128]{1,0:T(8,128)(2,1)S(1)} %collective-permute-done.1.refs_1_.refs_2_), channel_id=1, source_target_pairs={{0,1},{1,0},{2,3},{3,2},{4,5},{5,4},{6,7},{7,6},{8,9},{9,8},{10,11... | collective-permute-start | bytes 786440 | tf_op jit(solution)/shard_map/ppermute | solution.py:21
  11.6 7.3 %collective-permute-start.11 = (bf16[1024,128]{1,0:T(8,128)(2,1)S(1)}, bf16[1024,128]{1,0:T(8,128)(2,1)S(1)}, u32[]{:S(2)}, u32[]{:S(2)}) collective-permute-start(bf16[1024,128]{1,0:T(8,128)(2,1)S(1)} %collective-permute-done.9.refs_0_), channel_id=1, source_target_pairs={{0,2},{1,3},{2,0},{3,1},{4,6},{5,7},{6,4},{7,5},{8,10},{9,11},{10,... | collective-permute-start | bytes 786440 | tf_op jit(solution)/shard_map/ppermute | solution.py:21
  12.4 7.8 %collective-permute-start.4 = (bf16[512,128]{1,0:T(8,128)(2,1)S(1)}, bf16[512,128]{1,0:T(8,128)(2,1)S(1)}, u32[]{:S(2)}, u32[]{:S(2)}) collective-permute-start(bf16[512,128]{1,0:T(8,128)(2,1)S(1)} %get-tuple-element.20), channel_id=1, source_target_pairs={{0,8},{4,12},{8,0},{12,4},{16,24},{20,28},{24,16},{28,20},{1,9},{5... | collective-permute-start | bytes 393224 | tf_op jit(solution)/shard_map/ppermute | solution.py:21
  14.2 8.9 %collective-permute-start.3 = (bf16[512,128]{1,0:T(8,128)(2,1)S(1)}, bf16[512,128]{1,0:T(8,128)(2,1)S(1)}, u32[]{:S(2)}, u32[]{:S(2)}) collective-permute-start(bf16[512,128]{1,0:T(8,128)(2,1)S(1)} %get-tuple-element.19), channel_id=1, source_target_pairs={{0,16},{4,20},{8,24},{12,28},{16,0},{20,4},{24,8},{28,12},{1,17},{... | collective-permute-start | bytes 393224 | tf_op jit(solution)/shard_map/ppermute | solution.py:21
  16.8 13.5 %collective-permute-start.10 = (bf16[1024,128]{1,0:T(8,128)(2,1)S(1)}, bf16[1024,128]{1,0:T(8,128)(2,1)S(1)}, u32[]{:S(2)}, u32[]{:S(2)}) collective-permute-start(bf16[1024,128]{1,0:T(8,128)(2,1)S(1)} %collective-permute-done.9.refs_0_), channel_id=1, source_target_pairs={{0,1},{1,0},{2,3},{3,2},{4,5},{5,4},{6,7},{7,6},{8,9},{9,8},{10,11... | collective-permute-start | bytes 786440 | tf_op jit(solution)/shard_map/ppermute | solution.py:21
  18.9 11.3 %collective-permute-start.12 = (bf16[1024,128]{1,0:T(8,128)(2,1)S(1)}, bf16[1024,128]{1,0:T(8,128)(2,1)S(1)}, u32[]{:S(2)}, u32[]{:S(2)}) collective-permute-start(bf16[1024,128]{1,0:T(8,128)(2,1)S(1)} %collective-permute-done.11.refs_2_), channel_id=1, source_target_pairs={{0,1},{1,0},{2,3},{3,2},{4,5},{5,4},{6,7},{7,6},{8,9},{9,8},{10,11... | collective-permute-start | bytes 786440 | tf_op jit(solution)/shard_map/ppermute | solution.py:21
  20.2 5.0 %collective-permute-start.7 = (bf16[512,128]{1,0:T(8,128)(2,1)S(1)}, bf16[512,128]{1,0:T(8,128)(2,1)S(1)}, u32[]{:S(2)}, u32[]{:S(2)}) collective-permute-start(bf16[512,128]{1,0:T(8,128)(2,1)S(1)} %add.15), channel_id=1, source_target_pairs={{0,4},{4,0},{8,12},{12,8},{16,20},{20,16},{24,28},{28,24},{1,5},{5... | collective-permute-start | bytes 393224 | tf_op jit(solution)/shard_map/ppermute | solution.py:21
  23.1 5.0 %collective-permute-start.5 = (bf16[512,128]{1,0:T(8,128)(2,1)S(1)}, bf16[512,128]{1,0:T(8,128)(2,1)S(1)}, u32[]{:S(2)}, u32[]{:S(2)}) collective-permute-start(bf16[512,128]{1,0:T(8,128)(2,1)S(1)} %add.16), channel_id=1, source_target_pairs={{0,8},{4,12},{8,0},{12,4},{16,24},{20,28},{24,16},{28,20},{1,9},{5... | collective-permute-start | bytes 393224 | tf_op jit(solution)/shard_map/ppermute | solution.py:21
  25.3 4.4 %copy-start = (bf16[1024,128]{1,0:T(8,128)(2,1)S(1)}, bf16[1024,128]{1,0:T(8,128)(2,1)}, u32[]{:S(2)}) copy-start(bf16[1024,128]{1,0:T(8,128)(2,1)} %signals.5) | copy-start | bytes 786436
  25.3 8.8 %collective-permute-start.8 = (bf16[512,128]{1,0:T(8,128)(2,1)S(1)}, bf16[512,128]{1,0:T(8,128)(2,1)S(1)}, u32[]{:S(2)}, u32[]{:S(2)}) collective-permute-start(bf16[512,128]{1,0:T(8,128)(2,1)S(1)} %add.18), channel_id=1, source_target_pairs={{0,16},{4,20},{8,24},{12,28},{16,0},{20,4},{24,8},{28,12},{1,17},{... | collective-permute-start | bytes 393224 | tf_op jit(solution)/shard_map/ppermute | solution.py:21
  28.1 6.0 %collective-permute-start.6 = (bf16[512,128]{1,0:T(8,128)(2,1)S(1)}, bf16[512,128]{1,0:T(8,128)(2,1)S(1)}, u32[]{:S(2)}, u32[]{:S(2)}) collective-permute-start(bf16[512,128]{1,0:T(8,128)(2,1)S(1)} %add.17.refs_0_), channel_id=1, source_target_pairs={{0,4},{4,0},{8,12},{12,8},{16,20},{20,16},{24,28},{28,24},{1,5},{5... | collective-permute-start | bytes 393224 | tf_op jit(solution)/shard_map/ppermute | solution.py:21
  30.7 3.4 %copy-start.2 = (bf16[2,1,64,64]{3,2,1,0:T(8,128)(2,1)S(1)}, bf16[2,1,64,64]{3,2,1,0:T(8,128)(2,1)}, u32[]{:S(2)}) copy-start(bf16[2,1,64,64]{3,2,1,0:T(8,128)(2,1)} %inverses.1) | copy-start | bytes 49156
  35.3 4.5 %collective-permute-start.13 = (f32[1,128]{1,0:T(1,128)S(1)}, f32[1,128]{1,0:T(1,128)S(1)}, u32[]{:S(2)}, u32[]{:S(2)}) collective-permute-start(f32[1,128]{1,0:T(1,128)S(1)} %get-tuple-element.28), channel_id=1, source_target_pairs={{0,16},{4,20},{8,24},{12,28},{16,0},{20,4},{24,8},{28,12},{1,17},{... | collective-permute-start | bytes 1544 | tf_op jit(solution)/shard_map/ppermute | solution.py:21
  39.8 3.5 %collective-permute-start.14 = (f32[1,128]{1,0:T(1,128)S(1)}, f32[1,128]{1,0:T(1,128)S(1)}, u32[]{:S(2)}, u32[]{:S(2)}) collective-permute-start(f32[1,128]{1,0:T(1,128)S(1)} %max.6), channel_id=1, source_target_pairs={{0,8},{4,12},{8,0},{12,4},{16,24},{20,28},{24,16},{28,20},{1,9},{5... | collective-permute-start | bytes 1544 | tf_op jit(solution)/shard_map/ppermute | solution.py:21

commit v8 on v7

--- a/solution.py
+++ b/solution.py
@@ -175,7 +175,7 @@
     while bit < n_atoms:
         bits.append(bit)
         bit *= 2
-    top, twin = bits[-1], bits[0]
+    top, twin = bits[-1], bits[1]
 
     def gather(piece, local):
         pieces = {0: piece}

time: 44 us -> 44 us (level)
  waiting for transfers between devices: 20.3 us -> 19.5 us
  starting transfers between devices: 16.6 us -> 17.4 us
    ppermute x15, waiting for transfers between devices: 20.3 us -> 19.5 us  [swap(): return lax.ppermute(block, axis, [(i, i ^ mask) for i in range(size)])]
    ppermute x15, starting transfers between devices: 16.6 us -> 17.4 us  [swap(): return lax.ppermute(block, axis, [(i, i ^ mask) for i in range(size)])]
where the time goes in v8:
time: 44 us; the launch traced here: 43.9 us
  waiting for transfers between devices  19.5 us (44%)
  starting transfers between devices  17.4 us (40%)
  Pallas kernels  3.25 us (7%)
  local copies, waits for them, and re-layouts  2.27 us (5%)
  between operations  0.75 us (2%)
  other arithmetic  0.71 us (2%)
    ppermute x15, waiting for transfers between devices, swap(): return lax.ppermute(block, axis, [(i, i ^ mask) for i in range(size)])  19.5 us
    ppermute x15, starting transfers between devices, swap(): return lax.ppermute(block, axis, [(i, i ^ mask) for i in range(size)])  17.4 us
    unnamed x10, local copies, waits for them, and re-layouts  2.27 us
    pallas_call x1, Pallas kernels, finish(): pl.pallas_call(functools.partial(finish_kernel, n_sig, [len(term) for ter...  1.17 us
    pallas_call x2, Pallas kernels, ready(): pl.pallas_call(functools.partial(ready_kernel, [len(piece) for piece in p...  0.95 us
  transfers between devices with their start and end apart: 15, of which 10 were waited for; matrix products, arithmetic and copies ran while one was open for 3% of the time, Pallas kernels for 5%

profile of v8, /device:TPU:0, one launch (start us, length us, event | category | flops | bytes accessed | tf_op | source)
XLA Modules:
  0.0 43.9 jit_solution(6488226655297603313)
XLA Ops:
  0.6 0.0 copy-start.3
  0.6 3.0 %collective-permute-start.1 = (bf16[1024,128]{1,0:T(8,128)(2,1)}, bf16[1024,128]{1,0:T(8,128)(2,1)S(1)}, u32[]{:S(2)}, u32[]{:S(2)}) collective-permute-start(bf16[1024,128]{1,0:T(8,128)(2,1)} %own.1), channel_id=1, source_target_pairs={{0,2},{1,3},{2,0},{3,1},{4,6},{5,7},{6,4},{7,5},{8,10},{9,11},{10,... | collective-permute-start | bytes 786440 | tf_op jit(solution)/shard_map/ppermute | solution.py:21
  3.6 1.6 %collective-permute-start.9 = (bf16[1024,128]{1,0:T(8,128)(2,1)}, bf16[1024,128]{1,0:T(8,128)(2,1)S(1)}, u32[]{:S(2)}, u32[]{:S(2)}) collective-permute-start(bf16[1024,128]{1,0:T(8,128)(2,1)} %own.1), channel_id=1, source_target_pairs={{0,8},{4,12},{8,0},{12,4},{16,24},{20,28},{24,16},{28,20},{1,9},{5... | collective-permute-start | bytes 786440 | tf_op jit(solution)/shard_map/ppermute | solution.py:21
  5.2 0.0 copy-done.3
  5.2 0.0 copy-start.1
  5.2 1.0 %copy-done.1 = bf16[1024,128]{1,0:T(8,128)(2,1)S(1)} copy-done((bf16[1024,128]{1,0:T(8,128)(2,1)S(1)}, bf16[1024,128]{1,0:T(8,128)(2,1)}, u32[]{:S(2)}) %copy-start.1) | copy-done | bytes 262168
  6.2 0.8 %fetch.1 = (bf16[1024,128]{1,0:T(8,128)(2,1)S(1)}, bf16[1024,128]{1,0:T(8,128)(2,1)S(1)}, bf16[384,128]{1,0:T(8,128)(2,1)S(1)}) custom-call(s32[2]{0:T(128)S(1)} %bitcast.3, bf16[1024,128]{1,0:T(8,128)(2,1)S(1)} %copy-done.1), custom_call_target="tpu_custom_call" | custom-call | tf_op jit(solution)/shard_map/fetch/pallas_call | solution.py:56
  7.0 0.1 collective-permute-start
  7.1 3.1 %collective-permute-done.1.refs_1_.refs_2_ = bf16[1024,128]{1,0:T(8,128)(2,1)S(1)} collective-permute-done((bf16[1024,128]{1,0:T(8,128)(2,1)}, bf16[1024,128]{1,0:T(8,128)(2,1)S(1)}, u32[]{:S(2)}, u32[]{:S(2)}) %collective-permute-start.1) | collective-permute-done | bytes 262176 | tf_op jit(solution)/shard_map/ppermute | solution.py:21
  10.2 0.0 collective-permute-start.2
  10.2 1.5 %collective-permute-done.9.refs_0_ = bf16[1024,128]{1,0:T(8,128)(2,1)S(1)} collective-permute-done((bf16[1024,128]{1,0:T(8,128)(2,1)}, bf16[1024,128]{1,0:T(8,128)(2,1)S(1)}, u32[]{:S(2)}, u32[]{:S(2)}) %collective-permute-start.9) | collective-permute-done | bytes 262176 | tf_op jit(solution)/shard_map/ppermute | solution.py:21
  11.6 0.4 collective-permute-start.11
  12.1 0.0 collective-permute-done.refs_0_.refs_1_
  12.1 0.0 collective-permute-done.2.refs_2_.refs_3_
  12.1 0.4 pick.1
  12.4 1.7 %collective-permute-start.4 = (bf16[512,128]{1,0:T(8,128)(2,1)S(1)}, bf16[512,128]{1,0:T(8,128)(2,1)S(1)}, u32[]{:S(2)}, u32[]{:S(2)}) collective-permute-start(bf16[512,128]{1,0:T(8,128)(2,1)S(1)} %get-tuple-element.20), channel_id=1, source_target_pairs={{0,8},{4,12},{8,0},{12,4},{16,24},{20,28},{24,16},{28,20},{1,9},{5... | collective-permute-start | bytes 393224 | tf_op jit(solution)/shard_map/ppermute | solution.py:21
  14.2 2.6 %collective-permute-start.3 = (bf16[512,128]{1,0:T(8,128)(2,1)S(1)}, bf16[512,128]{1,0:T(8,128)(2,1)S(1)}, u32[]{:S(2)}, u32[]{:S(2)}) collective-permute-start(bf16[512,128]{1,0:T(8,128)(2,1)S(1)} %get-tuple-element.19), channel_id=1, source_target_pairs={{0,16},{4,20},{8,24},{12,28},{16,0},{20,4},{24,8},{28,12},{1,17},{... | collective-permute-start | bytes 393224 | tf_op jit(solution)/shard_map/ppermute | solution.py:21
  16.8 0.0 collective-permute-start.10
  16.8 2.1 %collective-permute-done.11.refs_2_ = bf16[1024,128]{1,0:T(8,128)(2,1)S(1)} collective-permute-done((bf16[1024,128]{1,0:T(8,128)(2,1)S(1)}, bf16[1024,128]{1,0:T(8,128)(2,1)S(1)}, u32[]{:S(2)}, u32[]{:S(2)}) %collective-permute-start.11) | collective-permute-done | bytes 262176 | tf_op jit(solution)/shard_map/ppermute | solution.py:21
  18.9 0.0 collective-permute-start.12
  18.9 1.3 %collective-permute-done.4 = bf16[512,128]{1,0:T(8,128)(2,1)S(1)} collective-permute-done((bf16[512,128]{1,0:T(8,128)(2,1)S(1)}, bf16[512,128]{1,0:T(8,128)(2,1)S(1)}, u32[]{:S(2)}, u32[]{:S(2)}) %collective-permute-start.4) | collective-permute-done | bytes 131104 | tf_op jit(solution)/shard_map/ppermute | solution.py:21
  20.2 1.6 %collective-permute-start.7 = (bf16[512,128]{1,0:T(8,128)(2,1)S(1)}, bf16[512,128]{1,0:T(8,128)(2,1)S(1)}, u32[]{:S(2)}, u32[]{:S(2)}) collective-permute-start(bf16[512,128]{1,0:T(8,128)(2,1)S(1)} %add.15), channel_id=1, source_target_pairs={{0,4},{4,0},{8,12},{12,8},{16,20},{20,16},{24,28},{28,24},{1,5},{5... | collective-permute-start | bytes 393224 | tf_op jit(solution)/shard_map/ppermute | solution.py:21
  21.8 1.3 %collective-permute-done.3 = bf16[512,128]{1,0:T(8,128)(2,1)S(1)} collective-permute-done((bf16[512,128]{1,0:T(8,128)(2,1)S(1)}, bf16[512,128]{1,0:T(8,128)(2,1)S(1)}, u32[]{:S(2)}, u32[]{:S(2)}) %collective-permute-start.3) | collective-permute-done | bytes 131104 | tf_op jit(solution)/shard_map/ppermute | solution.py:21
  23.1 0.5 %collective-permute-start.5 = (bf16[512,128]{1,0:T(8,128)(2,1)S(1)}, bf16[512,128]{1,0:T(8,128)(2,1)S(1)}, u32[]{:S(2)}, u32[]{:S(2)}) collective-permute-start(bf16[512,128]{1,0:T(8,128)(2,1)S(1)} %add.16), channel_id=1, source_target_pairs={{0,8},{4,12},{8,0},{12,4},{16,24},{20,28},{24,16},{28,20},{1,9},{5... | collective-permute-start | bytes 393224 | tf_op jit(solution)/shard_map/ppermute | solution.py:21
  23.6 1.6 %collective-permute-done.7 = bf16[512,128]{1,0:T(8,128)(2,1)S(1)} collective-permute-done((bf16[512,128]{1,0:T(8,128)(2,1)S(1)}, bf16[512,128]{1,0:T(8,128)(2,1)S(1)}, u32[]{:S(2)}, u32[]{:S(2)}) %collective-permute-start.7) | collective-permute-done | bytes 131104 | tf_op jit(solution)/shard_map/ppermute | solution.py:21
  25.3 0.0 copy-start
  25.3 2.6 %collective-permute-start.8 = (bf16[512,128]{1,0:T(8,128)(2,1)S(1)}, bf16[512,128]{1,0:T(8,128)(2,1)S(1)}, u32[]{:S(2)}, u32[]{:S(2)}) collective-permute-start(bf16[512,128]{1,0:T(8,128)(2,1)S(1)} %add.18), channel_id=1, source_target_pairs={{0,16},{4,20},{8,24},{12,28},{16,0},{20,4},{24,8},{28,12},{1,17},{... | collective-permute-start | bytes 393224 | tf_op jit(solution)/shard_map/ppermute | solution.py:21
  27.9 0.2 collective-permute-done.5
  28.1 1.6 %collective-permute-start.6 = (bf16[512,128]{1,0:T(8,128)(2,1)S(1)}, bf16[512,128]{1,0:T(8,128)(2,1)S(1)}, u32[]{:S(2)}, u32[]{:S(2)}) collective-permute-start(bf16[512,128]{1,0:T(8,128)(2,1)S(1)} %add.17.refs_0_), channel_id=1, source_target_pairs={{0,4},{4,0},{8,12},{12,8},{16,20},{20,16},{24,28},{28,24},{1,5},{5... | collective-permute-start | bytes 393224 | tf_op jit(solution)/shard_map/ppermute | solution.py:21
  29.7 0.0 copy-done
  29.7 0.5 %ready.2 = (bf16[512,1024]{1,0:T(8,128)(2,1)S(1)}, f32[512,128]{1,0:T(8,128)S(1)}) custom-call(bf16[1024,128]{1,0:T(8,128)(2,1)S(1)} %copy-done, bf16[1024,128]{1,0:T(8,128)(2,1)S(1)} %get-tuple-element.18.refs_0_, bf16[1024,128]{1,0:T(8,128)(2,1)S(1)} %collective-permute-done.refs_0_.refs_1_, bf16[1024,128]{1,0:T(8,128)(2,1)S(1)} %collective-permute-done.1.refs_1_.refs_2_, ...), custom_call_target="tpu_custom_call" | custom-call | tf_op jit(solution)/shard_map/ready/pallas_call | solution.py:98
  30.2 0.0 collective-permute-done.10.refs_1_
  30.2 0.0 collective-permute-done.12.refs_3_
  30.2 0.5 %ready.3 = (bf16[512,1024]{1,0:T(8,128)(2,1)S(1)}, f32[512,128]{1,0:T(8,128)S(1)}) custom-call(bf16[1024,128]{1,0:T(8,128)(2,1)S(1)} %copy-done, bf16[1024,128]{1,0:T(8,128)(2,1)S(1)} %collective-permute-done.9.refs_0_, bf16[1024,128]{1,0:T(8,128)(2,1)S(1)} %collective-permute-done.10.refs_1_, bf16[1024,128]{1,0:T(8,128)(2,1)S(1)} %collective-permute-done.11.refs_2_, ...), custom_call_target="tpu_custom_call" | custom-call | tf_op jit(solution)/shard_map/ready/pallas_call | solution.py:98
  30.7 0.0 copy-start.2
  30.7 3.3 %collective-permute-done.8 = bf16[512,128]{1,0:T(8,128)(2,1)S(1)} collective-permute-done((bf16[512,128]{1,0:T(8,128)(2,1)S(1)}, bf16[512,128]{1,0:T(8,128)(2,1)S(1)}, u32[]{:S(2)}, u32[]{:S(2)}) %collective-permute-start.8) | collective-permute-done | bytes 131104 | tf_op jit(solution)/shard_map/ppermute | solution.py:21
  34.1 0.0 collective-permute-done.6.refs_1_
  34.1 0.0 copy-done.2
  34.1 1.2 %finish.1 = (bf16[512,128]{1,0:T(8,128)(2,1)S(1)}, bf16[2,64,128]{2,1,0:T(8,128)(2,1)S(1)}, f32[1,128]{1,0:T(1,128)S(1)}) custom-call(bf16[2,1,64,64]{3,2,1,0:T(8,128)(2,1)S(1)} %copy-done.2, bf16[1024,128]{1,0:T(8,128)(2,1)S(1)} %copy-done, bf16[512,128]{1,0:T(8,128)(2,1)S(1)} %add.17.refs_0_, bf16[512,128]{1,0:T(8,128)(2,1)S(1)} %collective-permute-done.6.refs_1_, ...), custom_call_target="tpu_custom_call" | custom-call | tf_op jit(solution)/shard_map/finish/pallas_call | solution.py:156
  35.3 0.1 collective-permute-start.13
  35.4 4.4 %collective-permute-done.13 = f32[1,128]{1,0:T(1,128)S(1)} collective-permute-done((f32[1,128]{1,0:T(1,128)S(1)}, f32[1,128]{1,0:T(1,128)S(1)}, u32[]{:S(2)}, u32[]{:S(2)}) %collective-permute-start.13) | collective-permute-done | bytes 544 | tf_op jit(solution)/shard_map/ppermute | solution.py:21
  39.8 1.5 %collective-permute-start.14 = (f32[1,128]{1,0:T(1,128)S(1)}, f32[1,128]{1,0:T(1,128)S(1)}, u32[]{:S(2)}, u32[]{:S(2)}) collective-permute-start(f32[1,128]{1,0:T(1,128)S(1)} %max.6), channel_id=1, source_target_pairs={{0,4},{4,0},{8,12},{12,8},{16,20},{20,16},{24,28},{28,24},{1,5},{5... | collective-permute-start | bytes 1544 | tf_op jit(solution)/shard_map/ppermute | solution.py:21
  41.3 0.7 %copy.7 = bf16[512,128]{1,0:T(8,128)(2,1)} copy(bf16[512,128]{1,0:T(8,128)(2,1)S(1)} %get-tuple-element.29) | data formatting | bytes 262144
  42.0 0.6 %copy.8 = bf16[2,64,128]{2,1,0:T(8,128)(2,1)} copy(bf16[2,64,128]{2,1,0:T(8,128)(2,1)S(1)} %get-tuple-element.30) | data formatting | bytes 65536
  42.6 0.8 %collective-permute-done.14 = f32[1,128]{1,0:T(1,128)S(1)} collective-permute-done((f32[1,128]{1,0:T(1,128)S(1)}, f32[1,128]{1,0:T(1,128)S(1)}, u32[]{:S(2)}, u32[]{:S(2)}) %collective-permute-start.14) | collective-permute-done | bytes 544 | tf_op jit(solution)/shard_map/ppermute | solution.py:21
  43.3 0.5 %maximum_bitcast_fusion = f32[128]{0:T(128)} fusion(f32[1,128]{1,0:T(1,128)S(1)} %max.6, f32[1,128]{1,0:T(1,128)S(1)} %collective-permute-done.14), kind=kLoop, calls=%fused_computation | loop fusion | flops 128 | bytes 1536 | tf_op jit(solution)/shard_map/squeeze | solution.py:208
  (6 shorter events, 0.2 us)
Async XLA Ops:
  0.6 4.6 %copy-start.3 = (s32[2,1]{0,1:T(1,128)S(1)}, s32[2,1]{0,1:T(1,128)}, u32[]{:S(2)}) copy-start(s32[2,1]{0,1:T(1,128)} %param.6) | copy-start | bytes 28
  0.6 9.5 %collective-permute-start.1 = (bf16[1024,128]{1,0:T(8,128)(2,1)}, bf16[1024,128]{1,0:T(8,128)(2,1)S(1)}, u32[]{:S(2)}, u32[]{:S(2)}) collective-permute-start(bf16[1024,128]{1,0:T(8,128)(2,1)} %own.1), channel_id=1, source_target_pairs={{0,2},{1,3},{2,0},{3,1},{4,6},{5,7},{6,4},{7,5},{8,10},{9,11},{10,... | collective-permute-start | bytes 786440 | tf_op jit(solution)/shard_map/ppermute | solution.py:21
  3.6 8.0 %collective-permute-start.9 = (bf16[1024,128]{1,0:T(8,128)(2,1)}, bf16[1024,128]{1,0:T(8,128)(2,1)S(1)}, u32[]{:S(2)}, u32[]{:S(2)}) collective-permute-start(bf16[1024,128]{1,0:T(8,128)(2,1)} %own.1), channel_id=1, source_target_pairs={{0,8},{4,12},{8,0},{12,4},{16,24},{20,28},{24,16},{28,20},{1,9},{5... | collective-permute-start | bytes 786440 | tf_op jit(solution)/shard_map/ppermute | solution.py:21
  5.2 1.0 %copy-start.1 = (bf16[1024,128]{1,0:T(8,128)(2,1)S(1)}, bf16[1024,128]{1,0:T(8,128)(2,1)}, u32[]{:S(2)}) copy-start(bf16[1024,128]{1,0:T(8,128)(2,1)} %own.1) | copy-start | bytes 786436
  7.0 5.1 %collective-permute-start = (bf16[1024,128]{1,0:T(8,128)(2,1)S(1)}, bf16[1024,128]{1,0:T(8,128)(2,1)S(1)}, u32[]{:S(2)}, u32[]{:S(2)}) collective-permute-start(bf16[1024,128]{1,0:T(8,128)(2,1)S(1)} %get-tuple-element.18.refs_0_), channel_id=1, source_target_pairs={{0,1},{1,0},{2,3},{3,2},{4,5},{5,4},{6,7},{7,6},{8,9},{9,8},{10,11... | collective-permute-start | bytes 786440 | tf_op jit(solution)/shard_map/ppermute | solution.py:21
  10.2 1.9 %collective-permute-start.2 = (bf16[1024,128]{1,0:T(8,128)(2,1)S(1)}, bf16[1024,128]{1,0:T(8,128)(2,1)S(1)}, u32[]{:S(2)}, u32[]{:S(2)}) collective-permute-start(bf16[1024,128]{1,0:T(8,128)(2,1)S(1)} %collective-permute-done.1.refs_1_.refs_2_), channel_id=1, source_target_pairs={{0,1},{1,0},{2,3},{3,2},{4,5},{5,4},{6,7},{7,6},{8,9},{9,8},{10,11... | collective-permute-start | bytes 786440 | tf_op jit(solution)/shard_map/ppermute | solution.py:21
  11.6 7.3 %collective-permute-start.11 = (bf16[1024,128]{1,0:T(8,128)(2,1)S(1)}, bf16[1024,128]{1,0:T(8,128)(2,1)S(1)}, u32[]{:S(2)}, u32[]{:S(2)}) collective-permute-start(bf16[1024,128]{1,0:T(8,128)(2,1)S(1)} %collective-permute-done.9.refs_0_), channel_id=1, source_target_pairs={{0,2},{1,3},{2,0},{3,1},{4,6},{5,7},{6,4},{7,5},{8,10},{9,11},{10,... | collective-permute-start | bytes 786440 | tf_op jit(solution)/shard_map/ppermute | solution.py:21
  12.4 7.7 %collective-permute-start.4 = (bf16[512,128]{1,0:T(8,128)(2,1)S(1)}, bf16[512,128]{1,0:T(8,128)(2,1)S(1)}, u32[]{:S(2)}, u32[]{:S(2)}) collective-permute-start(bf16[512,128]{1,0:T(8,128)(2,1)S(1)} %get-tuple-element.20), channel_id=1, source_target_pairs={{0,8},{4,12},{8,0},{12,4},{16,24},{20,28},{24,16},{28,20},{1,9},{5... | collective-permute-start | bytes 393224 | tf_op jit(solution)/shard_map/ppermute | solution.py:21
  14.2 8.9 %collective-permute-start.3 = (bf16[512,128]{1,0:T(8,128)(2,1)S(1)}, bf16[512,128]{1,0:T(8,128)(2,1)S(1)}, u32[]{:S(2)}, u32[]{:S(2)}) collective-permute-start(bf16[512,128]{1,0:T(8,128)(2,1)S(1)} %get-tuple-element.19), channel_id=1, source_target_pairs={{0,16},{4,20},{8,24},{12,28},{16,0},{20,4},{24,8},{28,12},{1,17},{... | collective-permute-start | bytes 393224 | tf_op jit(solution)/shard_map/ppermute | solution.py:21
  16.8 13.5 %collective-permute-start.10 = (bf16[1024,128]{1,0:T(8,128)(2,1)S(1)}, bf16[1024,128]{1,0:T(8,128)(2,1)S(1)}, u32[]{:S(2)}, u32[]{:S(2)}) collective-permute-start(bf16[1024,128]{1,0:T(8,128)(2,1)S(1)} %collective-permute-done.9.refs_0_), channel_id=1, source_target_pairs={{0,1},{1,0},{2,3},{3,2},{4,5},{5,4},{6,7},{7,6},{8,9},{9,8},{10,11... | collective-permute-start | bytes 786440 | tf_op jit(solution)/shard_map/ppermute | solution.py:21
  18.9 11.3 %collective-permute-start.12 = (bf16[1024,128]{1,0:T(8,128)(2,1)S(1)}, bf16[1024,128]{1,0:T(8,128)(2,1)S(1)}, u32[]{:S(2)}, u32[]{:S(2)}) collective-permute-start(bf16[1024,128]{1,0:T(8,128)(2,1)S(1)} %collective-permute-done.11.refs_2_), channel_id=1, source_target_pairs={{0,1},{1,0},{2,3},{3,2},{4,5},{5,4},{6,7},{7,6},{8,9},{9,8},{10,11... | collective-permute-start | bytes 786440 | tf_op jit(solution)/shard_map/ppermute | solution.py:21
  20.2 5.0 %collective-permute-start.7 = (bf16[512,128]{1,0:T(8,128)(2,1)S(1)}, bf16[512,128]{1,0:T(8,128)(2,1)S(1)}, u32[]{:S(2)}, u32[]{:S(2)}) collective-permute-start(bf16[512,128]{1,0:T(8,128)(2,1)S(1)} %add.15), channel_id=1, source_target_pairs={{0,4},{4,0},{8,12},{12,8},{16,20},{20,16},{24,28},{28,24},{1,5},{5... | collective-permute-start | bytes 393224 | tf_op jit(solution)/shard_map/ppermute | solution.py:21
  23.1 5.0 %collective-permute-start.5 = (bf16[512,128]{1,0:T(8,128)(2,1)S(1)}, bf16[512,128]{1,0:T(8,128)(2,1)S(1)}, u32[]{:S(2)}, u32[]{:S(2)}) collective-permute-start(bf16[512,128]{1,0:T(8,128)(2,1)S(1)} %add.16), channel_id=1, source_target_pairs={{0,8},{4,12},{8,0},{12,4},{16,24},{20,28},{24,16},{28,20},{1,9},{5... | collective-permute-start | bytes 393224 | tf_op jit(solution)/shard_map/ppermute | solution.py:21
  25.3 4.5 %copy-start = (bf16[1024,128]{1,0:T(8,128)(2,1)S(1)}, bf16[1024,128]{1,0:T(8,128)(2,1)}, u32[]{:S(2)}) copy-start(bf16[1024,128]{1,0:T(8,128)(2,1)} %signals.5) | copy-start | bytes 786436
  25.3 8.8 %collective-permute-start.8 = (bf16[512,128]{1,0:T(8,128)(2,1)S(1)}, bf16[512,128]{1,0:T(8,128)(2,1)S(1)}, u32[]{:S(2)}, u32[]{:S(2)}) collective-permute-start(bf16[512,128]{1,0:T(8,128)(2,1)S(1)} %add.18), channel_id=1, source_target_pairs={{0,16},{4,20},{8,24},{12,28},{16,0},{20,4},{24,8},{28,12},{1,17},{... | collective-permute-start | bytes 393224 | tf_op jit(solution)/shard_map/ppermute | solution.py:21
  28.1 6.0 %collective-permute-start.6 = (bf16[512,128]{1,0:T(8,128)(2,1)S(1)}, bf16[512,128]{1,0:T(8,128)(2,1)S(1)}, u32[]{:S(2)}, u32[]{:S(2)}) collective-permute-start(bf16[512,128]{1,0:T(8,128)(2,1)S(1)} %add.17.refs_0_), channel_id=1, source_target_pairs={{0,4},{4,0},{8,12},{12,8},{16,20},{20,16},{24,28},{28,24},{1,5},{5... | collective-permute-start | bytes 393224 | tf_op jit(solution)/shard_map/ppermute | solution.py:21
  30.7 3.4 %copy-start.2 = (bf16[2,1,64,64]{3,2,1,0:T(8,128)(2,1)S(1)}, bf16[2,1,64,64]{3,2,1,0:T(8,128)(2,1)}, u32[]{:S(2)}) copy-start(bf16[2,1,64,64]{3,2,1,0:T(8,128)(2,1)} %inverses.1) | copy-start | bytes 49156
  35.3 4.5 %collective-permute-start.13 = (f32[1,128]{1,0:T(1,128)S(1)}, f32[1,128]{1,0:T(1,128)S(1)}, u32[]{:S(2)}, u32[]{:S(2)}) collective-permute-start(f32[1,128]{1,0:T(1,128)S(1)} %get-tuple-element.28), channel_id=1, source_target_pairs={{0,16},{4,20},{8,24},{12,28},{16,0},{20,4},{24,8},{28,12},{1,17},{... | collective-permute-start | bytes 1544 | tf_op jit(solution)/shard_map/ppermute | solution.py:21
  39.8 3.5 %collective-permute-start.14 = (f32[1,128]{1,0:T(1,128)S(1)}, f32[1,128]{1,0:T(1,128)S(1)}, u32[]{:S(2)}, u32[]{:S(2)}) collective-permute-start(f32[1,128]{1,0:T(1,128)S(1)} %max.6), channel_id=1, source_target_pairs={{0,4},{4,0},{8,12},{12,8},{16,20},{20,16},{24,28},{28,24},{1,5},{5... | collective-permute-start | bytes 1544 | tf_op jit(solution)/shard_map/ppermute | solution.py:21
